TPU v7x, 32 devices: a whole 2x2x4 slice. The times are simulated.
32 devices in a mesh: lat: 8 (over z, x), section: 4 (over y, core).
Axes of the slice: x: 2, y: 2, z: 4, core: 2. Of those that a mesh axis runs over, the one named last changes fastest.
Arguments:
- saved_input: bfloat16 [4, 2, 4096, 256], P('section', None, 'lat'), may hold values from -6 to 6
- cotangent: bfloat16 [2, 4096, 256], P(None, 'lat'), may hold values from -6 to 6
- quad_values: bfloat16 [3, 64, 5, 64, 64], P(None, 'lat'), may hold values from -0.3125 to 0.3125
- block_index: int32 [64, 5], P('lat'), may hold values from 0 to 63, as said below
- block_mask: int32 [64, 5], P('lat'), may hold values from 0 to 1
- weights: bfloat16 [4, 3, 256, 256], P('section'), may hold values from -0.21875 to 0.21875
Outputs:
- grad_input: bfloat16 [4, 2, 4096, 256], P('section', None, 'lat')
- grad_weight: float32 [4, 3, 256, 256], P('section')
Inputs may be any that keep to these rules, and one draw needn't show every extreme that they name: block_index[b, j] lies within 2 blocks of b; entries of one row name distinct blocks where block_mask is 1.
All inputs are finite; a program needn't handle non-finite values.
Results may differ from a plain program's by a relative error of at most 0.0085.
Values may be sent and summed in bfloat16 or wider, within the bound.
No kernel may reach another device: no remote copies, remote signals or barrier semaphores. Data moves between devices by JAX's collectives and lax.ppermute only.
A program may use at most 64 MiB of HBM per device.

v0:
```python
import jax
import jax.numpy as jnp
from jax import lax
from jax.sharding import PartitionSpec as P

KB = 3
BLK = 64
HALO = 2
MB = 2


def from_behind(block, axis, distance):
    devices = range(lax.axis_size(axis))
    route = [(i - distance, i) for i in devices if i - distance in devices]
    return lax.ppermute(block, axis, route)


def with_halo(cells, sides, width):
    for axis, dim in sides:
        count = lax.axis_size(axis)
        ends = count - 1
        head = lax.slice_in_dim(cells, 0, width, axis=dim)
        tail = lax.slice_in_dim(cells, cells.shape[dim] - width, cells.shape[dim], axis=dim)
        cells = jnp.concatenate(
            [
                lax.ppermute(tail, axis, [(i, (i + 1) % count) for i in range(ends)]),
                cells,
                lax.ppermute(head, axis, [((i + 1) % count, i) for i in range(ends)]),
            ],
            axis=dim,
        )
    return cells


def gelu_slope(value):
    return (
        0.5 * (1.0 + jax.scipy.special.erf(value * 0.7071067811865476))
        + value * jnp.exp(-0.5 * value * value) * 0.3989422804014327
    )


def layer_terms(extended, incoming, qmat, local_index, one_hot, w_cat):
    group = incoming.shape[0]
    blocks = incoming.shape[1]
    channels = incoming.shape[3]
    chosen = extended[:, local_index]
    hidden = jnp.einsum(
        "kbjpq,mbjqc->mbpkc", qmat, chosen, preferred_element_type=jnp.float32
    ).astype(jnp.bfloat16)
    flat = hidden.reshape(group * blocks * BLK, KB * channels)
    mixed = jnp.dot(flat, w_cat, preferred_element_type=jnp.float32)
    slope = (
        incoming.reshape(group * blocks * BLK, channels).astype(jnp.float32) * gelu_slope(mixed)
    ).astype(jnp.bfloat16)
    w_grad = lax.dot_general(
        flat, slope, (((0,), (0,)), ((), ())), preferred_element_type=jnp.float32
    )
    back = jnp.dot(slope, w_cat.T, preferred_element_type=jnp.float32).astype(jnp.bfloat16)
    back = back.reshape(group, blocks, BLK, KB, channels)
    terms = jnp.einsum("kbjpq,mbpkc->mbjqc", qmat, back, preferred_element_type=jnp.float32)
    partial_value = jnp.einsum("bjr,mbjqc->mrqc", one_hot, terms, precision=lax.Precision.HIGHEST)
    return (partial_value, w_grad)


def per_device(saved_input, cotangent, quad_values, block_index, block_mask, weights):
    sections = lax.axis_size("section")
    section_here = lax.axis_index("section")
    lat_here = lax.axis_index("lat")
    blocks = quad_values.shape[1]
    channels = saved_input.shape[3]
    local_index = block_index - (lat_here * blocks - HALO)
    one_hot = (
        local_index[:, :, None] == jnp.arange(blocks + 2 * HALO, dtype=jnp.int32)[None, None, :]
    ).astype(jnp.float32)
    qmat = quad_values * block_mask.astype(jnp.bfloat16)[None, :, :, None, None]
    acts = saved_input[0].reshape(MB, blocks, BLK, channels)
    grads_in = cotangent.reshape(MB, blocks, BLK, channels)
    w_cat = weights[0].reshape(KB * channels, channels)
    group = 1
    ticks = sections + MB - 1

    def busy(extended, incoming):
        return layer_terms(extended, incoming, qmat, local_index, one_hot, w_cat)

    def spare(extended, incoming):
        return (
            jnp.zeros((group, blocks + 2 * HALO, BLK, channels), jnp.float32),
            jnp.zeros((KB * channels, channels), jnp.float32),
        )

    def advance(step_index, state_tuple):
        last_grad, results, w_total = state_tuple
        micro_index = step_index - (sections - 1 - section_here)
        active = (micro_index >= 0) & (micro_index < MB)
        micro_start = jnp.clip(micro_index, 0, MB - 1)
        received = from_behind(last_grad, "section", -1)
        own_grads = lax.dynamic_slice_in_dim(grads_in, micro_start, group, 0)
        incoming = jnp.where(section_here == sections - 1, own_grads, received)
        extended = with_halo(
            lax.dynamic_slice_in_dim(acts, micro_start, group, 0), (("lat", 1),), HALO
        )
        partial_value, w_grad = lax.cond(active, busy, spare, extended, incoming)
        from_below = from_behind(partial_value[:, blocks + HALO :], "lat", 1)
        from_above = from_behind(partial_value[:, :HALO], "lat", -1)
        summed = incoming.astype(jnp.float32) + partial_value[:, HALO : HALO + blocks]
        summed = summed.at[:, :HALO].add(from_below)
        summed = summed.at[:, blocks - HALO :].add(from_above)
        grad_step = summed.astype(jnp.bfloat16)
        updated = lax.dynamic_update_slice_in_dim(results, grad_step, micro_start, 0)
        results = jnp.where(active, updated, results)
        return (grad_step, results, w_total + w_grad)

    start_state = (
        jnp.zeros((group, blocks, BLK, channels), jnp.bfloat16),
        jnp.zeros((MB, blocks, BLK, channels), jnp.bfloat16),
        jnp.zeros((KB * channels, channels), jnp.float32),
    )
    last_grad, results, w_total = lax.fori_loop(0, ticks, advance, start_state)
    w_summed = lax.psum(w_total, "lat")
    grad_input = results.reshape(1, MB, blocks * BLK, channels)
    grad_weight = w_summed.reshape(1, KB, channels, channels)
    return (grad_input, grad_weight)


def solution(mesh):
    in_specs = (
        P("section", None, "lat", None),
        P(None, "lat", None),
        P(None, "lat", None, None, None),
        P("lat", None),
        P("lat", None),
        P("section", None, None, None),
    )
    out_specs = (P("section", None, "lat", None), P("section", None, None, None))
    return jax.shard_map(
        per_device, mesh=mesh, in_specs=in_specs, out_specs=out_specs, check_vma=False
    )
```

profile of v0, /device:TPU:0, one launch (start us, length us, event | category | flops | bytes accessed | tf_op | source)
XLA Modules:
  0.0 301.0 jit_solution(1559633501406302809)
XLA Ops:
  7.9 4.0 %copy.21 = bf16[3,8,5,64,64]{3,4,0,2,1:T(8,128)(2,1)} copy(bf16[3,8,5,64,64]{4,3,2,1,0:T(8,128)(2,1)} %param.16) | data formatting | bytes 1966080 | tf_op args[2]
  12.0 1.7 broadcast_multiply_fusion
  14.6 204.1 %while.24 = (s32[]{:T(128)}, bf16[1,8,64,256]{3,1,2,0:T(8,128)(2,1)}, bf16[2,8,64,256]{3,2,1,0:T(8,128)(2,1)}, f32[768,256]{1,0:T(8,128)}, pred[]{:T(512)}, /*in...) while((s32[]{:T(128)}, ...), condition=%wide.region_3.4_spmd.clone.clone.clone, body=%wide.region_0.3_spmd.clone.clone.clone.sunk | while | flops 1205536896 | bytes 42878220 | solution.py:118
  15.5 1.3 collective-permute-start.1
  16.8 5.5 %collective-permute-start.2 = (bf16[1,2,64,256]{3,2,1,0:T(8,128)(2,1)S(1)}, bf16[1,2,64,256]{3,2,1,0:T(8,128)(2,1)S(1)}, u32[]{:S(2)}, u32[]{:S(2)}) collective-permute-start(bf16[1,2,64,256]{3,2,1,0:T(8,128)(2,1)S(1)} %get-tuple-element.577), channel_id=1, source_target_pairs={{0,4},{4,8},{8,12},{12,16},{16,20},{20,24},{24,28},{1,5},{5,9},{9,... | collective-permute-start | bytes 196616 | tf_op jit(solution)/shard_map/while/body/eval_jaxpr/ppermute | solution.py:26
  22.3 1.3 collective-permute-start
  26.5 1.1 copy_select_fusion.4
  27.6 1.1 conditional.5
  28.8 4.8 %collective-permute-start.3 = (f32[1,2,64,256]{3,1,2,0:T(2,128)S(1)}, f32[1,2,64,256]{3,1,2,0:T(2,128)S(1)}, u32[]{:S(2)}, u32[]{:S(2)}) collective-permute-start(f32[1,2,64,256]{3,1,2,0:T(2,128)S(1)} %get-tuple-element.579), channel_id=1, source_target_pairs={{0,4},{4,8},{8,12},{12,16},{16,20},{20,24},{24,28},{1,5},{5,9},{9,... | collective-permute-start | bytes 393224 | tf_op jit(solution)/shard_map/while/body/eval_jaxpr/ppermute | solution.py:15
  33.7 1.3 collective-permute-start.4
  35.0 2.1 select_add_fusion.2
  37.3 3.2 %collective-permute-done.4 = f32[1,2,64,256]{3,1,2,0:T(2,128)S(1)} collective-permute-done((f32[1,2,64,256]{3,1,2,0:T(2,128)S(1)}, f32[1,2,64,256]{3,1,2,0:T(2,128)S(1)}, u32[]{:S(2)}, u32[]{:S(2)}) %collective-permute-start.4) | collective-permute-done | bytes 131104 | tf_op jit(solution)/shard_map/while/body/eval_jaxpr/ppermute | solution.py:15
  43.3 1.3 collective-permute-start.1
  44.6 4.5 %collective-permute-start.2 = (bf16[1,2,64,256]{3,2,1,0:T(8,128)(2,1)S(1)}, bf16[1,2,64,256]{3,2,1,0:T(8,128)(2,1)S(1)}, u32[]{:S(2)}, u32[]{:S(2)}) collective-permute-start(bf16[1,2,64,256]{3,2,1,0:T(8,128)(2,1)S(1)} %get-tuple-element.577), channel_id=1, source_target_pairs={{0,4},{4,8},{8,12},{12,16},{16,20},{20,24},{24,28},{1,5},{5,9},{9,... | collective-permute-start | bytes 196616 | tf_op jit(solution)/shard_map/while/body/eval_jaxpr/ppermute | solution.py:26
  50.1 1.3 collective-permute-start
  54.7 1.1 copy_select_fusion.4
  55.8 1.1 conditional.5
  57.0 4.4 %collective-permute-start.3 = (f32[1,2,64,256]{3,1,2,0:T(2,128)S(1)}, f32[1,2,64,256]{3,1,2,0:T(2,128)S(1)}, u32[]{:S(2)}, u32[]{:S(2)}) collective-permute-start(f32[1,2,64,256]{3,1,2,0:T(2,128)S(1)} %get-tuple-element.579), channel_id=1, source_target_pairs={{0,4},{4,8},{8,12},{12,16},{16,20},{20,24},{24,28},{1,5},{5,9},{9,... | collective-permute-start | bytes 393224 | tf_op jit(solution)/shard_map/while/body/eval_jaxpr/ppermute | solution.py:15
  61.4 1.3 collective-permute-start.4
  62.7 2.4 select_add_fusion.2
  65.3 3.0 collective-permute-done.4
  71.0 1.3 collective-permute-start.1
  72.3 4.5 %collective-permute-start.2 = (bf16[1,2,64,256]{3,2,1,0:T(8,128)(2,1)S(1)}, bf16[1,2,64,256]{3,2,1,0:T(8,128)(2,1)S(1)}, u32[]{:S(2)}, u32[]{:S(2)}) collective-permute-start(bf16[1,2,64,256]{3,2,1,0:T(8,128)(2,1)S(1)} %get-tuple-element.577), channel_id=1, source_target_pairs={{0,4},{4,8},{8,12},{12,16},{16,20},{20,24},{24,28},{1,5},{5,9},{9,... | collective-permute-start | bytes 196616 | tf_op jit(solution)/shard_map/while/body/eval_jaxpr/ppermute | solution.py:26
  77.8 1.3 collective-permute-start
  82.0 1.5 collective-permute-done
  83.6 1.1 copy_select_fusion.4
  85.9 4.3 %collective-permute-start.3 = (f32[1,2,64,256]{3,1,2,0:T(2,128)S(1)}, f32[1,2,64,256]{3,1,2,0:T(2,128)S(1)}, u32[]{:S(2)}, u32[]{:S(2)}) collective-permute-start(f32[1,2,64,256]{3,1,2,0:T(2,128)S(1)} %get-tuple-element.579), channel_id=1, source_target_pairs={{0,4},{4,8},{8,12},{12,16},{16,20},{20,24},{24,28},{1,5},{5,9},{9,... | collective-permute-start | bytes 393224 | tf_op jit(solution)/shard_map/while/body/eval_jaxpr/ppermute | solution.py:15
  90.2 1.3 collective-permute-start.4
  91.5 2.4 select_add_fusion.2
  94.1 3.0 collective-permute-done.4
  99.8 1.3 collective-permute-start.1
  101.1 4.5 %collective-permute-start.2 = (bf16[1,2,64,256]{3,2,1,0:T(8,128)(2,1)S(1)}, bf16[1,2,64,256]{3,2,1,0:T(8,128)(2,1)S(1)}, u32[]{:S(2)}, u32[]{:S(2)}) collective-permute-start(bf16[1,2,64,256]{3,2,1,0:T(8,128)(2,1)S(1)} %get-tuple-element.577), channel_id=1, source_target_pairs={{0,4},{4,8},{8,12},{12,16},{16,20},{20,24},{24,28},{1,5},{5,9},{9,... | collective-permute-start | bytes 196616 | tf_op jit(solution)/shard_map/while/body/eval_jaxpr/ppermute | solution.py:26
  106.6 1.3 collective-permute-start
  110.8 36.8 %collective-permute-done = bf16[1,8,64,256]{3,1,2,0:T(8,128)(2,1)} collective-permute-done((bf16[1,8,64,256]{3,1,2,0:T(8,128)(2,1)S(1)}, bf16[1,8,64,256]{3,1,2,0:T(8,128)(2,1)}, u32[]{:S(2)}, u32[]{:S(2)}) %collective-permute-start) | collective-permute-done | bytes 262176 | tf_op jit(solution)/shard_map/while/body/eval_jaxpr/ppermute | solution.py:15
  147.6 1.1 copy_select_fusion.4
  148.7 14.5 %conditional.5 = (f32[1,12,64,256]{3,1,2,0:T(8,128)S(1)}, f32[768,256]{1,0:T(8,128)}) conditional(s32[]{:T(128)} %convert_element_type.90, () %tuple.97, (bf16[1,8,64,256]{3,1,2,0:T(8,128)(2,1)S(1)}, s32[8,5]{1,0:T(8,128)S(1)}, bf16[1,12,64,256]{3,2,1,0:T(8,128)(2,1)S(1)}, bf16[3,8,5,64,64]{3,4,0,2,1:T(8,128)(2,1)S(1)}, bf16[768,256]{1,0:T(8,128)(2,1)}, ...), branch_computations={%region_1.1_spmd, %region_2.2_spmd} | conditional | flops 1203897472 | bytes 25311624 | solution.py:102
  148.9 1.8 gather_fusion
  150.7 2.1 fusion.7
  154.3 1.3 fusion.20
  155.6 1.3 convolution_convert_fusion
  156.9 2.5 reshape.164
  160.2 3.0 fusion.4
  163.3 4.5 %collective-permute-start.3 = (f32[1,2,64,256]{3,1,2,0:T(2,128)S(1)}, f32[1,2,64,256]{3,1,2,0:T(2,128)S(1)}, u32[]{:S(2)}, u32[]{:S(2)}) collective-permute-start(f32[1,2,64,256]{3,1,2,0:T(2,128)S(1)} %get-tuple-element.579), channel_id=1, source_target_pairs={{0,4},{4,8},{8,12},{12,16},{16,20},{20,24},{24,28},{1,5},{5,9},{9,... | collective-permute-start | bytes 393224 | tf_op jit(solution)/shard_map/while/body/eval_jaxpr/ppermute | solution.py:15
  167.9 1.3 collective-permute-start.4
  169.2 2.4 select_add_fusion.2
  171.7 3.0 collective-permute-done.4
  177.5 1.3 collective-permute-start.1
  178.8 4.5 %collective-permute-start.2 = (bf16[1,2,64,256]{3,2,1,0:T(8,128)(2,1)S(1)}, bf16[1,2,64,256]{3,2,1,0:T(8,128)(2,1)S(1)}, u32[]{:S(2)}, u32[]{:S(2)}) collective-permute-start(bf16[1,2,64,256]{3,2,1,0:T(8,128)(2,1)S(1)} %get-tuple-element.577), channel_id=1, source_target_pairs={{0,4},{4,8},{8,12},{12,16},{16,20},{20,24},{24,28},{1,5},{5,9},{9,... | collective-permute-start | bytes 196616 | tf_op jit(solution)/shard_map/while/body/eval_jaxpr/ppermute | solution.py:26
  184.3 1.3 collective-permute-start
  188.5 1.6 collective-permute-done
  190.1 1.1 copy_select_fusion.4
  191.2 14.5 %conditional.5 = (f32[1,12,64,256]{3,1,2,0:T(8,128)S(1)}, f32[768,256]{1,0:T(8,128)}) conditional(s32[]{:T(128)} %convert_element_type.90, () %tuple.97, (bf16[1,8,64,256]{3,1,2,0:T(8,128)(2,1)S(1)}, s32[8,5]{1,0:T(8,128)S(1)}, bf16[1,12,64,256]{3,2,1,0:T(8,128)(2,1)S(1)}, bf16[3,8,5,64,64]{3,4,0,2,1:T(8,128)(2,1)S(1)}, bf16[768,256]{1,0:T(8,128)(2,1)}, ...), branch_computations={%region_1.1_spmd, %region_2.2_spmd} | conditional | flops 1203897472 | bytes 25311624 | solution.py:102
  191.4 1.8 gather_fusion
  193.2 2.1 fusion.7
  196.8 1.3 fusion.20
  198.1 1.3 convolution_convert_fusion
  199.4 2.5 reshape.164
  202.7 3.0 fusion.4
  205.8 4.1 %collective-permute-start.3 = (f32[1,2,64,256]{3,1,2,0:T(2,128)S(1)}, f32[1,2,64,256]{3,1,2,0:T(2,128)S(1)}, u32[]{:S(2)}, u32[]{:S(2)}) collective-permute-start(f32[1,2,64,256]{3,1,2,0:T(2,128)S(1)} %get-tuple-element.579), channel_id=1, source_target_pairs={{0,4},{4,8},{8,12},{12,16},{16,20},{20,24},{24,28},{1,5},{5,9},{9,... | collective-permute-start | bytes 393224 | tf_op jit(solution)/shard_map/while/body/eval_jaxpr/ppermute | solution.py:15
  209.9 1.3 collective-permute-start.4
  211.2 2.4 select_add_fusion.2
  213.8 3.0 collective-permute-done.4
  218.7 73.4 %all-reduce.2.cloned.1.call-done = f32[1,3,256,256]{3,2,1,0:T(8,128)} async-done(((f32[1,3,256,256]{3,2,1,0:T(8,128)}), f32[1,3,256,256]{3,2,1,0:T(8,128)}) %all-reduce.2.cloned.1.call-update) | async-done | bytes 786448 | tf_op jit(solution)/shard_map/psum | solution.py:119
  292.1 2.1 copy.75
  (142 shorter events, 44.1 us)
Async XLA Ops:
  7.2 284.9 %all-reduce.2.cloned.1.call-start = ((), (), s32[]{:S(2)}) async-start(), calls=%async_computation | async-start | bytes 1572864 | tf_op jit(solution)/shard_map/psum | solution.py:119
  7.9 4.0 %copy-start.4 = (s32[8,5]{1,0:T(8,128)S(1)}, s32[8,5]{1,0:T(8,128)}, u32[]{:S(2)}) copy-start(s32[8,5]{1,0:T(8,128)} %param.17) | copy-start | bytes 484
  15.5 11.0 %collective-permute-start.1 = (bf16[1,2,64,256]{3,2,1,0:T(8,128)(2,1)S(1)}, bf16[1,2,64,256]{3,2,1,0:T(8,128)(2,1)S(1)}, u32[]{:S(2)}, u32[]{:S(2)}) collective-permute-start(bf16[1,2,64,256]{3,2,1,0:T(8,128)(2,1)S(1)} %get-tuple-element.575), channel_id=1, source_target_pairs={{4,0},{8,4},{12,8},{16,12},{20,16},{24,20},{28,24},{5,1},{9,5},{13... | collective-permute-start | bytes 196616 | tf_op jit(solution)/shard_map/while/body/eval_jaxpr/ppermute | solution.py:28
  16.8 9.7 %collective-permute-start.2 = (bf16[1,2,64,256]{3,2,1,0:T(8,128)(2,1)S(1)}, bf16[1,2,64,256]{3,2,1,0:T(8,128)(2,1)S(1)}, u32[]{:S(2)}, u32[]{:S(2)}) collective-permute-start(bf16[1,2,64,256]{3,2,1,0:T(8,128)(2,1)S(1)} %get-tuple-element.577), channel_id=1, source_target_pairs={{0,4},{4,8},{8,12},{12,16},{16,20},{20,24},{24,28},{1,5},{5,9},{9,... | collective-permute-start | bytes 196616 | tf_op jit(solution)/shard_map/while/body/eval_jaxpr/ppermute | solution.py:26
  22.3 4.2 %collective-permute-start = (bf16[1,8,64,256]{3,1,2,0:T(8,128)(2,1)S(1)}, bf16[1,8,64,256]{3,1,2,0:T(8,128)(2,1)}, u32[]{:S(2)}, u32[]{:S(2)}) collective-permute-start(bf16[1,8,64,256]{3,1,2,0:T(8,128)(2,1)S(1)} %broadcast_select_fusion.2), channel_id=1, source_target_pairs={{1,0},{2,1},{3,2},{5,4},{6,5},{7,6},{9,8},{10,9},{11,10},{13,12},{... | collective-permute-start | bytes 786440 | tf_op jit(solution)/shard_map/while/body/eval_jaxpr/ppermute | solution.py:15
  28.8 8.3 %collective-permute-start.3 = (f32[1,2,64,256]{3,1,2,0:T(2,128)S(1)}, f32[1,2,64,256]{3,1,2,0:T(2,128)S(1)}, u32[]{:S(2)}, u32[]{:S(2)}) collective-permute-start(f32[1,2,64,256]{3,1,2,0:T(2,128)S(1)} %get-tuple-element.579), channel_id=1, source_target_pairs={{0,4},{4,8},{8,12},{12,16},{16,20},{20,24},{24,28},{1,5},{5,9},{9,... | collective-permute-start | bytes 393224 | tf_op jit(solution)/shard_map/while/body/eval_jaxpr/ppermute | solution.py:15
  33.7 6.9 %collective-permute-start.4 = (f32[1,2,64,256]{3,1,2,0:T(2,128)S(1)}, f32[1,2,64,256]{3,1,2,0:T(2,128)S(1)}, u32[]{:S(2)}, u32[]{:S(2)}) collective-permute-start(f32[1,2,64,256]{3,1,2,0:T(2,128)S(1)} %get-tuple-element.580), channel_id=1, source_target_pairs={{4,0},{8,4},{12,8},{16,12},{20,16},{24,20},{28,24},{5,1},{9,5},{13... | collective-permute-start | bytes 393224 | tf_op jit(solution)/shard_map/while/body/eval_jaxpr/ppermute | solution.py:15
  37.1 4.4 %copy-start.1 = (bf16[2,8,64,256]{3,2,1,0:T(8,128)(2,1)S(1)}, bf16[2,8,64,256]{3,2,1,0:T(8,128)(2,1)}, u32[]{:S(2)}) copy-start(bf16[2,8,64,256]{3,2,1,0:T(8,128)(2,1)} %get-tuple-element.605) | copy-start | bytes 1572868 | tf_op jit(solution)/shard_map/while
  41.6 0.8 copy-start.2
  43.3 11.0 %collective-permute-start.1 = (bf16[1,2,64,256]{3,2,1,0:T(8,128)(2,1)S(1)}, bf16[1,2,64,256]{3,2,1,0:T(8,128)(2,1)S(1)}, u32[]{:S(2)}, u32[]{:S(2)}) collective-permute-start(bf16[1,2,64,256]{3,2,1,0:T(8,128)(2,1)S(1)} %get-tuple-element.575), channel_id=1, source_target_pairs={{4,0},{8,4},{12,8},{16,12},{20,16},{24,20},{28,24},{5,1},{9,5},{13... | collective-permute-start | bytes 196616 | tf_op jit(solution)/shard_map/while/body/eval_jaxpr/ppermute | solution.py:28
  44.6 9.7 %collective-permute-start.2 = (bf16[1,2,64,256]{3,2,1,0:T(8,128)(2,1)S(1)}, bf16[1,2,64,256]{3,2,1,0:T(8,128)(2,1)S(1)}, u32[]{:S(2)}, u32[]{:S(2)}) collective-permute-start(bf16[1,2,64,256]{3,2,1,0:T(8,128)(2,1)S(1)} %get-tuple-element.577), channel_id=1, source_target_pairs={{0,4},{4,8},{8,12},{12,16},{16,20},{20,24},{24,28},{1,5},{5,9},{9,... | collective-permute-start | bytes 196616 | tf_op jit(solution)/shard_map/while/body/eval_jaxpr/ppermute | solution.py:26
  50.1 4.6 %collective-permute-start = (bf16[1,8,64,256]{3,1,2,0:T(8,128)(2,1)S(1)}, bf16[1,8,64,256]{3,1,2,0:T(8,128)(2,1)}, u32[]{:S(2)}, u32[]{:S(2)}) collective-permute-start(bf16[1,8,64,256]{3,1,2,0:T(8,128)(2,1)S(1)} %broadcast_select_fusion.2), channel_id=1, source_target_pairs={{1,0},{2,1},{3,2},{5,4},{6,5},{7,6},{9,8},{10,9},{11,10},{13,12},{... | collective-permute-start | bytes 786440 | tf_op jit(solution)/shard_map/while/body/eval_jaxpr/ppermute | solution.py:15
  57.0 8.2 %collective-permute-start.3 = (f32[1,2,64,256]{3,1,2,0:T(2,128)S(1)}, f32[1,2,64,256]{3,1,2,0:T(2,128)S(1)}, u32[]{:S(2)}, u32[]{:S(2)}) collective-permute-start(f32[1,2,64,256]{3,1,2,0:T(2,128)S(1)} %get-tuple-element.579), channel_id=1, source_target_pairs={{0,4},{4,8},{8,12},{12,16},{16,20},{20,24},{24,28},{1,5},{5,9},{9,... | collective-permute-start | bytes 393224 | tf_op jit(solution)/shard_map/while/body/eval_jaxpr/ppermute | solution.py:15
  61.4 6.9 %collective-permute-start.4 = (f32[1,2,64,256]{3,1,2,0:T(2,128)S(1)}, f32[1,2,64,256]{3,1,2,0:T(2,128)S(1)}, u32[]{:S(2)}, u32[]{:S(2)}) collective-permute-start(f32[1,2,64,256]{3,1,2,0:T(2,128)S(1)} %get-tuple-element.580), channel_id=1, source_target_pairs={{4,0},{8,4},{12,8},{16,12},{20,16},{24,20},{28,24},{5,1},{9,5},{13... | collective-permute-start | bytes 393224 | tf_op jit(solution)/shard_map/while/body/eval_jaxpr/ppermute | solution.py:15
  65.1 4.2 %copy-start.1 = (bf16[2,8,64,256]{3,2,1,0:T(8,128)(2,1)S(1)}, bf16[2,8,64,256]{3,2,1,0:T(8,128)(2,1)}, u32[]{:S(2)}) copy-start(bf16[2,8,64,256]{3,2,1,0:T(8,128)(2,1)} %get-tuple-element.605) | copy-start | bytes 1572868 | tf_op jit(solution)/shard_map/while
  69.3 0.8 copy-start.2
  71.0 11.0 %collective-permute-start.1 = (bf16[1,2,64,256]{3,2,1,0:T(8,128)(2,1)S(1)}, bf16[1,2,64,256]{3,2,1,0:T(8,128)(2,1)S(1)}, u32[]{:S(2)}, u32[]{:S(2)}) collective-permute-start(bf16[1,2,64,256]{3,2,1,0:T(8,128)(2,1)S(1)} %get-tuple-element.575), channel_id=1, source_target_pairs={{4,0},{8,4},{12,8},{16,12},{20,16},{24,20},{28,24},{5,1},{9,5},{13... | collective-permute-start | bytes 196616 | tf_op jit(solution)/shard_map/while/body/eval_jaxpr/ppermute | solution.py:28
  72.3 9.7 %collective-permute-start.2 = (bf16[1,2,64,256]{3,2,1,0:T(8,128)(2,1)S(1)}, bf16[1,2,64,256]{3,2,1,0:T(8,128)(2,1)S(1)}, u32[]{:S(2)}, u32[]{:S(2)}) collective-permute-start(bf16[1,2,64,256]{3,2,1,0:T(8,128)(2,1)S(1)} %get-tuple-element.577), channel_id=1, source_target_pairs={{0,4},{4,8},{8,12},{12,16},{16,20},{20,24},{24,28},{1,5},{5,9},{9,... | collective-permute-start | bytes 196616 | tf_op jit(solution)/shard_map/while/body/eval_jaxpr/ppermute | solution.py:26
  77.8 5.7 %collective-permute-start = (bf16[1,8,64,256]{3,1,2,0:T(8,128)(2,1)S(1)}, bf16[1,8,64,256]{3,1,2,0:T(8,128)(2,1)}, u32[]{:S(2)}, u32[]{:S(2)}) collective-permute-start(bf16[1,8,64,256]{3,1,2,0:T(8,128)(2,1)S(1)} %broadcast_select_fusion.2), channel_id=1, source_target_pairs={{1,0},{2,1},{3,2},{5,4},{6,5},{7,6},{9,8},{10,9},{11,10},{13,12},{... | collective-permute-start | bytes 786440 | tf_op jit(solution)/shard_map/while/body/eval_jaxpr/ppermute | solution.py:15
  85.9 8.1 %collective-permute-start.3 = (f32[1,2,64,256]{3,1,2,0:T(2,128)S(1)}, f32[1,2,64,256]{3,1,2,0:T(2,128)S(1)}, u32[]{:S(2)}, u32[]{:S(2)}) collective-permute-start(f32[1,2,64,256]{3,1,2,0:T(2,128)S(1)} %get-tuple-element.579), channel_id=1, source_target_pairs={{0,4},{4,8},{8,12},{12,16},{16,20},{20,24},{24,28},{1,5},{5,9},{9,... | collective-permute-start | bytes 393224 | tf_op jit(solution)/shard_map/while/body/eval_jaxpr/ppermute | solution.py:15
  90.2 6.9 %collective-permute-start.4 = (f32[1,2,64,256]{3,1,2,0:T(2,128)S(1)}, f32[1,2,64,256]{3,1,2,0:T(2,128)S(1)}, u32[]{:S(2)}, u32[]{:S(2)}) collective-permute-start(f32[1,2,64,256]{3,1,2,0:T(2,128)S(1)} %get-tuple-element.580), channel_id=1, source_target_pairs={{4,0},{8,4},{12,8},{16,12},{20,16},{24,20},{28,24},{5,1},{9,5},{13... | collective-permute-start | bytes 393224 | tf_op jit(solution)/shard_map/while/body/eval_jaxpr/ppermute | solution.py:15
  93.9 4.2 %copy-start.1 = (bf16[2,8,64,256]{3,2,1,0:T(8,128)(2,1)S(1)}, bf16[2,8,64,256]{3,2,1,0:T(8,128)(2,1)}, u32[]{:S(2)}) copy-start(bf16[2,8,64,256]{3,2,1,0:T(8,128)(2,1)} %get-tuple-element.605) | copy-start | bytes 1572868 | tf_op jit(solution)/shard_map/while
  98.1 0.8 copy-start.2
  99.8 11.0 %collective-permute-start.1 = (bf16[1,2,64,256]{3,2,1,0:T(8,128)(2,1)S(1)}, bf16[1,2,64,256]{3,2,1,0:T(8,128)(2,1)S(1)}, u32[]{:S(2)}, u32[]{:S(2)}) collective-permute-start(bf16[1,2,64,256]{3,2,1,0:T(8,128)(2,1)S(1)} %get-tuple-element.575), channel_id=1, source_target_pairs={{4,0},{8,4},{12,8},{16,12},{20,16},{24,20},{28,24},{5,1},{9,5},{13... | collective-permute-start | bytes 196616 | tf_op jit(solution)/shard_map/while/body/eval_jaxpr/ppermute | solution.py:28
  101.1 9.7 %collective-permute-start.2 = (bf16[1,2,64,256]{3,2,1,0:T(8,128)(2,1)S(1)}, bf16[1,2,64,256]{3,2,1,0:T(8,128)(2,1)S(1)}, u32[]{:S(2)}, u32[]{:S(2)}) collective-permute-start(bf16[1,2,64,256]{3,2,1,0:T(8,128)(2,1)S(1)} %get-tuple-element.577), channel_id=1, source_target_pairs={{0,4},{4,8},{8,12},{12,16},{16,20},{20,24},{24,28},{1,5},{5,9},{9,... | collective-permute-start | bytes 196616 | tf_op jit(solution)/shard_map/while/body/eval_jaxpr/ppermute | solution.py:26
  106.6 41.0 %collective-permute-start = (bf16[1,8,64,256]{3,1,2,0:T(8,128)(2,1)S(1)}, bf16[1,8,64,256]{3,1,2,0:T(8,128)(2,1)}, u32[]{:S(2)}, u32[]{:S(2)}) collective-permute-start(bf16[1,8,64,256]{3,1,2,0:T(8,128)(2,1)S(1)} %broadcast_select_fusion.2), channel_id=1, source_target_pairs={{1,0},{2,1},{3,2},{5,4},{6,5},{7,6},{9,8},{10,9},{11,10},{13,12},{... | collective-permute-start | bytes 786440 | tf_op jit(solution)/shard_map/while/body/eval_jaxpr/ppermute | solution.py:15
  152.8 1.0 copy-start
  159.5 0.7 copy-start.3
  163.3 8.3 %collective-permute-start.3 = (f32[1,2,64,256]{3,1,2,0:T(2,128)S(1)}, f32[1,2,64,256]{3,1,2,0:T(2,128)S(1)}, u32[]{:S(2)}, u32[]{:S(2)}) collective-permute-start(f32[1,2,64,256]{3,1,2,0:T(2,128)S(1)} %get-tuple-element.579), channel_id=1, source_target_pairs={{0,4},{4,8},{8,12},{12,16},{16,20},{20,24},{24,28},{1,5},{5,9},{9,... | collective-permute-start | bytes 393224 | tf_op jit(solution)/shard_map/while/body/eval_jaxpr/ppermute | solution.py:15
  167.9 6.9 %collective-permute-start.4 = (f32[1,2,64,256]{3,1,2,0:T(2,128)S(1)}, f32[1,2,64,256]{3,1,2,0:T(2,128)S(1)}, u32[]{:S(2)}, u32[]{:S(2)}) collective-permute-start(f32[1,2,64,256]{3,1,2,0:T(2,128)S(1)} %get-tuple-element.580), channel_id=1, source_target_pairs={{4,0},{8,4},{12,8},{16,12},{20,16},{24,20},{28,24},{5,1},{9,5},{13... | collective-permute-start | bytes 393224 | tf_op jit(solution)/shard_map/while/body/eval_jaxpr/ppermute | solution.py:15
  171.5 4.2 %copy-start.1 = (bf16[2,8,64,256]{3,2,1,0:T(8,128)(2,1)S(1)}, bf16[2,8,64,256]{3,2,1,0:T(8,128)(2,1)}, u32[]{:S(2)}) copy-start(bf16[2,8,64,256]{3,2,1,0:T(8,128)(2,1)} %get-tuple-element.605) | copy-start | bytes 1572868 | tf_op jit(solution)/shard_map/while
  175.8 0.8 copy-start.2
  177.5 11.0 %collective-permute-start.1 = (bf16[1,2,64,256]{3,2,1,0:T(8,128)(2,1)S(1)}, bf16[1,2,64,256]{3,2,1,0:T(8,128)(2,1)S(1)}, u32[]{:S(2)}, u32[]{:S(2)}) collective-permute-start(bf16[1,2,64,256]{3,2,1,0:T(8,128)(2,1)S(1)} %get-tuple-element.575), channel_id=1, source_target_pairs={{4,0},{8,4},{12,8},{16,12},{20,16},{24,20},{28,24},{5,1},{9,5},{13... | collective-permute-start | bytes 196616 | tf_op jit(solution)/shard_map/while/body/eval_jaxpr/ppermute | solution.py:28
  178.8 9.7 %collective-permute-start.2 = (bf16[1,2,64,256]{3,2,1,0:T(8,128)(2,1)S(1)}, bf16[1,2,64,256]{3,2,1,0:T(8,128)(2,1)S(1)}, u32[]{:S(2)}, u32[]{:S(2)}) collective-permute-start(bf16[1,2,64,256]{3,2,1,0:T(8,128)(2,1)S(1)} %get-tuple-element.577), channel_id=1, source_target_pairs={{0,4},{4,8},{8,12},{12,16},{16,20},{20,24},{24,28},{1,5},{5,9},{9,... | collective-permute-start | bytes 196616 | tf_op jit(solution)/shard_map/while/body/eval_jaxpr/ppermute | solution.py:26
  184.3 5.8 %collective-permute-start = (bf16[1,8,64,256]{3,1,2,0:T(8,128)(2,1)S(1)}, bf16[1,8,64,256]{3,1,2,0:T(8,128)(2,1)}, u32[]{:S(2)}, u32[]{:S(2)}) collective-permute-start(bf16[1,8,64,256]{3,1,2,0:T(8,128)(2,1)S(1)} %broadcast_select_fusion.2), channel_id=1, source_target_pairs={{1,0},{2,1},{3,2},{5,4},{6,5},{7,6},{9,8},{10,9},{11,10},{13,12},{... | collective-permute-start | bytes 786440 | tf_op jit(solution)/shard_map/while/body/eval_jaxpr/ppermute | solution.py:15
  195.3 1.0 copy-start
  202.0 0.7 copy-start.3
  205.8 7.9 %collective-permute-start.3 = (f32[1,2,64,256]{3,1,2,0:T(2,128)S(1)}, f32[1,2,64,256]{3,1,2,0:T(2,128)S(1)}, u32[]{:S(2)}, u32[]{:S(2)}) collective-permute-start(f32[1,2,64,256]{3,1,2,0:T(2,128)S(1)} %get-tuple-element.579), channel_id=1, source_target_pairs={{0,4},{4,8},{8,12},{12,16},{16,20},{20,24},{24,28},{1,5},{5,9},{9,... | collective-permute-start | bytes 393224 | tf_op jit(solution)/shard_map/while/body/eval_jaxpr/ppermute | solution.py:15
  209.9 6.9 %collective-permute-start.4 = (f32[1,2,64,256]{3,1,2,0:T(2,128)S(1)}, f32[1,2,64,256]{3,1,2,0:T(2,128)S(1)}, u32[]{:S(2)}, u32[]{:S(2)}) collective-permute-start(f32[1,2,64,256]{3,1,2,0:T(2,128)S(1)} %get-tuple-element.580), channel_id=1, source_target_pairs={{4,0},{8,4},{12,8},{16,12},{20,16},{24,20},{28,24},{5,1},{9,5},{13... | collective-permute-start | bytes 393224 | tf_op jit(solution)/shard_map/while/body/eval_jaxpr/ppermute | solution.py:15
  213.6 4.2 %copy-start.1 = (bf16[2,8,64,256]{3,2,1,0:T(8,128)(2,1)S(1)}, bf16[2,8,64,256]{3,2,1,0:T(8,128)(2,1)}, u32[]{:S(2)}) copy-start(bf16[2,8,64,256]{3,2,1,0:T(8,128)(2,1)} %get-tuple-element.605) | copy-start | bytes 1572868 | tf_op jit(solution)/shard_map/while
  217.8 0.8 copy-start.2
Sparse Core Ops, SparseCore 0:
  218.8 73.2 all-reduce.1
where the time goes:
time: 303 us; the launch traced here: 301 us
  waiting for transfers between devices  129 us (43%)
  starting transfers between devices  65.3 us (22%)
  local copies, waits for them, and re-layouts  41 us (14%)
  other arithmetic  33.1 us (11%)
  matrix products  17.6 us (6%)
  between operations  14.1 us (5%)
    psum x1, waiting for transfers between devices, per_device(): w_summed = lax.psum(w_total, 'lat')  73.4 us
    ppermute x15, waiting for transfers between devices, from_behind(): return lax.ppermute(block, axis, route)  55.5 us
    ppermute x15, starting transfers between devices, from_behind(): return lax.ppermute(block, axis, route)  35.1 us
    ppermute x5, starting transfers between devices, with_halo(): lax.ppermute(tail, axis, [(i, (i + 1) % count) for i in range(ends)])  23.7 us
    add x5, other arithmetic, advance(): return (grad_step, results, w_total + w_grad)  11.6 us
    another operation x10, local copies, waits for them, and re-layouts  8.33 us
    ppermute x5, starting transfers between devices, with_halo(): lax.ppermute(head, axis, [((i + 1) % count, i) for i in range(ends)])  6.46 us
    unnamed x4, local copies, waits for them, and re-layouts  6.11 us
  transfers between devices with their start and end apart: 26, of which 10 were waited for; matrix products, arithmetic and copies ran while one was open for 10% of the time, Pallas kernels for 0%

commit v1 on v0

v1 whole, which is shorter than its diff:
```python
import functools

import jax
import jax.numpy as jnp
from jax import lax
from jax.experimental import pallas as pl
from jax.experimental.pallas import tpu as pltpu
from jax.sharding import PartitionSpec as P

KB = 3
BLK = 64
HALO = 2
MB = 2
GRP = 4
SPAN = GRP + 2 * HALO
BF = jnp.bfloat16
F32 = jnp.float32
VM = pl.BlockSpec(memory_space=pltpu.VMEM)
ANY = pl.BlockSpec(memory_space=pl.ANY)
SM = pl.BlockSpec(memory_space=pltpu.SMEM)


def gelu_slope(value):
    return (
        0.5 * (1.0 + lax.erf(value * 0.7071067811865476))
        + value * jnp.exp(-0.5 * value * value) * 0.3989422804014327
    )


def params(mib=24):
    return pltpu.CompilerParams(vmem_limit_bytes=mib << 20)


def dot(a, b):
    return jnp.dot(a, b, preferred_element_type=F32)


def band_kernel(blocks, index_ref, mask_ref, quad_ref, band_ref, flip_ref, table_ref):
    first = lax.axis_index("lat") * blocks
    for b in range(blocks):
        for d in range(2 * HALO + 2):
            table_ref[b, d] = 0
        for j in range(index_ref.shape[1]):
            d = index_ref[b, j] - (first + b) + HALO
            table_ref[b, jnp.where(mask_ref[b, j] != 0, d, 2 * HALO + 1)] = j + 1
    empty = jnp.zeros((BLK, BLK), BF)
    for g in range(blocks // GRP):
        for r in range(GRP):
            b = g * GRP + r
            for k in range(KB):
                tiles = [empty] * r
                for d in range(2 * HALO + 1):
                    entry = table_ref[b, d]
                    tile = quad_ref[k, b, jnp.maximum(entry - 1, 0)]
                    tiles.append(jnp.where(entry > 0, tile, empty))
                tiles += [empty] * (GRP - 1 - r)
                row = k * GRP * BLK + r * BLK
                band_ref[g, row : row + BLK, :] = jnp.concatenate(tiles, axis=1)
        flip_ref[g] = band_ref[g].T


def band_call(block_index, block_mask, quad):
    blocks = quad.shape[1]
    groups = blocks // GRP
    return pl.pallas_call(
        functools.partial(band_kernel, blocks),
        out_shape=(
            pltpu.VMEM((groups, KB * GRP * BLK, SPAN * BLK), BF),
            pltpu.VMEM((groups, SPAN * BLK, KB * GRP * BLK), BF),
        ),
        in_specs=[SM, SM, VM],
        out_specs=(VM, VM),
        scratch_shapes=[pltpu.SMEM((blocks, 2 * HALO + 2), jnp.int32)],
        compiler_params=params(),
        name="band",
    )(block_index, block_mask, quad)


def hidden_kernel(x_ref, below_ref, above_ref, band_ref, w_ref, hid_ref, gp_ref, ext_ref, sems):
    rows = x_ref.shape[2]
    edge = HALO * BLK
    copies = [
        pltpu.make_async_copy(below_ref, ext_ref.at[:, pl.ds(0, edge)], sems.at[0]),
        pltpu.make_async_copy(x_ref.at[0], ext_ref.at[:, pl.ds(edge, rows)], sems.at[1]),
        pltpu.make_async_copy(above_ref, ext_ref.at[:, pl.ds(edge + rows, edge)], sems.at[2]),
    ]
    for c in copies:
        c.start()
    for c in copies:
        c.wait()
    size = GRP * BLK
    for m in range(MB):
        for g in range(rows // size):
            window = ext_ref[m, g * size : g * size + SPAN * BLK, :]
            hid = dot(band_ref[g], window).astype(BF)
            hid_ref[m, g] = hid
            z = dot(hid[:size], w_ref[0, 0])
            for k in range(1, KB):
                z += dot(hid[k * size : (k + 1) * size], w_ref[0, k])
            gp_ref[m, g * size : (g + 1) * size, :] = gelu_slope(z)


def hidden_call(x, below, above, band, weights):
    _, mb, rows, ch = x.shape
    groups = band.shape[0]
    return pl.pallas_call(
        hidden_kernel,
        out_shape=(
            pltpu.VMEM((mb, groups, KB * GRP * BLK, ch), BF),
            pltpu.VMEM((mb, rows, ch), F32),
        ),
        in_specs=[ANY, ANY, ANY, VM, VM],
        out_specs=(VM, VM),
        scratch_shapes=[
            pltpu.VMEM((mb, rows + 2 * HALO * BLK, ch), BF),
            pltpu.SemaphoreType.DMA((3,)),
        ],
        compiler_params=params(),
        name="hidden",
    )(x, below, above, band, weights)


def step_kernel(turn, first, main_ref, below_ref, above_ref, gp_ref, flip_ref, w_ref, *rest):
    olds, rest = ((), rest) if first else (rest[:4], rest[4:])
    out_ref, left_ref, right_ref, slope_ref, stack_ref, term_ref = rest
    rows = gp_ref.shape[1]
    size = GRP * BLK
    edge = HALO * BLK
    groups = rows // size

    @pl.when(lax.axis_index("section") == turn)
    def _():
        for m in range(MB):
            for g in range(groups):
                at = pl.ds(g * size, size)
                grad = main_ref[m, at, :].astype(F32)
                if not first:
                    parts = [grad[i * edge : (i + 1) * edge] for i in range(size // edge)]
                    if g == 0:
                        parts[0] += below_ref[m].astype(F32)
                    if g == groups - 1:
                        parts[-1] += above_ref[m].astype(F32)
                    grad = jnp.concatenate(parts, axis=0).astype(BF).astype(F32)
                slope = (grad * gp_ref[m, at, :]).astype(BF)
                slope_ref[m, at, :] = slope
                for k in range(KB):
                    back = lax.dot_general(
                        slope, w_ref[0, k], (((1,), (1,)), ((), ())), preferred_element_type=F32
                    )
                    stack_ref[k * size : (k + 1) * size, :] = back.astype(BF)
                term = dot(flip_ref[g], stack_ref[...])
                lap = 2 * edge
                low = g * size
                if g == 0:
                    left_ref[m] = term[:edge].astype(BF)
                    term_ref[low + edge : low + lap, :] = term[edge:lap] + grad[: lap - edge]
                else:
                    term_ref[low : low + lap, :] += term[:lap]
                    term_ref[low + edge : low + lap, :] += grad[: lap - edge]
                term_ref[low + lap : low + size + edge, :] = (
                    term[lap : size + edge] + grad[lap - edge :]
                )
                if g == groups - 1:
                    right_ref[m] = term[size + edge :].astype(BF)
                else:
                    term_ref[low + size + edge : low + size + lap, :] = term[size + edge :]
            out_ref[m] = term_ref[edge : edge + rows, :].astype(BF)


def step_call(turn, main, below, above, gp, flip, weights, olds):
    mb, rows, ch = gp.shape
    edge = HALO * BLK
    first = olds is None
    shapes = ((mb, rows, ch), (mb, edge, ch), (mb, edge, ch), (mb, rows, ch))
    args = (main, below, above, gp, flip, weights) + (() if first else tuple(olds))
    aliases = {} if first else {6 + i: i for i in range(4)}
    return pl.pallas_call(
        functools.partial(step_kernel, turn, first),
        out_shape=tuple(pltpu.VMEM(s, BF) for s in shapes),
        in_specs=[VM] * len(args),
        out_specs=(VM,) * 4,
        input_output_aliases=aliases,
        scratch_shapes=[
            pltpu.VMEM((KB * GRP * BLK, ch), BF),
            pltpu.VMEM((rows + 2 * edge, ch), F32),
        ],
        compiler_params=params(),
        name=f"step{turn}",
    )(*args)


def weight_kernel(n, hid_ref, slope_ref, *out_refs):
    piece = out_refs[0].shape[0]
    acc_ref = out_refs[-1]
    me = lax.axis_index("lat")
    size = GRP * BLK
    groups = hid_ref.shape[1]
    for k in range(KB):
        total = None
        for m in range(MB):
            for g in range(groups):
                part = lax.dot_general(
                    hid_ref[m, g, k * size : (k + 1) * size, :],
                    slope_ref[m, g * size : (g + 1) * size, :],
                    (((0,), (0,)), ((), ())),
                    preferred_element_type=F32,
                )
                total = part if total is None else total + part
        acc_ref[k * total.shape[0] : (k + 1) * total.shape[0], :] = total
    if n == 1:
        out_refs[0][...] = acc_ref[...]
        return
    out_refs[0][...] = acc_ref[pl.ds(pl.multiple_of(me * piece, piece), piece), :]
    for s in range(1, n):
        other = me ^ s
        out_refs[s][...] = acc_ref[pl.ds(pl.multiple_of(other * piece, piece), piece), :].astype(BF)


def weight_call(n, hid, slope):
    ch = slope.shape[2]
    piece = KB * ch // n
    return pl.pallas_call(
        functools.partial(weight_kernel, n),
        out_shape=(pltpu.VMEM((piece, ch), F32),) + (pltpu.VMEM((piece, ch), BF),) * (n - 1),
        in_specs=[VM] * 2,
        out_specs=(VM,) * n,
        scratch_shapes=[pltpu.VMEM((KB * ch, ch), F32)],
        compiler_params=params(),
        name="weight",
    )(hid, slope)


def sum_kernel(own_ref, *refs):
    total = own_ref[...]
    for ref in refs[:-1]:
        total += ref[...].astype(F32)
    refs[-1][...] = total.astype(BF)


def sum_call(own, others):
    return pl.pallas_call(
        sum_kernel,
        out_shape=pltpu.VMEM(own.shape, BF),
        in_specs=[VM] * (1 + len(others)),
        out_specs=VM,
        compiler_params=params(),
        name="sum",
    )(own, *others)


def close_kernel(n, main_ref, below_ref, above_ref, *refs):
    pieces, grad_ref, weight_ref = refs[:n], refs[n], refs[n + 1 :]
    rows = main_ref.shape[1]
    edge = HALO * BLK
    me = lax.axis_index("lat")
    for s in range(n):
        other, piece = me ^ s, pieces[s].shape[0]
        weight_ref[0][pl.ds(pl.multiple_of(other * piece, piece), piece), :] = pieces[s][...].astype(F32)
    for m in range(MB):
        low = main_ref[m, :edge, :].astype(F32) + below_ref[m].astype(F32)
        grad_ref[0, m, :edge, :] = low.astype(BF)
        grad_ref[0, m, edge : rows - edge, :] = main_ref[m, edge : rows - edge, :]
        high = main_ref[m, rows - edge :, :].astype(F32) + above_ref[m].astype(F32)
        grad_ref[0, m, rows - edge :, :] = high.astype(BF)


def close_call(main, below, above, pieces):
    mb, rows, ch = main.shape
    shapes = (jax.ShapeDtypeStruct((1, mb, rows, ch), BF),)
    if pieces:
        shapes += (jax.ShapeDtypeStruct((KB * ch, ch), F32),)
    return pl.pallas_call(
        functools.partial(close_kernel, len(pieces)),
        out_shape=shapes,
        in_specs=[VM] * (3 + len(pieces)),
        out_specs=(VM,) * len(shapes),
        compiler_params=params(),
        name="close",
    )(main, below, above, *pieces)


def per_device(saved_input, cotangent, quad_values, block_index, block_mask, weights):
    sections = lax.axis_size("section")
    lats = lax.axis_size("lat")
    edge = HALO * BLK
    rows = saved_input.shape[2]
    both = ("lat", "section")
    up = [(i, i + 1) for i in range(lats - 1)]
    down = [(i + 1, i) for i in range(lats - 1)]

    below = lax.ppermute(saved_input[0, :, rows - edge :], "lat", up)
    above = lax.ppermute(saved_input[0, :, :edge], "lat", down)
    band, flip = band_call(block_index, block_mask, quad_values)
    hid, gp = hidden_call(saved_input, below, above, band, weights)

    state, main = None, cotangent
    low = high = jnp.zeros((MB, edge, cotangent.shape[2]), BF)
    for turn in reversed(range(sections)):
        state = step_call(turn, main, low, high, gp, flip, weights, state)
        out, left, right, slope = state
        if turn > 0:
            main = lax.ppermute(out, "section", [(turn, turn - 1)])
            low = lax.ppermute(
                right, both, [(a * sections + turn, b * sections + turn - 1) for a, b in up]
            )
            high = lax.ppermute(
                left, both, [(a * sections + turn, b * sections + turn - 1) for a, b in down]
            )

    if lats & (lats - 1) == 0 and lats <= 8:
        partial_sums = weight_call(lats, hid, slope)
        met = [
            lax.ppermute(partial_sums[s], "lat", [(i, i ^ s) for i in range(lats)])
            for s in range(1, lats)
        ]
        low = lax.ppermute(right, "lat", up)
        high = lax.ppermute(left, "lat", down)
        mine = sum_call(partial_sums[0], met)
        pieces = [mine] + [
            lax.ppermute(mine, "lat", [(i, i ^ s) for i in range(lats)]) for s in range(1, lats)
        ]
    else:
        low = lax.ppermute(right, "lat", up)
        high = lax.ppermute(left, "lat", down)
        pieces = []
        w_sum = [lax.psum(weight_call(1, hid, slope)[0], "lat")]
    grad, *weight = close_call(out, low, high, pieces)
    weight = (weight or w_sum)[0]
    channels = saved_input.shape[3]
    return grad, weight.reshape(1, KB, channels, channels)


def solution(mesh):
    in_specs = (
        P("section", None, "lat", None),
        P(None, "lat", None),
        P(None, "lat", None, None, None),
        P("lat", None),
        P("lat", None),
        P("section", None, None, None),
    )
    out_specs = (P("section", None, "lat", None), P("section", None, None, None))
    return jax.shard_map(
        per_device, mesh=mesh, in_specs=in_specs, out_specs=out_specs, check_vma=False
    )
```

time: 303 us -> 93 us (0.31)
  waiting for transfers between devices: 129 us -> 39.5 us
  local copies, waits for them, and re-layouts: 41 us -> 3.98 us
  other arithmetic: 33.1 us -> 0 us
  starting transfers between devices: 65.3 us -> 40 us
  matrix products: 17.6 us -> 0 us
  between operations: 14.1 us -> 0.93 us
  Pallas kernels: 0 us -> 8.19 us
    psum x1 -> x0, waiting for transfers between devices: 73.4 us -> none  [per_device(): w_summed = lax.psum(w_total, 'lat')]
    ppermute x25 -> x27, starting transfers between devices: 65.3 us -> 40 us  [the longest x7 11.2 us: per_device(): lax.ppermute(partial_sums[s], 'lat', [(i, i ^ s) for i in range(lats)])]
    dot_general x12 -> x0, matrix products: 17.6 us -> none  [the longest x2 6.02 us: layer_terms(): jnp.einsum('bjr,mbjqc->mrqc', one_hot, terms, precision=lax.Precision.HIG...]
    ppermute x25 -> x27, waiting for transfers between devices: 55.6 us -> 39.5 us  [the longest x3 27.9 us: per_device(): lax.ppermute(left, both, [(a * sections + turn, b * sections + turn - 1)...]
    add x10 -> x0, other arithmetic: 12 us -> none  [the longest x5 11.6 us: advance(): return (grad_step, results, w_total + w_grad)]
    select_n x12 -> x0, other arithmetic: 9.91 us -> none  [the longest x5 5.55 us: advance(): incoming = jnp.where(section_here == sections - 1, own_grads, received)]
    another operation x10 -> x0, local copies, waits for them, and re-layouts: 8.33 us -> none
    pallas_call x0 -> x9, Pallas kernels: none -> 8.19 us  [the longest x1 2.8 us: hidden_call(): pl.pallas_call(hidden_kernel, out_shape=(pltpu.VMEM((mb, groups, KB * GRP...]
  transfers between devices with their start and end apart: 26 -> 27, of which waited for: 10 -> 8; matrix products, arithmetic and copies ran while one was open for 10% -> 0% of each run, Pallas kernels for 0% -> 2%
where the time goes in v1:
time: 93 us; the launch traced here: 92.6 us
  starting transfers between devices  40 us (43%)
  waiting for transfers between devices  39.5 us (42%)
  Pallas kernels  8.19 us (9%)
  local copies, waits for them, and re-layouts  3.98 us (4%)
  between operations  0.93 us (1%)
    ppermute x3, waiting for transfers between devices, per_device(): lax.ppermute(left, both, [(a * sections + turn, b * sections + turn - 1)...  27.9 us
    ppermute x7, starting transfers between devices, per_device(): lax.ppermute(partial_sums[s], 'lat', [(i, i ^ s) for i in range(lats)])  11.2 us
    ppermute x7, starting transfers between devices, per_device(): lax.ppermute(mine, 'lat', [(i, i ^ s) for i in range(lats)])  10 us
    ppermute x7, waiting for transfers between devices, per_device(): lax.ppermute(mine, 'lat', [(i, i ^ s) for i in range(lats)])  7.18 us
    ppermute x1, starting transfers between devices, per_device(): below = lax.ppermute(saved_input[0, :, rows - edge:], 'lat', up)  5.51 us
    ppermute x7, waiting for transfers between devices, per_device(): lax.ppermute(partial_sums[s], 'lat', [(i, i ^ s) for i in range(lats)])  4.36 us
    ppermute x1, starting transfers between devices, per_device(): low = lax.ppermute(right, 'lat', up)  3.41 us
    unnamed x12, local copies, waits for them, and re-layouts  2.93 us
  transfers between devices with their start and end apart: 27, of which 8 were waited for; matrix products, arithmetic and copies ran while one was open for 0% of the time, Pallas kernels for 2%

profile of v1, /device:TPU:0, one launch (start us, length us, event | category | flops | bytes accessed | tf_op | source)
XLA Modules:
  0.0 92.6 jit_solution(2129250763026036615)
XLA Ops:
  0.6 1.0 %slice_bitcast_fusion = (bf16[2,128,256]{2,1,0:T(8,128)(2,1)S(1)}, bf16[2,128,256]{2,1,0:T(8,128)(2,1)S(1)}) fusion(bf16[1,2,512,256]{3,2,1,0:T(8,128)(2,1)} %x_ref.1), kind=kLoop, calls=%fused_computation | loop fusion | bytes 524288 | tf_op jit(solution)/shard_map/squeeze | solution.py:292
  1.7 1.3 %collective-permute-start.1 = (bf16[2,128,256]{2,1,0:T(8,128)(2,1)S(1)}, bf16[2,128,256]{2,1,0:T(8,128)(2,1)S(1)}, u32[]{:S(2)}, u32[]{:S(2)}) collective-permute-start(bf16[2,128,256]{2,1,0:T(8,128)(2,1)S(1)} %get-tuple-element.62), channel_id=1, source_target_pairs={{4,0},{8,4},{12,8},{16,12},{20,16},{24,20},{28,24},{5,1},{9,5},{13... | collective-permute-start | bytes 393224 | tf_op jit(solution)/shard_map/ppermute | solution.py:292
  3.0 5.5 %collective-permute-start = (bf16[2,128,256]{2,1,0:T(8,128)(2,1)S(1)}, bf16[2,128,256]{2,1,0:T(8,128)(2,1)S(1)}, u32[]{:S(2)}, u32[]{:S(2)}) collective-permute-start(bf16[2,128,256]{2,1,0:T(8,128)(2,1)S(1)} %get-tuple-element.63), channel_id=1, source_target_pairs={{0,4},{4,8},{8,12},{12,16},{16,20},{20,24},{24,28},{1,5},{5,9},{9,... | collective-permute-start | bytes 393224 | tf_op jit(solution)/shard_map/ppermute | solution.py:291
  8.5 0.0 copy-start.1
  8.5 1.5 %copy-done.1 = bf16[3,8,5,64,64]{4,3,2,1,0:T(8,128)(2,1)S(1)} copy-done((bf16[3,8,5,64,64]{4,3,2,1,0:T(8,128)(2,1)S(1)}, bf16[3,8,5,64,64]{4,3,2,1,0:T(8,128)(2,1)}, u32[]{:S(2)}) %copy-start.1) | copy-done | bytes 983064
  10.0 0.7 copy-done.4
  10.7 0.7 copy-done.5
  11.4 1.6 %band.1 = (bf16[2,768,512]{2,1,0:T(8,128)(2,1)S(1)}, bf16[2,512,768]{2,1,0:T(8,128)(2,1)S(1)}) custom-call(s32[8,5]{1,0:T(8,128)S(1)} %copy-done.4, s32[8,5]{1,0:T(8,128)S(1)} %copy-done.5, bf16[3,8,5,64,64]{4,3,2,1,0:T(8,128)(2,1)S(1)} %copy-done.1), custom_call_target="tpu_custom_call" | custom-call | tf_op jit(solution)/shard_map/band/pallas_call | solution.py:65
  13.0 0.0 copy-start.3
  13.0 0.0 collective-permute-done.1.above_ref
  13.0 0.0 collective-permute-done.below_ref
  13.1 2.8 %hidden.1 = (bf16[2,2,768,256]{3,2,1,0:T(8,128)(2,1)S(1)}, f32[2,512,256]{2,1,0:T(8,128)S(1)}) custom-call(bf16[1,2,512,256]{3,2,1,0:T(8,128)(2,1)S(1)} %copy-done.2, bf16[2,128,256]{2,1,0:T(8,128)(2,1)S(1)} %collective-permute-done.below_ref, bf16[2,128,256]{2,1,0:T(8,128)(2,1)S(1)} %collective-permute-done.1.above_ref, ...), custom_call_target="tpu_custom_call" | custom-call | tf_op jit(solution)/shard_map/hidden/pallas_call | solution.py:106
  15.9 0.7 collective-permute-start.2
  16.6 0.7 collective-permute-start.3
  17.3 0.7 collective-permute-start.4
  18.0 0.0 collective-permute-done.3.below_ref
  18.0 0.0 collective-permute-done.4.above_ref
  18.0 0.0 collective-permute-done.2.main_ref
  18.0 0.7 collective-permute-start.5
  18.7 0.7 collective-permute-start.6
  19.4 0.7 collective-permute-start.7
  20.1 0.0 collective-permute-done.6.below_ref
  20.1 0.0 collective-permute-done.7.above_ref
  20.1 0.0 collective-permute-done.5.main_ref
  20.1 1.3 %collective-permute-start.8 = (bf16[2,512,256]{2,1,0:T(8,128)(2,1)S(1)}, bf16[2,512,256]{2,1,0:T(8,128)(2,1)S(1)}, u32[]{:S(2)}, u32[]{:S(2)}) collective-permute-start(bf16[2,512,256]{2,1,0:T(8,128)(2,1)S(1)} %get-tuple-element.43.rest_0_), channel_id=1, source_target_pairs={{1,0},{5,4},{9,8},{13,12},{17,16},{21,20},{25,24},{29,28}} | collective-permute-start | bytes 1572872 | tf_op jit(solution)/shard_map/ppermute | solution.py:302
  21.4 0.7 collective-permute-start.9
  22.1 1.3 %collective-permute-start.10 = (bf16[2,128,256]{2,1,0:T(8,128)(2,1)S(1)}, bf16[2,128,256]{2,1,0:T(8,128)(2,1)S(1)}, u32[]{:S(2)}, u32[]{:S(2)}) collective-permute-start(bf16[2,128,256]{2,1,0:T(8,128)(2,1)S(1)} %get-tuple-element.45.rest_1_), channel_id=1, source_target_pairs={{5,0},{9,4},{13,8},{17,12},{21,16},{25,20},{29,24}} | collective-permute-start | bytes 393224 | tf_op jit(solution)/shard_map/ppermute | solution.py:306
  23.4 0.0 collective-permute-done.9.below_ref
  23.4 27.9 %collective-permute-done.10.above_ref = bf16[2,128,256]{2,1,0:T(8,128)(2,1)S(1)} collective-permute-done((bf16[2,128,256]{2,1,0:T(8,128)(2,1)S(1)}, bf16[2,128,256]{2,1,0:T(8,128)(2,1)S(1)}, u32[]{:S(2)}, u32[]{:S(2)}) %collective-permute-start.10) | collective-permute-done | bytes 131104 | tf_op jit(solution)/shard_map/ppermute | solution.py:306
  51.3 0.0 collective-permute-done.8.main_ref
  51.3 1.9 %step0.1 = (bf16[2,512,256]{2,1,0:T(8,128)(2,1)S(1)}, bf16[2,128,256]{2,1,0:T(8,128)(2,1)S(1)}, bf16[2,128,256]{2,1,0:T(8,128)(2,1)S(1)}, bf16[2,512,256]{2,1,0:T(8,128)(2,1)S(1)}) custom-call(bf16[2,512,256]{2,1,0:T(8,128)(2,1)S(1)} %collective-permute-done.8.main_ref, ...), custom_call_target="tpu_custom_call", output_to_operand_aliasing={{0}: (6, {}), {1}: (7, {}), {2}: (8, {}), {3}: (9, {})} | custom-call | tf_op jit(solution)/shard_map/step0/pallas_call | solution.py:177
  53.3 0.7 weight.1
  53.9 1.3 %collective-permute-start.13 = (bf16[96,256]{1,0:T(8,128)(2,1)S(1)}, bf16[96,256]{1,0:T(8,128)(2,1)S(1)}, u32[]{:S(2)}, u32[]{:S(2)}) collective-permute-start(bf16[96,256]{1,0:T(8,128)(2,1)S(1)} %get-tuple-element.53), channel_id=1, source_target_pairs={{0,4},{4,0},{8,12},{12,8},{16,20},{20,16},{24,28},{28,24},{1,5},{5... | collective-permute-start | bytes 147464 | tf_op jit(solution)/shard_map/ppermute | solution.py:313
  55.3 1.6 %collective-permute-start.14 = (bf16[96,256]{1,0:T(8,128)(2,1)S(1)}, bf16[96,256]{1,0:T(8,128)(2,1)S(1)}, u32[]{:S(2)}, u32[]{:S(2)}) collective-permute-start(bf16[96,256]{1,0:T(8,128)(2,1)S(1)} %get-tuple-element.54), channel_id=1, source_target_pairs={{0,8},{4,12},{8,0},{12,4},{16,24},{20,28},{24,16},{28,20},{1,9},{5... | collective-permute-start | bytes 147464 | tf_op jit(solution)/shard_map/ppermute | solution.py:313
  56.8 0.6 collective-permute-start.15
  57.5 2.6 %collective-permute-start.16 = (bf16[96,256]{1,0:T(8,128)(2,1)S(1)}, bf16[96,256]{1,0:T(8,128)(2,1)S(1)}, u32[]{:S(2)}, u32[]{:S(2)}) collective-permute-start(bf16[96,256]{1,0:T(8,128)(2,1)S(1)} %get-tuple-element.56), channel_id=1, source_target_pairs={{0,16},{4,20},{8,24},{12,28},{16,0},{20,4},{24,8},{28,12},{1,17},{... | collective-permute-start | bytes 147464 | tf_op jit(solution)/shard_map/ppermute | solution.py:313
  60.0 1.1 %collective-permute-start.17 = (bf16[96,256]{1,0:T(8,128)(2,1)S(1)}, bf16[96,256]{1,0:T(8,128)(2,1)S(1)}, u32[]{:S(2)}, u32[]{:S(2)}) collective-permute-start(bf16[96,256]{1,0:T(8,128)(2,1)S(1)} %get-tuple-element.57), channel_id=1, source_target_pairs={{0,20},{4,16},{8,28},{12,24},{16,4},{20,0},{24,12},{28,8},{1,21},{... | collective-permute-start | bytes 147464 | tf_op jit(solution)/shard_map/ppermute | solution.py:313
  61.1 1.6 %collective-permute-start.18 = (bf16[96,256]{1,0:T(8,128)(2,1)S(1)}, bf16[96,256]{1,0:T(8,128)(2,1)S(1)}, u32[]{:S(2)}, u32[]{:S(2)}) collective-permute-start(bf16[96,256]{1,0:T(8,128)(2,1)S(1)} %get-tuple-element.58), channel_id=1, source_target_pairs={{0,24},{4,28},{8,16},{12,20},{16,8},{20,12},{24,0},{28,4},{1,25},{... | collective-permute-start | bytes 147464 | tf_op jit(solution)/shard_map/ppermute | solution.py:313
  62.7 0.0 collective-permute-done.14.refs_1_
  62.7 2.4 %collective-permute-start.19 = (bf16[96,256]{1,0:T(8,128)(2,1)S(1)}, bf16[96,256]{1,0:T(8,128)(2,1)S(1)}, u32[]{:S(2)}, u32[]{:S(2)}) collective-permute-start(bf16[96,256]{1,0:T(8,128)(2,1)S(1)} %get-tuple-element.59), channel_id=1, source_target_pairs={{0,28},{4,24},{8,20},{12,16},{16,12},{20,8},{24,4},{28,0},{1,29},{... | collective-permute-start | bytes 147464 | tf_op jit(solution)/shard_map/ppermute | solution.py:313
  65.1 0.0 collective-permute-done.15.refs_2_
  65.1 0.0 collective-permute-done.16.refs_3_
  65.1 0.8 collective-permute-done.17.refs_4_
  65.9 1.0 %collective-permute-done.18.refs_5_ = bf16[96,256]{1,0:T(8,128)(2,1)S(1)} collective-permute-done((bf16[96,256]{1,0:T(8,128)(2,1)S(1)}, bf16[96,256]{1,0:T(8,128)(2,1)S(1)}, u32[]{:S(2)}, u32[]{:S(2)}) %collective-permute-start.18) | collective-permute-done | bytes 49184 | tf_op jit(solution)/shard_map/ppermute | solution.py:313
  67.0 2.5 %collective-permute-done.19.refs_6_ = bf16[96,256]{1,0:T(8,128)(2,1)S(1)} collective-permute-done((bf16[96,256]{1,0:T(8,128)(2,1)S(1)}, bf16[96,256]{1,0:T(8,128)(2,1)S(1)}, u32[]{:S(2)}, u32[]{:S(2)}) %collective-permute-start.19) | collective-permute-done | bytes 49184 | tf_op jit(solution)/shard_map/ppermute | solution.py:313
  69.5 0.1 sum.1.refs_0_
  69.5 2.5 %collective-permute-start.26 = (bf16[96,256]{1,0:T(8,128)(2,1)S(1)}, bf16[96,256]{1,0:T(8,128)(2,1)S(1)}, u32[]{:S(2)}, u32[]{:S(2)}) collective-permute-start(bf16[96,256]{1,0:T(8,128)(2,1)S(1)} %sum.1.refs_0_), channel_id=1, source_target_pairs={{0,28},{4,24},{8,20},{12,16},{16,12},{20,8},{24,4},{28,0},{1,29},{... | collective-permute-start | bytes 147464 | tf_op jit(solution)/shard_map/ppermute | solution.py:320
  72.0 3.4 %collective-permute-start.11 = (bf16[2,128,256]{2,1,0:T(8,128)(2,1)S(1)}, bf16[2,128,256]{2,1,0:T(8,128)(2,1)S(1)}, u32[]{:S(2)}, u32[]{:S(2)}) collective-permute-start(bf16[2,128,256]{2,1,0:T(8,128)(2,1)S(1)} %get-tuple-element.48), channel_id=1, source_target_pairs={{0,4},{4,8},{8,12},{12,16},{16,20},{20,24},{24,28},{1,5},{5,9},{9,... | collective-permute-start | bytes 393224 | tf_op jit(solution)/shard_map/ppermute | solution.py:316
  75.5 1.3 %collective-permute-start.12 = (bf16[2,128,256]{2,1,0:T(8,128)(2,1)S(1)}, bf16[2,128,256]{2,1,0:T(8,128)(2,1)S(1)}, u32[]{:S(2)}, u32[]{:S(2)}) collective-permute-start(bf16[2,128,256]{2,1,0:T(8,128)(2,1)S(1)} %get-tuple-element.49), channel_id=1, source_target_pairs={{4,0},{8,4},{12,8},{16,12},{20,16},{24,20},{28,24},{5,1},{9,5},{13... | collective-permute-start | bytes 393224 | tf_op jit(solution)/shard_map/ppermute | solution.py:317
  76.8 4.2 %collective-permute-start.25 = (bf16[96,256]{1,0:T(8,128)(2,1)S(1)}, bf16[96,256]{1,0:T(8,128)(2,1)S(1)}, u32[]{:S(2)}, u32[]{:S(2)}) collective-permute-start(bf16[96,256]{1,0:T(8,128)(2,1)S(1)} %sum.1.refs_0_), channel_id=1, source_target_pairs={{0,24},{4,28},{8,16},{12,20},{16,8},{20,12},{24,0},{28,4},{1,25},{... | collective-permute-start | bytes 147464 | tf_op jit(solution)/shard_map/ppermute | solution.py:320
  80.9 0.0 collective-permute-start.24
  80.9 0.0 collective-permute-done.26.refs_7_
  80.9 2.2 %collective-permute-start.23 = (bf16[96,256]{1,0:T(8,128)(2,1)S(1)}, bf16[96,256]{1,0:T(8,128)(2,1)S(1)}, u32[]{:S(2)}, u32[]{:S(2)}) collective-permute-start(bf16[96,256]{1,0:T(8,128)(2,1)S(1)} %sum.1.refs_0_), channel_id=1, source_target_pairs={{0,16},{4,20},{8,24},{12,28},{16,0},{20,4},{24,8},{28,12},{1,17},{... | collective-permute-start | bytes 147464 | tf_op jit(solution)/shard_map/ppermute | solution.py:320
  83.2 1.1 %collective-permute-done.25.refs_6_ = bf16[96,256]{1,0:T(8,128)(2,1)S(1)} collective-permute-done((bf16[96,256]{1,0:T(8,128)(2,1)S(1)}, bf16[96,256]{1,0:T(8,128)(2,1)S(1)}, u32[]{:S(2)}, u32[]{:S(2)}) %collective-permute-start.25) | collective-permute-done | bytes 49184 | tf_op jit(solution)/shard_map/ppermute | solution.py:320
  84.3 3.0 %collective-permute-done.24.refs_5_ = bf16[96,256]{1,0:T(8,128)(2,1)S(1)} collective-permute-done((bf16[96,256]{1,0:T(8,128)(2,1)S(1)}, bf16[96,256]{1,0:T(8,128)(2,1)S(1)}, u32[]{:S(2)}, u32[]{:S(2)}) %collective-permute-start.24) | collective-permute-done | bytes 49184 | tf_op jit(solution)/shard_map/ppermute | solution.py:320
  87.3 0.0 collective-permute-start.21
  87.3 0.0 collective-permute-done.23.refs_4_
  87.4 1.1 %collective-permute-start.20 = (bf16[96,256]{1,0:T(8,128)(2,1)S(1)}, bf16[96,256]{1,0:T(8,128)(2,1)S(1)}, u32[]{:S(2)}, u32[]{:S(2)}) collective-permute-start(bf16[96,256]{1,0:T(8,128)(2,1)S(1)} %sum.1.refs_0_), channel_id=1, source_target_pairs={{0,4},{4,0},{8,12},{12,8},{16,20},{20,16},{24,28},{28,24},{1,5},{5... | collective-permute-start | bytes 147464 | tf_op jit(solution)/shard_map/ppermute | solution.py:320
  88.4 0.9 collective-permute-done.22.refs_3_
  89.3 2.1 %collective-permute-done.21.refs_2_ = bf16[96,256]{1,0:T(8,128)(2,1)S(1)} collective-permute-done((bf16[96,256]{1,0:T(8,128)(2,1)S(1)}, bf16[96,256]{1,0:T(8,128)(2,1)S(1)}, u32[]{:S(2)}, u32[]{:S(2)}) %collective-permute-start.21) | collective-permute-done | bytes 49184 | tf_op jit(solution)/shard_map/ppermute | solution.py:320
  91.4 0.0 collective-permute-done.20.refs_1_
  91.4 0.0 collective-permute-done.11.below_ref
  91.4 0.0 collective-permute-done.12.above_ref
  91.5 1.1 %close.1 = (bf16[1,2,512,256]{3,2,1,0:T(8,128)(2,1)}, f32[768,256]{1,0:T(8,128)}) custom-call(bf16[2,512,256]{2,1,0:T(8,128)(2,1)S(1)} %get-tuple-element.47.main_ref, bf16[2,128,256]{2,1,0:T(8,128)(2,1)S(1)} %collective-permute-done.11.below_ref, bf16[2,128,256]{2,1,0:T(8,128)(2,1)S(1)} %collective-permute-done.12.above_ref, ...), custom_call_target="tpu_custom_call" | custom-call | tf_op jit(solution)/shard_map/close/pallas_call | solution.py:272
  (13 shorter events, 0.1 us)
Async XLA Ops:
  0.6 12.4 %copy-start = (bf16[1,3,256,256]{3,2,1,0:T(8,128)(2,1)S(1)}, bf16[1,3,256,256]{3,2,1,0:T(8,128)(2,1)}, u32[]{:S(2)}) copy-start(bf16[1,3,256,256]{3,2,1,0:T(8,128)(2,1)} %w_ref.9) | copy-start | bytes 1179652
  1.7 11.3 %collective-permute-start.1 = (bf16[2,128,256]{2,1,0:T(8,128)(2,1)S(1)}, bf16[2,128,256]{2,1,0:T(8,128)(2,1)S(1)}, u32[]{:S(2)}, u32[]{:S(2)}) collective-permute-start(bf16[2,128,256]{2,1,0:T(8,128)(2,1)S(1)} %get-tuple-element.62), channel_id=1, source_target_pairs={{4,0},{8,4},{12,8},{16,12},{20,16},{24,20},{28,24},{5,1},{9,5},{13... | collective-permute-start | bytes 393224 | tf_op jit(solution)/shard_map/ppermute | solution.py:292
  3.0 10.1 %collective-permute-start = (bf16[2,128,256]{2,1,0:T(8,128)(2,1)S(1)}, bf16[2,128,256]{2,1,0:T(8,128)(2,1)S(1)}, u32[]{:S(2)}, u32[]{:S(2)}) collective-permute-start(bf16[2,128,256]{2,1,0:T(8,128)(2,1)S(1)} %get-tuple-element.63), channel_id=1, source_target_pairs={{0,4},{4,8},{8,12},{12,16},{16,20},{20,24},{24,28},{1,5},{5,9},{9,... | collective-permute-start | bytes 393224 | tf_op jit(solution)/shard_map/ppermute | solution.py:291
  8.5 1.5 %copy-start.1 = (bf16[3,8,5,64,64]{4,3,2,1,0:T(8,128)(2,1)S(1)}, bf16[3,8,5,64,64]{4,3,2,1,0:T(8,128)(2,1)}, u32[]{:S(2)}) copy-start(bf16[3,8,5,64,64]{4,3,2,1,0:T(8,128)(2,1)} %quad_ref.1) | copy-start | bytes 2949124
  10.0 0.7 copy-start.4
  10.7 0.7 copy-start.5
  11.4 1.6 %copy-start.2 = (bf16[1,2,512,256]{3,2,1,0:T(8,128)(2,1)S(1)}, bf16[1,2,512,256]{3,2,1,0:T(8,128)(2,1)}, u32[]{:S(2)}) copy-start(bf16[1,2,512,256]{3,2,1,0:T(8,128)(2,1)} %x_ref.1) | copy-start | bytes 1572868
  13.0 2.9 %copy-start.3 = (bf16[2,512,256]{2,1,0:T(8,128)(2,1)S(1)}, bf16[2,512,256]{2,1,0:T(8,128)(2,1)}, u32[]{:S(2)}) copy-start(bf16[2,512,256]{2,1,0:T(8,128)(2,1)} %main_ref.1) | copy-start | bytes 1572868
  15.9 2.1 %collective-permute-start.2 = (bf16[2,512,256]{2,1,0:T(8,128)(2,1)S(1)}, bf16[2,512,256]{2,1,0:T(8,128)(2,1)S(1)}, u32[]{:S(2)}, u32[]{:S(2)}) collective-permute-start(bf16[2,512,256]{2,1,0:T(8,128)(2,1)S(1)} %get-tuple-element.35.rest_0_), channel_id=1, source_target_pairs={{3,2},{7,6},{11,10},{15,14},{19,18},{23,22},{27,26},{31,30}} | collective-permute-start | bytes 1572872 | tf_op jit(solution)/shard_map/ppermute | solution.py:302
  16.6 1.4 %collective-permute-start.3 = (bf16[2,128,256]{2,1,0:T(8,128)(2,1)S(1)}, bf16[2,128,256]{2,1,0:T(8,128)(2,1)S(1)}, u32[]{:S(2)}, u32[]{:S(2)}) collective-permute-start(bf16[2,128,256]{2,1,0:T(8,128)(2,1)S(1)} %get-tuple-element.36.rest_2_), channel_id=1, source_target_pairs={{3,6},{7,10},{11,14},{15,18},{19,22},{23,26},{27,30}} | collective-permute-start | bytes 393224 | tf_op jit(solution)/shard_map/ppermute | solution.py:303
  17.3 0.7 collective-permute-start.4
  18.0 2.1 %collective-permute-start.5 = (bf16[2,512,256]{2,1,0:T(8,128)(2,1)S(1)}, bf16[2,512,256]{2,1,0:T(8,128)(2,1)S(1)}, u32[]{:S(2)}, u32[]{:S(2)}) collective-permute-start(bf16[2,512,256]{2,1,0:T(8,128)(2,1)S(1)} %get-tuple-element.39.rest_0_), channel_id=1, source_target_pairs={{2,1},{6,5},{10,9},{14,13},{18,17},{22,21},{26,25},{30,29}} | collective-permute-start | bytes 1572872 | tf_op jit(solution)/shard_map/ppermute | solution.py:302
  18.7 1.4 %collective-permute-start.6 = (bf16[2,128,256]{2,1,0:T(8,128)(2,1)S(1)}, bf16[2,128,256]{2,1,0:T(8,128)(2,1)S(1)}, u32[]{:S(2)}, u32[]{:S(2)}) collective-permute-start(bf16[2,128,256]{2,1,0:T(8,128)(2,1)S(1)} %get-tuple-element.40.rest_2_), channel_id=1, source_target_pairs={{2,5},{6,9},{10,13},{14,17},{18,21},{22,25},{26,29}} | collective-permute-start | bytes 393224 | tf_op jit(solution)/shard_map/ppermute | solution.py:303
  19.4 0.7 collective-permute-start.7
  20.1 31.2 %collective-permute-start.8 = (bf16[2,512,256]{2,1,0:T(8,128)(2,1)S(1)}, bf16[2,512,256]{2,1,0:T(8,128)(2,1)S(1)}, u32[]{:S(2)}, u32[]{:S(2)}) collective-permute-start(bf16[2,512,256]{2,1,0:T(8,128)(2,1)S(1)} %get-tuple-element.43.rest_0_), channel_id=1, source_target_pairs={{1,0},{5,4},{9,8},{13,12},{17,16},{21,20},{25,24},{29,28}} | collective-permute-start | bytes 1572872 | tf_op jit(solution)/shard_map/ppermute | solution.py:302
  21.4 2.0 %collective-permute-start.9 = (bf16[2,128,256]{2,1,0:T(8,128)(2,1)S(1)}, bf16[2,128,256]{2,1,0:T(8,128)(2,1)S(1)}, u32[]{:S(2)}, u32[]{:S(2)}) collective-permute-start(bf16[2,128,256]{2,1,0:T(8,128)(2,1)S(1)} %get-tuple-element.44.rest_2_), channel_id=1, source_target_pairs={{1,4},{5,8},{9,12},{13,16},{17,20},{21,24},{25,28}} | collective-permute-start | bytes 393224 | tf_op jit(solution)/shard_map/ppermute | solution.py:303
  22.1 29.2 %collective-permute-start.10 = (bf16[2,128,256]{2,1,0:T(8,128)(2,1)S(1)}, bf16[2,128,256]{2,1,0:T(8,128)(2,1)S(1)}, u32[]{:S(2)}, u32[]{:S(2)}) collective-permute-start(bf16[2,128,256]{2,1,0:T(8,128)(2,1)S(1)} %get-tuple-element.45.rest_1_), channel_id=1, source_target_pairs={{5,0},{9,4},{13,8},{17,12},{21,16},{25,20},{29,24}} | collective-permute-start | bytes 393224 | tf_op jit(solution)/shard_map/ppermute | solution.py:306
  53.9 7.2 %collective-permute-start.13 = (bf16[96,256]{1,0:T(8,128)(2,1)S(1)}, bf16[96,256]{1,0:T(8,128)(2,1)S(1)}, u32[]{:S(2)}, u32[]{:S(2)}) collective-permute-start(bf16[96,256]{1,0:T(8,128)(2,1)S(1)} %get-tuple-element.53), channel_id=1, source_target_pairs={{0,4},{4,0},{8,12},{12,8},{16,20},{20,16},{24,28},{28,24},{1,5},{5... | collective-permute-start | bytes 147464 | tf_op jit(solution)/shard_map/ppermute | solution.py:313
  55.3 7.4 %collective-permute-start.14 = (bf16[96,256]{1,0:T(8,128)(2,1)S(1)}, bf16[96,256]{1,0:T(8,128)(2,1)S(1)}, u32[]{:S(2)}, u32[]{:S(2)}) collective-permute-start(bf16[96,256]{1,0:T(8,128)(2,1)S(1)} %get-tuple-element.54), channel_id=1, source_target_pairs={{0,8},{4,12},{8,0},{12,4},{16,24},{20,28},{24,16},{28,20},{1,9},{5... | collective-permute-start | bytes 147464 | tf_op jit(solution)/shard_map/ppermute | solution.py:313
  56.8 8.3 %collective-permute-start.15 = (bf16[96,256]{1,0:T(8,128)(2,1)S(1)}, bf16[96,256]{1,0:T(8,128)(2,1)S(1)}, u32[]{:S(2)}, u32[]{:S(2)}) collective-permute-start(bf16[96,256]{1,0:T(8,128)(2,1)S(1)} %get-tuple-element.55), channel_id=1, source_target_pairs={{0,12},{4,8},{8,4},{12,0},{16,28},{20,24},{24,20},{28,16},{1,13},{... | collective-permute-start | bytes 147464 | tf_op jit(solution)/shard_map/ppermute | solution.py:313
  57.5 7.7 %collective-permute-start.16 = (bf16[96,256]{1,0:T(8,128)(2,1)S(1)}, bf16[96,256]{1,0:T(8,128)(2,1)S(1)}, u32[]{:S(2)}, u32[]{:S(2)}) collective-permute-start(bf16[96,256]{1,0:T(8,128)(2,1)S(1)} %get-tuple-element.56), channel_id=1, source_target_pairs={{0,16},{4,20},{8,24},{12,28},{16,0},{20,4},{24,8},{28,12},{1,17},{... | collective-permute-start | bytes 147464 | tf_op jit(solution)/shard_map/ppermute | solution.py:313
  60.0 5.9 %collective-permute-start.17 = (bf16[96,256]{1,0:T(8,128)(2,1)S(1)}, bf16[96,256]{1,0:T(8,128)(2,1)S(1)}, u32[]{:S(2)}, u32[]{:S(2)}) collective-permute-start(bf16[96,256]{1,0:T(8,128)(2,1)S(1)} %get-tuple-element.57), channel_id=1, source_target_pairs={{0,20},{4,16},{8,28},{12,24},{16,4},{20,0},{24,12},{28,8},{1,21},{... | collective-permute-start | bytes 147464 | tf_op jit(solution)/shard_map/ppermute | solution.py:313
  61.1 5.9 %collective-permute-start.18 = (bf16[96,256]{1,0:T(8,128)(2,1)S(1)}, bf16[96,256]{1,0:T(8,128)(2,1)S(1)}, u32[]{:S(2)}, u32[]{:S(2)}) collective-permute-start(bf16[96,256]{1,0:T(8,128)(2,1)S(1)} %get-tuple-element.58), channel_id=1, source_target_pairs={{0,24},{4,28},{8,16},{12,20},{16,8},{20,12},{24,0},{28,4},{1,25},{... | collective-permute-start | bytes 147464 | tf_op jit(solution)/shard_map/ppermute | solution.py:313
  62.7 6.8 %collective-permute-start.19 = (bf16[96,256]{1,0:T(8,128)(2,1)S(1)}, bf16[96,256]{1,0:T(8,128)(2,1)S(1)}, u32[]{:S(2)}, u32[]{:S(2)}) collective-permute-start(bf16[96,256]{1,0:T(8,128)(2,1)S(1)} %get-tuple-element.59), channel_id=1, source_target_pairs={{0,28},{4,24},{8,20},{12,16},{16,12},{20,8},{24,4},{28,0},{1,29},{... | collective-permute-start | bytes 147464 | tf_op jit(solution)/shard_map/ppermute | solution.py:313
  69.5 11.4 %collective-permute-start.26 = (bf16[96,256]{1,0:T(8,128)(2,1)S(1)}, bf16[96,256]{1,0:T(8,128)(2,1)S(1)}, u32[]{:S(2)}, u32[]{:S(2)}) collective-permute-start(bf16[96,256]{1,0:T(8,128)(2,1)S(1)} %sum.1.refs_0_), channel_id=1, source_target_pairs={{0,28},{4,24},{8,20},{12,16},{16,12},{20,8},{24,4},{28,0},{1,29},{... | collective-permute-start | bytes 147464 | tf_op jit(solution)/shard_map/ppermute | solution.py:320
  72.0 19.4 %collective-permute-start.11 = (bf16[2,128,256]{2,1,0:T(8,128)(2,1)S(1)}, bf16[2,128,256]{2,1,0:T(8,128)(2,1)S(1)}, u32[]{:S(2)}, u32[]{:S(2)}) collective-permute-start(bf16[2,128,256]{2,1,0:T(8,128)(2,1)S(1)} %get-tuple-element.48), channel_id=1, source_target_pairs={{0,4},{4,8},{8,12},{12,16},{16,20},{20,24},{24,28},{1,5},{5,9},{9,... | collective-permute-start | bytes 393224 | tf_op jit(solution)/shard_map/ppermute | solution.py:316
  75.5 16.0 %collective-permute-start.12 = (bf16[2,128,256]{2,1,0:T(8,128)(2,1)S(1)}, bf16[2,128,256]{2,1,0:T(8,128)(2,1)S(1)}, u32[]{:S(2)}, u32[]{:S(2)}) collective-permute-start(bf16[2,128,256]{2,1,0:T(8,128)(2,1)S(1)} %get-tuple-element.49), channel_id=1, source_target_pairs={{4,0},{8,4},{12,8},{16,12},{20,16},{24,20},{28,24},{5,1},{9,5},{13... | collective-permute-start | bytes 393224 | tf_op jit(solution)/shard_map/ppermute | solution.py:317
  76.8 7.6 %collective-permute-start.25 = (bf16[96,256]{1,0:T(8,128)(2,1)S(1)}, bf16[96,256]{1,0:T(8,128)(2,1)S(1)}, u32[]{:S(2)}, u32[]{:S(2)}) collective-permute-start(bf16[96,256]{1,0:T(8,128)(2,1)S(1)} %sum.1.refs_0_), channel_id=1, source_target_pairs={{0,24},{4,28},{8,16},{12,20},{16,8},{20,12},{24,0},{28,4},{1,25},{... | collective-permute-start | bytes 147464 | tf_op jit(solution)/shard_map/ppermute | solution.py:320
  80.9 6.4 %collective-permute-start.24 = (bf16[96,256]{1,0:T(8,128)(2,1)S(1)}, bf16[96,256]{1,0:T(8,128)(2,1)S(1)}, u32[]{:S(2)}, u32[]{:S(2)}) collective-permute-start(bf16[96,256]{1,0:T(8,128)(2,1)S(1)} %sum.1.refs_0_), channel_id=1, source_target_pairs={{0,20},{4,16},{8,28},{12,24},{16,4},{20,0},{24,12},{28,8},{1,21},{... | collective-permute-start | bytes 147464 | tf_op jit(solution)/shard_map/ppermute | solution.py:320
  80.9 6.4 %collective-permute-start.23 = (bf16[96,256]{1,0:T(8,128)(2,1)S(1)}, bf16[96,256]{1,0:T(8,128)(2,1)S(1)}, u32[]{:S(2)}, u32[]{:S(2)}) collective-permute-start(bf16[96,256]{1,0:T(8,128)(2,1)S(1)} %sum.1.refs_0_), channel_id=1, source_target_pairs={{0,16},{4,20},{8,24},{12,28},{16,0},{20,4},{24,8},{28,12},{1,17},{... | collective-permute-start | bytes 147464 | tf_op jit(solution)/shard_map/ppermute | solution.py:320
  84.3 5.0 %collective-permute-start.22 = (bf16[96,256]{1,0:T(8,128)(2,1)S(1)}, bf16[96,256]{1,0:T(8,128)(2,1)S(1)}, u32[]{:S(2)}, u32[]{:S(2)}) collective-permute-start(bf16[96,256]{1,0:T(8,128)(2,1)S(1)} %sum.1.refs_0_), channel_id=1, source_target_pairs={{0,12},{4,8},{8,4},{12,0},{16,28},{20,24},{24,20},{28,16},{1,13},{... | collective-permute-start | bytes 147464 | tf_op jit(solution)/shard_map/ppermute | solution.py:320
  87.3 4.1 %collective-permute-start.21 = (bf16[96,256]{1,0:T(8,128)(2,1)S(1)}, bf16[96,256]{1,0:T(8,128)(2,1)S(1)}, u32[]{:S(2)}, u32[]{:S(2)}) collective-permute-start(bf16[96,256]{1,0:T(8,128)(2,1)S(1)} %sum.1.refs_0_), channel_id=1, source_target_pairs={{0,8},{4,12},{8,0},{12,4},{16,24},{20,28},{24,16},{28,20},{1,9},{5... | collective-permute-start | bytes 147464 | tf_op jit(solution)/shard_map/ppermute | solution.py:320
  87.4 4.1 %collective-permute-start.20 = (bf16[96,256]{1,0:T(8,128)(2,1)S(1)}, bf16[96,256]{1,0:T(8,128)(2,1)S(1)}, u32[]{:S(2)}, u32[]{:S(2)}) collective-permute-start(bf16[96,256]{1,0:T(8,128)(2,1)S(1)} %sum.1.refs_0_), channel_id=1, source_target_pairs={{0,4},{4,0},{8,12},{12,8},{16,20},{20,16},{24,28},{28,24},{1,5},{5... | collective-permute-start | bytes 147464 | tf_op jit(solution)/shard_map/ppermute | solution.py:320

commit v2 on v1

v2 whole, which is shorter than its diff:
```python
import functools

import jax
import jax.numpy as jnp
from jax import lax
from jax.experimental import pallas as pl
from jax.experimental.pallas import tpu as pltpu
from jax.sharding import PartitionSpec as P

KB = 3
BLK = 64
HALO = 2
MB = 2
GRP = 4
SPAN = GRP + 2 * HALO
BF = jnp.bfloat16
F32 = jnp.float32
VM = pl.BlockSpec(memory_space=pltpu.VMEM)
ANY = pl.BlockSpec(memory_space=pl.ANY)
HB = pl.BlockSpec(memory_space=pltpu.HBM)


def gelu_slope(value):
    return (
        0.5 * (1.0 + lax.erf(value * 0.7071067811865476))
        + value * jnp.exp(-0.5 * value * value) * 0.3989422804014327
    )


def params(mib=24):
    return pltpu.CompilerParams(vmem_limit_bytes=mib << 20)


def matchings(n):
    near = [tuple(i ^ 1 for i in range(n)), tuple((i + 1 if i % 2 else i - 1) % n for i in range(n))]
    used = {(i, m[i]) for m in near for i in range(n)}

    def extend(found, now):
        if None not in now:
            found, now = found + [tuple(now)], [None] * n
        if len(found) == n - 3:
            return found
        i = now.index(None)
        for j in range(n - 1, i, -1):
            taken = any(m[i] == j for m in found)
            if now[j] is None and (i, j) not in used and not taken:
                after = list(now)
                after[i], after[j] = j, i
                result = extend(found, after)
                if result:
                    return result
        return None

    return near + extend([], [None] * n)


def partner_of(match, me):
    return sum((jnp.where(me == i, j, 0) for i, j in enumerate(match)), 0)


def near_pairs(lats, sections, side):
    pairs = []
    for i in range(lats):
        j = i ^ 1 if side == 0 else (i + 1 if i % 2 else i - 1)
        for s in range(sections):
            other = j * sections + s if 0 <= j < lats else i * sections + (s ^ 1)
            pairs.append((i * sections + s, other))
    return pairs


def hop_pairs(sections, turn):
    if turn % 2:
        return [(s, s ^ 1) for s in range(sections)]
    return [(s, (s - 1) % sections) for s in range(sections)]


def slant_pairs(lats, sections, turn, upward):
    last, low = lats - 1, turn - 1
    ways = {(i, turn): (i + 1, low) for i in range(last)}
    ways[last, turn] = (last - 1, turn)
    ways[last, low] = (last, turn)
    ways.update({(i, low): (i - 1, turn) for i in range(2, last)})
    ways[1, low] = (0, low)
    ways[0, low] = (0, turn)
    if not upward:
        ways = {(last - i, s): (last - j, r) for (i, s), (j, r) in ways.items()}
    for i in range(lats):
        for s in range(sections):
            ways.setdefault((i, s), (i, s ^ 1) if turn % 2 else (i ^ 1, s))
    pairs = [(i * sections + s, j * sections + r) for (i, s), (j, r) in ways.items()]
    assert len({b for _, b in pairs}) == lats * sections
    return pairs


def dot(a, b):
    return jnp.dot(a, b, preferred_element_type=F32)


def band_kernel(
    blocks, index_in, mask_in, quad_in, band_ref, flip_ref, index_ref, mask_ref, quad_ref, table_ref, sems
):
    first = lax.axis_index("lat") * blocks
    small = [
        pltpu.make_async_copy(index_in, index_ref, sems.at[KB]),
        pltpu.make_async_copy(mask_in, mask_ref, sems.at[KB + 1]),
    ]
    large = [pltpu.make_async_copy(quad_in.at[k], quad_ref.at[k], sems.at[k]) for k in range(KB)]
    for c in small + large:
        c.start()
    for c in small:
        c.wait()
    for b in range(blocks):
        for d in range(2 * HALO + 2):
            table_ref[b, d] = 0
        for j in range(index_ref.shape[1]):
            d = index_ref[b, j] - (first + b) + HALO
            table_ref[b, jnp.where(mask_ref[b, j] != 0, d, 2 * HALO + 1)] = j + 1
    empty = jnp.zeros((BLK, BLK), BF)
    for k in range(KB):
        large[k].wait()
        for b in range(blocks):
            g, r = b // GRP, b % GRP
            tiles = [empty] * r
            for d in range(2 * HALO + 1):
                entry = table_ref[b, d]
                tile = quad_ref[k, b, jnp.maximum(entry - 1, 0)]
                tiles.append(jnp.where(entry > 0, tile, empty))
            tiles += [empty] * (GRP - 1 - r)
            row = k * GRP * BLK + r * BLK
            band_ref[g, row : row + BLK, :] = jnp.concatenate(tiles, axis=1)
            if r == GRP - 1:
                part = slice(k * GRP * BLK, (k + 1) * GRP * BLK)
                flip_ref[g, :, part] = band_ref[g, part, :].T


def band_call(block_index, block_mask, quad):
    blocks = quad.shape[1]
    groups = blocks // GRP
    return pl.pallas_call(
        functools.partial(band_kernel, blocks),
        out_shape=(
            pltpu.VMEM((groups, KB * GRP * BLK, SPAN * BLK), BF),
            pltpu.VMEM((groups, SPAN * BLK, KB * GRP * BLK), BF),
        ),
        in_specs=[HB] * 3,
        out_specs=(VM, VM),
        scratch_shapes=[
            pltpu.SMEM(block_index.shape, jnp.int32),
            pltpu.SMEM(block_mask.shape, jnp.int32),
            pltpu.VMEM(quad.shape, BF),
            pltpu.SMEM((blocks, 2 * HALO + 2), jnp.int32),
            pltpu.SemaphoreType.DMA((KB + 2,)),
        ],
        compiler_params=params(),
        name="band",
    )(block_index, block_mask, quad)


def hidden_kernel(x_ref, near_ref, far_ref, band_ref, w_ref, hid_ref, gp_ref, ext_ref, sems):
    rows = x_ref.shape[2]
    edge = HALO * BLK
    odd = lax.axis_index("lat") % 2
    ends = [pl.multiple_of(side * (edge + rows), edge) for side in (1 - odd, odd)]
    copies = [
        pltpu.make_async_copy(near_ref, ext_ref.at[:, pl.ds(ends[0], edge)], sems.at[0]),
        pltpu.make_async_copy(x_ref.at[0], ext_ref.at[:, pl.ds(edge, rows)], sems.at[1]),
        pltpu.make_async_copy(far_ref, ext_ref.at[:, pl.ds(ends[1], edge)], sems.at[2]),
    ]
    for c in copies:
        c.start()
    for c in copies:
        c.wait()
    size = GRP * BLK
    for m in range(MB):
        for g in range(rows // size):
            window = ext_ref[m, g * size : g * size + SPAN * BLK, :]
            hid = dot(band_ref[g], window).astype(BF)
            hid_ref[m, g] = hid
            z = dot(hid[:size], w_ref[0, 0])
            for k in range(1, KB):
                z += dot(hid[k * size : (k + 1) * size], w_ref[0, k])
            gp_ref[m, g * size : (g + 1) * size, :] = gelu_slope(z)


def hidden_call(x, near, far, band, weights):
    _, mb, rows, ch = x.shape
    groups = band.shape[0]
    return pl.pallas_call(
        hidden_kernel,
        out_shape=(
            pltpu.VMEM((mb, groups, KB * GRP * BLK, ch), BF),
            pltpu.VMEM((mb, rows, ch), F32),
        ),
        in_specs=[ANY, ANY, ANY, VM, VM],
        out_specs=(VM, VM),
        scratch_shapes=[
            pltpu.VMEM((mb, rows + 2 * HALO * BLK, ch), BF),
            pltpu.SemaphoreType.DMA((3,)),
        ],
        compiler_params=params(),
        name="hidden",
    )(x, near, far, band, weights)


def step_kernel(turn, lats, *refs):
    first = lats is None
    (main_ref, gp_ref, flip_ref, w_ref), rest = refs[:4], refs[4:]
    if not first:
        (below_ref, above_ref), rest = rest[:2], rest[6:]
    lat = lax.axis_index("lat")
    out_ref, left_ref, right_ref, slope_ref, stack_ref, term_ref = rest
    rows = gp_ref.shape[1]
    size = GRP * BLK
    edge = HALO * BLK
    groups = rows // size

    @pl.when(lax.axis_index("section") == turn)
    def _():
        for m in range(MB):
            for g in range(groups):
                at = pl.ds(g * size, size)
                grad = main_ref[m, at, :].astype(F32)
                if not first:
                    parts = [grad[i * edge : (i + 1) * edge] for i in range(size // edge)]
                    if g == 0:
                        parts[0] += jnp.where(lat > 0, below_ref[m].astype(F32), 0.0)
                    if g == groups - 1:
                        parts[-1] += jnp.where(lat < lats - 1, above_ref[m].astype(F32), 0.0)
                    grad = jnp.concatenate(parts, axis=0).astype(BF).astype(F32)
                slope = (grad * gp_ref[m, at, :]).astype(BF)
                slope_ref[m, at, :] = slope
                for k in range(KB):
                    back = lax.dot_general(
                        slope, w_ref[0, k], (((1,), (1,)), ((), ())), preferred_element_type=F32
                    )
                    stack_ref[k * size : (k + 1) * size, :] = back.astype(BF)
                term = dot(flip_ref[g], stack_ref[...])
                lap = 2 * edge
                low = g * size
                if g == 0:
                    left_ref[m] = term[:edge].astype(BF)
                    term_ref[low + edge : low + lap, :] = term[edge:lap] + grad[: lap - edge]
                else:
                    term_ref[low : low + lap, :] += term[:lap]
                    term_ref[low + edge : low + lap, :] += grad[: lap - edge]
                term_ref[low + lap : low + size + edge, :] = (
                    term[lap : size + edge] + grad[lap - edge :]
                )
                if g == groups - 1:
                    right_ref[m] = term[size + edge :].astype(BF)
                else:
                    term_ref[low + size + edge : low + size + lap, :] = term[size + edge :]
            out_ref[m] = term_ref[edge : edge + rows, :].astype(BF)


def step_call(turn, lats, main, sides, gp, flip, weights, olds):
    mb, rows, ch = gp.shape
    edge = HALO * BLK
    shapes = ((mb, rows, ch), (mb, edge, ch), (mb, edge, ch), (mb, rows, ch))
    args = (main, gp, flip, weights) + sides + olds
    aliases = {6 + i: i for i in range(len(olds))}
    return pl.pallas_call(
        functools.partial(step_kernel, turn, lats if olds else None),
        out_shape=tuple(pltpu.VMEM(s, BF) for s in shapes),
        in_specs=[VM] * len(args),
        out_specs=(VM,) * 4,
        input_output_aliases=aliases,
        scratch_shapes=[
            pltpu.VMEM((KB * GRP * BLK, ch), BF),
            pltpu.VMEM((rows + 2 * edge, ch), F32),
        ],
        compiler_params=params(),
        name=f"step{turn}",
    )(*args)


def weight_kernel(ways, hid_ref, slope_ref, left_ref, right_ref, *refs):
    out_refs, acc_ref = refs[:-1], refs[-1]
    n = len(ways) + 1
    me = lax.axis_index("lat")
    size = GRP * BLK
    groups = hid_ref.shape[1]
    for k in range(KB):
        total = None
        for m in range(MB):
            for g in range(groups):
                part = lax.dot_general(
                    hid_ref[m, g, k * size : (k + 1) * size, :],
                    slope_ref[m, g * size : (g + 1) * size, :],
                    (((0,), (0,)), ((), ())),
                    preferred_element_type=F32,
                )
                total = part if total is None else total + part
        acc_ref[k * total.shape[0] : (k + 1) * total.shape[0], :] = total
    piece = acc_ref.shape[0] // n

    def cut(i):
        return acc_ref[pl.ds(pl.multiple_of(i * piece, piece), piece), :]

    if n == 1:
        out_refs[0][...] = acc_ref[...]
        return
    out_refs[0][...] = cut(me)
    odd = me % 2 == 1
    edge = left_ref.shape[1]
    for s, way in enumerate(ways):
        out_refs[s + 1][:piece, :] = cut(partner_of(way, me)).astype(BF)
        if s < 2:
            for m in range(MB):
                rows = slice(piece + m * edge, piece + (m + 1) * edge)
                low, high = (right_ref, left_ref) if s == 0 else (left_ref, right_ref)
                out_refs[s + 1][rows, :] = jnp.where(odd, high[m], low[m])


def weight_call(ways, hid, slope, left, right):
    ch = slope.shape[2]
    piece = KB * ch // (len(ways) + 1)
    extra = MB * left.shape[1]
    return pl.pallas_call(
        functools.partial(weight_kernel, ways),
        out_shape=(pltpu.VMEM((piece, ch), F32),)
        + tuple(pltpu.VMEM((piece + (extra if s < 2 else 0), ch), BF) for s in range(len(ways))),
        in_specs=[VM] * 4,
        out_specs=(VM,) * (len(ways) + 1),
        scratch_shapes=[pltpu.VMEM((KB * ch, ch), F32)],
        compiler_params=params(),
        name="weight",
    )(hid, slope, left, right)


def sum_kernel(own_ref, *refs):
    piece = own_ref.shape[0]
    total = own_ref[...]
    for ref in refs[:-1]:
        total += ref[:piece, :].astype(F32)
    refs[-1][...] = total.astype(BF)


def sum_call(own, others):
    return pl.pallas_call(
        sum_kernel,
        out_shape=pltpu.VMEM(own.shape, BF),
        in_specs=[VM] * (1 + len(others)),
        out_specs=VM,
        compiler_params=params(),
        name="sum",
    )(own, *others)


def grad_kernel(lats, skip, main_ref, near_ref, far_ref, grad_ref):
    rows = main_ref.shape[1]
    edge = HALO * BLK
    me = lax.axis_index("lat")
    odd = me % 2 == 1
    for m in range(MB):
        at = slice(skip + m * edge, skip + (m + 1) * edge)
        near, far = near_ref[at, :].astype(F32), far_ref[at, :].astype(F32)
        below = jnp.where(me > 0, jnp.where(odd, near, far), 0.0)
        above = jnp.where(me < lats - 1, jnp.where(odd, far, near), 0.0)
        grad_ref[0, m, :edge, :] = (main_ref[m, :edge, :].astype(F32) + below).astype(BF)
        grad_ref[0, m, edge : rows - edge, :] = main_ref[m, edge : rows - edge, :]
        grad_ref[0, m, rows - edge :, :] = (main_ref[m, rows - edge :, :].astype(F32) + above).astype(BF)


def grad_call(lats, skip, main, near, far):
    return pl.pallas_call(
        functools.partial(grad_kernel, lats, skip),
        out_shape=jax.ShapeDtypeStruct((1,) + main.shape, BF),
        in_specs=[VM] * 3,
        out_specs=VM,
        compiler_params=params(),
        name="grad",
    )(main, near, far)


def join_kernel(ways, *refs):
    pieces, weight_ref = refs[:-1], refs[-1]
    me = lax.axis_index("lat")
    piece = pieces[0].shape[0]
    for ref, other in zip(pieces, [me] + [partner_of(way, me) for way in ways]):
        weight_ref[pl.ds(pl.multiple_of(other * piece, piece), piece), :] = ref[...].astype(F32)


def join_call(ways, pieces):
    piece, ch = pieces[0].shape
    return pl.pallas_call(
        functools.partial(join_kernel, ways),
        out_shape=jax.ShapeDtypeStruct((piece * len(pieces), ch), F32),
        in_specs=[VM] * len(pieces),
        out_specs=VM,
        compiler_params=params(),
        name="join",
    )(*pieces)


def per_device(saved_input, cotangent, quad_values, block_index, block_mask, weights):
    sections = lax.axis_size("section")
    lats = lax.axis_size("lat")
    edge = HALO * BLK
    rows = saved_input.shape[2]
    both = ("lat", "section")
    odd = lax.axis_index("lat") % 2
    sides = [near_pairs(lats, sections, side) for side in range(2)]

    def rim(high):
        return lax.dynamic_slice_in_dim(saved_input[0], high * (rows - edge), edge, axis=1)

    far = lax.ppermute(rim(odd), both, sides[1])
    near = lax.ppermute(rim(1 - odd), both, sides[0])
    band, flip = band_call(block_index, block_mask, quad_values)
    hid, gp = hidden_call(saved_input, near, far, band, weights)

    state, main, terms = (), cotangent, ()
    for turn in reversed(range(sections)):
        state = step_call(turn, lats, main, terms, gp, flip, weights, state)
        out, left, right, slope = state
        if turn > 0:
            low = lax.ppermute(right, both, slant_pairs(lats, sections, turn, True))
            high = lax.ppermute(left, both, slant_pairs(lats, sections, turn, False))
            main = lax.ppermute(out, "section", hop_pairs(sections, turn))
            terms = (low, high)

    channels = saved_input.shape[3]
    if lats == 8:
        ways = matchings(lats)
        own, *cuts = weight_call(ways, hid, slope, left, right)
        met = [lax.ppermute(cut, "lat", list(enumerate(way))) for cut, way in zip(cuts, ways)]
        mine = sum_call(own, met)
        grad = grad_call(lats, own.shape[0], out, met[0], met[1])
        pieces = [mine] + [lax.ppermute(mine, "lat", list(enumerate(way))) for way in ways]
        weight = join_call(ways, pieces)
    else:
        give = jnp.where(odd == 1, left, right), jnp.where(odd == 1, right, left)
        near, far = (lax.ppermute(g, both, p).reshape(-1, channels) for g, p in zip(give, sides))
        grad = grad_call(lats, 0, out, near, far)
        weight = lax.psum(weight_call([], hid, slope, left, right)[0], "lat")
    return grad, weight.reshape(1, KB, channels, channels)


def solution(mesh):
    in_specs = (
        P("section", None, "lat", None),
        P(None, "lat", None),
        P(None, "lat", None, None, None),
        P("lat", None),
        P("lat", None),
        P("section", None, None, None),
    )
    out_specs = (P("section", None, "lat", None), P("section", None, None, None))
    return jax.shard_map(
        per_device, mesh=mesh, in_specs=in_specs, out_specs=out_specs, check_vma=False
    )
```

time: 93 us -> 86.4 us (0.929)
  waiting for transfers between devices: 39.5 us -> 25.5 us
  starting transfers between devices: 40 us -> 46.8 us
  Pallas kernels: 8.19 us -> 9.18 us
    ppermute x27 -> x25, waiting for transfers between devices: 39.5 us -> 25.5 us  [the longest x3 8.25 us: per_device(): low = lax.ppermute(right, both, slant_pairs(lats, sections, turn, True))]
    ppermute x27 -> x25, starting transfers between devices: 40 us -> 46.8 us  [the longest x7 13.1 us: per_device(): lax.ppermute(cut, 'lat', list(enumerate(way)))]
    squeeze x1 -> x0, local copies, waits for them, and re-layouts: 1.04 us -> none  [per_device(): above = lax.ppermute(saved_input[0, :, :edge], 'lat', down)]
    dynamic_slice x0 -> x1, local copies, waits for them, and re-layouts: none -> 1.04 us  [rim(): lax.dynamic_slice_in_dim(saved_input[0], high * (rows - edge), edge, axis=1)]
    pallas_call x6 -> x7, Pallas kernels: 3.76 us -> 4.45 us  [the longest x4 1.93 us: step_call(): pl.pallas_call(functools.partial(step_kernel, turn, lats if olds else Non...]
  transfers between devices with their start and end apart: 27 -> 25, of which waited for: 8 -> 15; matrix products, arithmetic and copies ran while one was open for 0% -> 0% of each run, Pallas kernels for 2% -> 3%
where the time goes in v2:
time: 86.4 us; the launch traced here: 86.2 us
  starting transfers between devices  46.8 us (54%)
  waiting for transfers between devices  25.5 us (30%)
  Pallas kernels  9.18 us (11%)
  local copies, waits for them, and re-layouts  3.97 us (5%)
    ppermute x7, starting transfers between devices, per_device(): lax.ppermute(cut, 'lat', list(enumerate(way)))  13.1 us
    ppermute x7, starting transfers between devices, per_device(): lax.ppermute(mine, 'lat', list(enumerate(way)))  12.4 us
    ppermute x3, starting transfers between devices, per_device(): main = lax.ppermute(out, 'section', hop_pairs(sections, turn))  10.9 us
    ppermute x3, waiting for transfers between devices, per_device(): low = lax.ppermute(right, both, slant_pairs(lats, sections, turn, True))  8.25 us
    ppermute x7, waiting for transfers between devices, per_device(): lax.ppermute(cut, 'lat', list(enumerate(way)))  6.72 us
    ppermute x3, waiting for transfers between devices, per_device(): high = lax.ppermute(left, both, slant_pairs(lats, sections, turn, False))  4.74 us
    ppermute x1, starting transfers between devices, per_device(): near = lax.ppermute(rim(1 - odd), both, sides[0])  4.02 us
    ppermute x7, waiting for transfers between devices, per_device(): lax.ppermute(mine, 'lat', list(enumerate(way)))  3.69 us
  transfers between devices with their start and end apart: 25, of which 15 were waited for; matrix products, arithmetic and copies ran while one was open for 0% of the time, Pallas kernels for 3%

profile of v2, /device:TPU:0, one launch (start us, length us, event | category | flops | bytes accessed | tf_op | source)
XLA Modules:
  0.0 86.2 jit_solution(7251265487712481189)
XLA Ops:
  0.6 0.0 copy-start
  0.7 1.0 %dynamic-slice_bitcast_fusion = (bf16[2,128,256]{2,1,0:T(8,128)(2,1)S(1)}, bf16[2,128,256]{2,1,0:T(8,128)(2,1)S(1)}) fusion(bf16[1,2,512,256]{3,2,1,0:T(8,128)(2,1)} %x_ref.1, s32[]{:T(128)S(6)} %select_n.15, s32[]{:T(128)S(6)} %select_n.14), kind=kLoop, calls=%fused_computation | loop fusion | bytes 524296 | tf_op jit(solution)/shard_map/dynamic_slice | solution.py:406
  1.7 0.6 collective-permute-start.1
  2.3 4.0 %collective-permute-start = (bf16[2,128,256]{2,1,0:T(8,128)(2,1)S(1)}, bf16[2,128,256]{2,1,0:T(8,128)(2,1)S(1)}, u32[]{:S(2)}, u32[]{:S(2)}) collective-permute-start(bf16[2,128,256]{2,1,0:T(8,128)(2,1)S(1)} %get-tuple-element.59), channel_id=1, source_target_pairs={{0,4},{1,5},{2,6},{3,7},{4,0},{5,1},{6,2},{7,3},{8,12},{9,13},{10,... | collective-permute-start | bytes 393224 | tf_op jit(solution)/shard_map/ppermute | solution.py:409
  6.3 1.5 %copy-done.1 = bf16[3,8,5,64,64]{4,3,2,1,0:T(8,128)(2,1)S(1)} copy-done((bf16[3,8,5,64,64]{4,3,2,1,0:T(8,128)(2,1)S(1)}, bf16[3,8,5,64,64]{4,3,2,1,0:T(8,128)(2,1)}, u32[]{:S(2)}) %copy-start.1) | copy-done | bytes 983064
  7.8 0.7 copy-done.4
  8.5 0.7 copy-done.5
  9.2 1.9 %band.1 = (bf16[2,768,512]{2,1,0:T(8,128)(2,1)S(1)}, bf16[2,512,768]{2,1,0:T(8,128)(2,1)S(1)}) custom-call(s32[8,5]{1,0:T(8,128)S(1)} %copy-done.4, s32[8,5]{1,0:T(8,128)S(1)} %copy-done.5, bf16[3,8,5,64,64]{4,3,2,1,0:T(8,128)(2,1)S(1)} %copy-done.1), custom_call_target="tpu_custom_call" | custom-call | tf_op jit(solution)/shard_map/band/pallas_call | solution.py:139
  11.1 0.0 copy-start.3
  11.1 0.0 collective-permute-done.1.far_ref
  11.1 0.1 collective-permute-done.near_ref
  11.2 0.0 copy-done
  11.2 2.8 %hidden.1 = (bf16[2,2,768,256]{3,2,1,0:T(8,128)(2,1)S(1)}, f32[2,512,256]{2,1,0:T(8,128)S(1)}) custom-call(bf16[1,2,512,256]{3,2,1,0:T(8,128)(2,1)S(1)} %copy-done.2, bf16[2,128,256]{2,1,0:T(8,128)(2,1)S(1)} %collective-permute-done.near_ref, bf16[2,128,256]{2,1,0:T(8,128)(2,1)S(1)} %collective-permute-done.1.far_ref, ...), custom_call_target="tpu_custom_call" | custom-call | tf_op jit(solution)/shard_map/hidden/pallas_call | solution.py:188
  14.0 0.1 collective-permute-start.2
  14.1 0.5 collective-permute-start.3
  14.6 0.1 collective-permute-start.4
  14.7 1.5 %collective-permute-done.3.refs_4_ = bf16[2,128,256]{2,1,0:T(8,128)(2,1)S(1)} collective-permute-done((bf16[2,128,256]{2,1,0:T(8,128)(2,1)S(1)}, bf16[2,128,256]{2,1,0:T(8,128)(2,1)S(1)}, u32[]{:S(2)}, u32[]{:S(2)}) %collective-permute-start.3) | collective-permute-done | bytes 131104 | tf_op jit(solution)/shard_map/ppermute | solution.py:418
  16.2 0.2 collective-permute-done.4.refs_5_
  16.4 0.0 collective-permute-done.2.refs_0_
  16.4 9.5 %collective-permute-start.5 = (bf16[2,512,256]{2,1,0:T(8,128)(2,1)S(1)}, bf16[2,512,256]{2,1,0:T(8,128)(2,1)S(1)}, u32[]{:S(2)}, u32[]{:S(2)}) collective-permute-start(bf16[2,512,256]{2,1,0:T(8,128)(2,1)S(1)} %get-tuple-element.37.refs_6_), channel_id=1, source_target_pairs={{0,3},{1,0},{2,1},{3,2},{4,7},{5,4},{6,5},{7,6},{8,11},{9,8},{10,9... | collective-permute-start | bytes 1572872 | tf_op jit(solution)/shard_map/ppermute | solution.py:420
  25.9 2.2 %collective-permute-start.6 = (bf16[2,128,256]{2,1,0:T(8,128)(2,1)S(1)}, bf16[2,128,256]{2,1,0:T(8,128)(2,1)S(1)}, u32[]{:S(2)}, u32[]{:S(2)}) collective-permute-start(bf16[2,128,256]{2,1,0:T(8,128)(2,1)S(1)} %get-tuple-element.38.refs_8_), channel_id=1, source_target_pairs={{2,5},{6,9},{10,13},{14,17},{18,21},{22,25},{26,29},{30,26},{29,30... | collective-permute-start | bytes 393224 | tf_op jit(solution)/shard_map/ppermute | solution.py:418
  28.1 0.0 collective-permute-start.7
  28.1 3.9 %collective-permute-done.6.refs_4_ = bf16[2,128,256]{2,1,0:T(8,128)(2,1)S(1)} collective-permute-done((bf16[2,128,256]{2,1,0:T(8,128)(2,1)S(1)}, bf16[2,128,256]{2,1,0:T(8,128)(2,1)S(1)}, u32[]{:S(2)}, u32[]{:S(2)}) %collective-permute-start.6) | collective-permute-done | bytes 131104 | tf_op jit(solution)/shard_map/ppermute | solution.py:418
  32.0 1.4 %collective-permute-done.7.refs_5_ = bf16[2,128,256]{2,1,0:T(8,128)(2,1)S(1)} collective-permute-done((bf16[2,128,256]{2,1,0:T(8,128)(2,1)S(1)}, bf16[2,128,256]{2,1,0:T(8,128)(2,1)S(1)}, u32[]{:S(2)}, u32[]{:S(2)}) %collective-permute-start.7) | collective-permute-done | bytes 131104 | tf_op jit(solution)/shard_map/ppermute | solution.py:419
  33.4 2.0 %collective-permute-done.5.refs_0_ = bf16[2,512,256]{2,1,0:T(8,128)(2,1)S(1)} collective-permute-done((bf16[2,512,256]{2,1,0:T(8,128)(2,1)S(1)}, bf16[2,512,256]{2,1,0:T(8,128)(2,1)S(1)}, u32[]{:S(2)}, u32[]{:S(2)}) %collective-permute-start.5) | collective-permute-done | bytes 524320 | tf_op jit(solution)/shard_map/ppermute | solution.py:420
  35.3 1.4 %collective-permute-start.8 = (bf16[2,512,256]{2,1,0:T(8,128)(2,1)S(1)}, bf16[2,512,256]{2,1,0:T(8,128)(2,1)S(1)}, u32[]{:S(2)}, u32[]{:S(2)}) collective-permute-start(bf16[2,512,256]{2,1,0:T(8,128)(2,1)S(1)} %get-tuple-element.41.refs_6_), channel_id=1, source_target_pairs={{0,1},{1,0},{2,3},{3,2},{4,5},{5,4},{6,7},{7,6},{8,9},{9,8},{10,11... | collective-permute-start | bytes 1572872 | tf_op jit(solution)/shard_map/ppermute | solution.py:420
  36.7 0.1 collective-permute-start.9
  36.8 3.0 %collective-permute-start.10 = (bf16[2,128,256]{2,1,0:T(8,128)(2,1)S(1)}, bf16[2,128,256]{2,1,0:T(8,128)(2,1)S(1)}, u32[]{:S(2)}, u32[]{:S(2)}) collective-permute-start(bf16[2,128,256]{2,1,0:T(8,128)(2,1)S(1)} %get-tuple-element.43.refs_7_), channel_id=1, source_target_pairs={{29,24},{25,20},{21,16},{17,12},{13,8},{9,4},{5,0},{1,5},{0,1},{20... | collective-permute-start | bytes 393224 | tf_op jit(solution)/shard_map/ppermute | solution.py:419
  39.8 2.8 %collective-permute-done.9.refs_4_ = bf16[2,128,256]{2,1,0:T(8,128)(2,1)S(1)} collective-permute-done((bf16[2,128,256]{2,1,0:T(8,128)(2,1)S(1)}, bf16[2,128,256]{2,1,0:T(8,128)(2,1)S(1)}, u32[]{:S(2)}, u32[]{:S(2)}) %collective-permute-start.9) | collective-permute-done | bytes 131104 | tf_op jit(solution)/shard_map/ppermute | solution.py:418
  42.6 3.2 %collective-permute-done.10.refs_5_ = bf16[2,128,256]{2,1,0:T(8,128)(2,1)S(1)} collective-permute-done((bf16[2,128,256]{2,1,0:T(8,128)(2,1)S(1)}, bf16[2,128,256]{2,1,0:T(8,128)(2,1)S(1)}, u32[]{:S(2)}, u32[]{:S(2)}) %collective-permute-start.10) | collective-permute-done | bytes 131104 | tf_op jit(solution)/shard_map/ppermute | solution.py:419
  45.8 0.0 collective-permute-done.8.refs_0_
  45.8 1.9 %step0.1 = (bf16[2,512,256]{2,1,0:T(8,128)(2,1)S(1)}, bf16[2,128,256]{2,1,0:T(8,128)(2,1)S(1)}, bf16[2,128,256]{2,1,0:T(8,128)(2,1)S(1)}, bf16[2,512,256]{2,1,0:T(8,128)(2,1)S(1)}) custom-call(bf16[2,512,256]{2,1,0:T(8,128)(2,1)S(1)} %collective-permute-done.8.refs_0_, ...), custom_call_target="tpu_custom_call", output_to_operand_aliasing={{0}: (6, {}), {1}: (7, {}), {2}: (8, {}), {3}: (9, {})} | custom-call | tf_op jit(solution)/shard_map/step0/pallas_call | solution.py:262
  47.7 0.7 weight.1
  48.4 2.1 %collective-permute-start.11 = (bf16[352,256]{1,0:T(8,128)(2,1)S(1)}, bf16[352,256]{1,0:T(8,128)(2,1)S(1)}, u32[]{:S(2)}, u32[]{:S(2)}) collective-permute-start(bf16[352,256]{1,0:T(8,128)(2,1)S(1)} %get-tuple-element.50), channel_id=1, source_target_pairs={{0,4},{4,0},{8,12},{12,8},{16,20},{20,16},{24,28},{28,24},{1,5},{5... | collective-permute-start | bytes 540680 | tf_op jit(solution)/shard_map/ppermute | solution.py:427
  50.5 6.0 %collective-permute-start.12 = (bf16[352,256]{1,0:T(8,128)(2,1)S(1)}, bf16[352,256]{1,0:T(8,128)(2,1)S(1)}, u32[]{:S(2)}, u32[]{:S(2)}) collective-permute-start(bf16[352,256]{1,0:T(8,128)(2,1)S(1)} %get-tuple-element.51), channel_id=1, source_target_pairs={{0,28},{4,8},{8,4},{12,16},{16,12},{20,24},{24,20},{28,0},{1,29},{... | collective-permute-start | bytes 540680 | tf_op jit(solution)/shard_map/ppermute | solution.py:427
  56.5 1.0 %collective-permute-start.13 = (bf16[96,256]{1,0:T(8,128)(2,1)S(1)}, bf16[96,256]{1,0:T(8,128)(2,1)S(1)}, u32[]{:S(2)}, u32[]{:S(2)}) collective-permute-start(bf16[96,256]{1,0:T(8,128)(2,1)S(1)} %get-tuple-element.53), channel_id=1, source_target_pairs={{0,24},{4,28},{8,16},{12,20},{16,8},{20,12},{24,0},{28,4},{1,25},{... | collective-permute-start | bytes 147464 | tf_op jit(solution)/shard_map/ppermute | solution.py:427
  57.6 0.1 collective-permute-start.14
  57.7 1.8 %collective-permute-start.15 = (bf16[96,256]{1,0:T(8,128)(2,1)S(1)}, bf16[96,256]{1,0:T(8,128)(2,1)S(1)}, u32[]{:S(2)}, u32[]{:S(2)}) collective-permute-start(bf16[96,256]{1,0:T(8,128)(2,1)S(1)} %get-tuple-element.55), channel_id=1, source_target_pairs={{0,16},{4,24},{8,20},{12,28},{16,0},{20,8},{24,4},{28,12},{1,17},{... | collective-permute-start | bytes 147464 | tf_op jit(solution)/shard_map/ppermute | solution.py:427
  59.5 3.0 %collective-permute-done.13.refs_2_ = bf16[96,256]{1,0:T(8,128)(2,1)S(1)} collective-permute-done((bf16[96,256]{1,0:T(8,128)(2,1)S(1)}, bf16[96,256]{1,0:T(8,128)(2,1)S(1)}, u32[]{:S(2)}, u32[]{:S(2)}) %collective-permute-start.13) | collective-permute-done | bytes 49184 | tf_op jit(solution)/shard_map/ppermute | solution.py:427
  62.4 1.0 %collective-permute-start.16 = (bf16[96,256]{1,0:T(8,128)(2,1)S(1)}, bf16[96,256]{1,0:T(8,128)(2,1)S(1)}, u32[]{:S(2)}, u32[]{:S(2)}) collective-permute-start(bf16[96,256]{1,0:T(8,128)(2,1)S(1)} %get-tuple-element.56), channel_id=1, source_target_pairs={{0,12},{4,20},{8,24},{12,0},{16,28},{20,4},{24,8},{28,16},{1,13},{... | collective-permute-start | bytes 147464 | tf_op jit(solution)/shard_map/ppermute | solution.py:427
  63.4 0.7 collective-permute-done.14.refs_3_
  64.1 1.0 %collective-permute-start.17 = (bf16[96,256]{1,0:T(8,128)(2,1)S(1)}, bf16[96,256]{1,0:T(8,128)(2,1)S(1)}, u32[]{:S(2)}, u32[]{:S(2)}) collective-permute-start(bf16[96,256]{1,0:T(8,128)(2,1)S(1)} %get-tuple-element.57), channel_id=1, source_target_pairs={{0,8},{4,12},{8,0},{12,4},{16,24},{20,28},{24,16},{28,20},{1,9},{5... | collective-permute-start | bytes 147464 | tf_op jit(solution)/shard_map/ppermute | solution.py:427
  65.1 0.2 collective-permute-done.15.refs_4_
  65.3 2.6 %collective-permute-done.16.refs_5_ = bf16[96,256]{1,0:T(8,128)(2,1)S(1)} collective-permute-done((bf16[96,256]{1,0:T(8,128)(2,1)S(1)}, bf16[96,256]{1,0:T(8,128)(2,1)S(1)}, u32[]{:S(2)}, u32[]{:S(2)}) %collective-permute-start.16) | collective-permute-done | bytes 49184 | tf_op jit(solution)/shard_map/ppermute | solution.py:427
  68.0 0.2 collective-permute-done.17.refs_6_
  68.2 0.0 collective-permute-done.11.near_ref.refs_0_
  68.2 0.0 collective-permute-done.12.far_ref.refs_1_
  68.2 0.1 sum.1.refs_0_
  68.2 1.7 %collective-permute-start.24 = (bf16[96,256]{1,0:T(8,128)(2,1)S(1)}, bf16[96,256]{1,0:T(8,128)(2,1)S(1)}, u32[]{:S(2)}, u32[]{:S(2)}) collective-permute-start(bf16[96,256]{1,0:T(8,128)(2,1)S(1)} %sum.1.refs_0_), channel_id=1, source_target_pairs={{0,8},{4,12},{8,0},{12,4},{16,24},{20,28},{24,16},{28,20},{1,9},{5... | collective-permute-start | bytes 147464 | tf_op jit(solution)/shard_map/ppermute | solution.py:430
  70.0 3.0 %collective-permute-start.23 = (bf16[96,256]{1,0:T(8,128)(2,1)S(1)}, bf16[96,256]{1,0:T(8,128)(2,1)S(1)}, u32[]{:S(2)}, u32[]{:S(2)}) collective-permute-start(bf16[96,256]{1,0:T(8,128)(2,1)S(1)} %sum.1.refs_0_), channel_id=1, source_target_pairs={{0,12},{4,20},{8,24},{12,0},{16,28},{20,4},{24,8},{28,16},{1,13},{... | collective-permute-start | bytes 147464 | tf_op jit(solution)/shard_map/ppermute | solution.py:430
  73.0 0.0 collective-permute-start.22
  73.0 2.2 %collective-permute-start.21 = (bf16[96,256]{1,0:T(8,128)(2,1)S(1)}, bf16[96,256]{1,0:T(8,128)(2,1)S(1)}, u32[]{:S(2)}, u32[]{:S(2)}) collective-permute-start(bf16[96,256]{1,0:T(8,128)(2,1)S(1)} %sum.1.refs_0_), channel_id=1, source_target_pairs={{0,20},{4,16},{8,28},{12,24},{16,4},{20,0},{24,12},{28,8},{1,21},{... | collective-permute-start | bytes 147464 | tf_op jit(solution)/shard_map/ppermute | solution.py:430
  75.2 2.8 %collective-permute-start.20 = (bf16[96,256]{1,0:T(8,128)(2,1)S(1)}, bf16[96,256]{1,0:T(8,128)(2,1)S(1)}, u32[]{:S(2)}, u32[]{:S(2)}) collective-permute-start(bf16[96,256]{1,0:T(8,128)(2,1)S(1)} %sum.1.refs_0_), channel_id=1, source_target_pairs={{0,24},{4,28},{8,16},{12,20},{16,8},{20,12},{24,0},{28,4},{1,25},{... | collective-permute-start | bytes 147464 | tf_op jit(solution)/shard_map/ppermute | solution.py:430
  78.0 0.0 collective-permute-done.24.refs_7_
  78.0 2.6 %collective-permute-start.19 = (bf16[96,256]{1,0:T(8,128)(2,1)S(1)}, bf16[96,256]{1,0:T(8,128)(2,1)S(1)}, u32[]{:S(2)}, u32[]{:S(2)}) collective-permute-start(bf16[96,256]{1,0:T(8,128)(2,1)S(1)} %sum.1.refs_0_), channel_id=1, source_target_pairs={{0,28},{4,8},{8,4},{12,16},{16,12},{20,24},{24,20},{28,0},{1,29},{... | collective-permute-start | bytes 147464 | tf_op jit(solution)/shard_map/ppermute | solution.py:430
  80.6 0.0 collective-permute-done.23.refs_6_
  80.6 0.0 collective-permute-start.18
  80.6 0.9 %grad.1 = bf16[1,2,512,256]{3,2,1,0:T(8,128)(2,1)} custom-call(bf16[2,512,256]{2,1,0:T(8,128)(2,1)S(1)} %get-tuple-element.45.main_ref, bf16[352,256]{1,0:T(8,128)(2,1)S(1)} %collective-permute-done.11.near_ref.refs_0_, bf16[352,256]{1,0:T(8,128)(2,1)S(1)} %collective-permute-done.12.far_ref.refs_1_), custom_call_target="tpu_custom_call" | custom-call | tf_op jit(solution)/shard_map/grad/pallas_call | solution.py:366
  81.5 0.0 collective-permute-done.22.refs_5_
  81.5 0.0 collective-permute-done.21.refs_4_
  81.6 0.0 collective-permute-done.20.refs_3_
  81.6 3.3 %collective-permute-done.19.refs_2_ = bf16[96,256]{1,0:T(8,128)(2,1)S(1)} collective-permute-done((bf16[96,256]{1,0:T(8,128)(2,1)S(1)}, bf16[96,256]{1,0:T(8,128)(2,1)S(1)}, u32[]{:S(2)}, u32[]{:S(2)}) %collective-permute-start.19) | collective-permute-done | bytes 49184 | tf_op jit(solution)/shard_map/ppermute | solution.py:430
  84.9 0.3 collective-permute-done.18.refs_1_
  85.2 0.9 %join.1 = f32[768,256]{1,0:T(8,128)} custom-call(bf16[96,256]{1,0:T(8,128)(2,1)S(1)} %sum.1.refs_0_, bf16[96,256]{1,0:T(8,128)(2,1)S(1)} %collective-permute-done.18.refs_1_, bf16[96,256]{1,0:T(8,128)(2,1)S(1)} %collective-permute-done.19.refs_2_, bf16[96,256]{1,0:T(8,128)(2,1)S(1)} %collective-permute-done.20.refs_3_, ...), custom_call_target="tpu_custom_call" | custom-call | tf_op jit(solution)/shard_map/join/pallas_call | solution.py:386
  (9 shorter events, 0.0 us)
Async XLA Ops:
  0.6 10.6 %copy-start = (bf16[1,3,256,256]{3,2,1,0:T(8,128)(2,1)S(1)}, bf16[1,3,256,256]{3,2,1,0:T(8,128)(2,1)}, u32[]{:S(2)}) copy-start(bf16[1,3,256,256]{3,2,1,0:T(8,128)(2,1)} %refs_3_.7) | copy-start | bytes 1179652
  1.7 9.4 %collective-permute-start.1 = (bf16[2,128,256]{2,1,0:T(8,128)(2,1)S(1)}, bf16[2,128,256]{2,1,0:T(8,128)(2,1)S(1)}, u32[]{:S(2)}, u32[]{:S(2)}) collective-permute-start(bf16[2,128,256]{2,1,0:T(8,128)(2,1)S(1)} %get-tuple-element.58), channel_id=1, source_target_pairs={{0,1},{1,0},{2,3},{3,2},{4,8},{5,9},{6,10},{7,11},{8,4},{9,5},{10,... | collective-permute-start | bytes 393224 | tf_op jit(solution)/shard_map/ppermute | solution.py:408
  2.3 8.9 %collective-permute-start = (bf16[2,128,256]{2,1,0:T(8,128)(2,1)S(1)}, bf16[2,128,256]{2,1,0:T(8,128)(2,1)S(1)}, u32[]{:S(2)}, u32[]{:S(2)}) collective-permute-start(bf16[2,128,256]{2,1,0:T(8,128)(2,1)S(1)} %get-tuple-element.59), channel_id=1, source_target_pairs={{0,4},{1,5},{2,6},{3,7},{4,0},{5,1},{6,2},{7,3},{8,12},{9,13},{10,... | collective-permute-start | bytes 393224 | tf_op jit(solution)/shard_map/ppermute | solution.py:409
  6.3 1.5 %copy-start.1 = (bf16[3,8,5,64,64]{4,3,2,1,0:T(8,128)(2,1)S(1)}, bf16[3,8,5,64,64]{4,3,2,1,0:T(8,128)(2,1)}, u32[]{:S(2)}) copy-start(bf16[3,8,5,64,64]{4,3,2,1,0:T(8,128)(2,1)} %quad_in.1) | copy-start | bytes 2949124
  7.8 0.7 copy-start.4
  8.5 0.7 copy-start.5
  9.2 2.0 %copy-start.2 = (bf16[1,2,512,256]{3,2,1,0:T(8,128)(2,1)S(1)}, bf16[1,2,512,256]{3,2,1,0:T(8,128)(2,1)}, u32[]{:S(2)}) copy-start(bf16[1,2,512,256]{3,2,1,0:T(8,128)(2,1)} %x_ref.1) | copy-start | bytes 1572868
  11.1 2.9 %copy-start.3 = (bf16[2,512,256]{2,1,0:T(8,128)(2,1)S(1)}, bf16[2,512,256]{2,1,0:T(8,128)(2,1)}, u32[]{:S(2)}) copy-start(bf16[2,512,256]{2,1,0:T(8,128)(2,1)} %refs_0_.1) | copy-start | bytes 1572868
  14.0 2.4 %collective-permute-start.2 = (bf16[2,512,256]{2,1,0:T(8,128)(2,1)S(1)}, bf16[2,512,256]{2,1,0:T(8,128)(2,1)S(1)}, u32[]{:S(2)}, u32[]{:S(2)}) collective-permute-start(bf16[2,512,256]{2,1,0:T(8,128)(2,1)S(1)} %get-tuple-element.33.refs_6_), channel_id=1, source_target_pairs={{0,1},{1,0},{2,3},{3,2},{4,5},{5,4},{6,7},{7,6},{8,9},{9,8},{10,11... | collective-permute-start | bytes 1572872 | tf_op jit(solution)/shard_map/ppermute | solution.py:420
  14.1 2.1 %collective-permute-start.3 = (bf16[2,128,256]{2,1,0:T(8,128)(2,1)S(1)}, bf16[2,128,256]{2,1,0:T(8,128)(2,1)S(1)}, u32[]{:S(2)}, u32[]{:S(2)}) collective-permute-start(bf16[2,128,256]{2,1,0:T(8,128)(2,1)S(1)} %get-tuple-element.34.refs_8_), channel_id=1, source_target_pairs={{3,6},{7,10},{11,14},{15,18},{19,22},{23,26},{27,30},{31,27},{30,3... | collective-permute-start | bytes 393224 | tf_op jit(solution)/shard_map/ppermute | solution.py:418
  14.6 1.8 %collective-permute-start.4 = (bf16[2,128,256]{2,1,0:T(8,128)(2,1)S(1)}, bf16[2,128,256]{2,1,0:T(8,128)(2,1)S(1)}, u32[]{:S(2)}, u32[]{:S(2)}) collective-permute-start(bf16[2,128,256]{2,1,0:T(8,128)(2,1)S(1)} %get-tuple-element.35.refs_7_), channel_id=1, source_target_pairs={{31,26},{27,22},{23,18},{19,14},{15,10},{11,6},{7,2},{3,7},{2,3},{... | collective-permute-start | bytes 393224 | tf_op jit(solution)/shard_map/ppermute | solution.py:419
  16.4 19.0 %collective-permute-start.5 = (bf16[2,512,256]{2,1,0:T(8,128)(2,1)S(1)}, bf16[2,512,256]{2,1,0:T(8,128)(2,1)S(1)}, u32[]{:S(2)}, u32[]{:S(2)}) collective-permute-start(bf16[2,512,256]{2,1,0:T(8,128)(2,1)S(1)} %get-tuple-element.37.refs_6_), channel_id=1, source_target_pairs={{0,3},{1,0},{2,1},{3,2},{4,7},{5,4},{6,5},{7,6},{8,11},{9,8},{10,9... | collective-permute-start | bytes 1572872 | tf_op jit(solution)/shard_map/ppermute | solution.py:420
  25.9 6.1 %collective-permute-start.6 = (bf16[2,128,256]{2,1,0:T(8,128)(2,1)S(1)}, bf16[2,128,256]{2,1,0:T(8,128)(2,1)S(1)}, u32[]{:S(2)}, u32[]{:S(2)}) collective-permute-start(bf16[2,128,256]{2,1,0:T(8,128)(2,1)S(1)} %get-tuple-element.38.refs_8_), channel_id=1, source_target_pairs={{2,5},{6,9},{10,13},{14,17},{18,21},{22,25},{26,29},{30,26},{29,30... | collective-permute-start | bytes 393224 | tf_op jit(solution)/shard_map/ppermute | solution.py:418
  28.1 5.3 %collective-permute-start.7 = (bf16[2,128,256]{2,1,0:T(8,128)(2,1)S(1)}, bf16[2,128,256]{2,1,0:T(8,128)(2,1)S(1)}, u32[]{:S(2)}, u32[]{:S(2)}) collective-permute-start(bf16[2,128,256]{2,1,0:T(8,128)(2,1)S(1)} %get-tuple-element.39.refs_7_), channel_id=1, source_target_pairs={{30,25},{26,21},{22,17},{18,13},{14,9},{10,5},{6,1},{2,6},{1,2},{2... | collective-permute-start | bytes 393224 | tf_op jit(solution)/shard_map/ppermute | solution.py:419
  35.3 10.4 %collective-permute-start.8 = (bf16[2,512,256]{2,1,0:T(8,128)(2,1)S(1)}, bf16[2,512,256]{2,1,0:T(8,128)(2,1)S(1)}, u32[]{:S(2)}, u32[]{:S(2)}) collective-permute-start(bf16[2,512,256]{2,1,0:T(8,128)(2,1)S(1)} %get-tuple-element.41.refs_6_), channel_id=1, source_target_pairs={{0,1},{1,0},{2,3},{3,2},{4,5},{5,4},{6,7},{7,6},{8,9},{9,8},{10,11... | collective-permute-start | bytes 1572872 | tf_op jit(solution)/shard_map/ppermute | solution.py:420
  36.7 5.9 %collective-permute-start.9 = (bf16[2,128,256]{2,1,0:T(8,128)(2,1)S(1)}, bf16[2,128,256]{2,1,0:T(8,128)(2,1)S(1)}, u32[]{:S(2)}, u32[]{:S(2)}) collective-permute-start(bf16[2,128,256]{2,1,0:T(8,128)(2,1)S(1)} %get-tuple-element.42.refs_8_), channel_id=1, source_target_pairs={{1,4},{5,8},{9,12},{13,16},{17,20},{21,24},{25,28},{29,25},{28,29}... | collective-permute-start | bytes 393224 | tf_op jit(solution)/shard_map/ppermute | solution.py:418
  36.8 9.0 %collective-permute-start.10 = (bf16[2,128,256]{2,1,0:T(8,128)(2,1)S(1)}, bf16[2,128,256]{2,1,0:T(8,128)(2,1)S(1)}, u32[]{:S(2)}, u32[]{:S(2)}) collective-permute-start(bf16[2,128,256]{2,1,0:T(8,128)(2,1)S(1)} %get-tuple-element.43.refs_7_), channel_id=1, source_target_pairs={{29,24},{25,20},{21,16},{17,12},{13,8},{9,4},{5,0},{1,5},{0,1},{20... | collective-permute-start | bytes 393224 | tf_op jit(solution)/shard_map/ppermute | solution.py:419
  48.4 19.8 %collective-permute-start.11 = (bf16[352,256]{1,0:T(8,128)(2,1)S(1)}, bf16[352,256]{1,0:T(8,128)(2,1)S(1)}, u32[]{:S(2)}, u32[]{:S(2)}) collective-permute-start(bf16[352,256]{1,0:T(8,128)(2,1)S(1)} %get-tuple-element.50), channel_id=1, source_target_pairs={{0,4},{4,0},{8,12},{12,8},{16,20},{20,16},{24,28},{28,24},{1,5},{5... | collective-permute-start | bytes 540680 | tf_op jit(solution)/shard_map/ppermute | solution.py:427
  50.5 17.7 %collective-permute-start.12 = (bf16[352,256]{1,0:T(8,128)(2,1)S(1)}, bf16[352,256]{1,0:T(8,128)(2,1)S(1)}, u32[]{:S(2)}, u32[]{:S(2)}) collective-permute-start(bf16[352,256]{1,0:T(8,128)(2,1)S(1)} %get-tuple-element.51), channel_id=1, source_target_pairs={{0,28},{4,8},{8,4},{12,16},{16,12},{20,24},{24,20},{28,0},{1,29},{... | collective-permute-start | bytes 540680 | tf_op jit(solution)/shard_map/ppermute | solution.py:427
  56.5 5.9 %collective-permute-start.13 = (bf16[96,256]{1,0:T(8,128)(2,1)S(1)}, bf16[96,256]{1,0:T(8,128)(2,1)S(1)}, u32[]{:S(2)}, u32[]{:S(2)}) collective-permute-start(bf16[96,256]{1,0:T(8,128)(2,1)S(1)} %get-tuple-element.53), channel_id=1, source_target_pairs={{0,24},{4,28},{8,16},{12,20},{16,8},{20,12},{24,0},{28,4},{1,25},{... | collective-permute-start | bytes 147464 | tf_op jit(solution)/shard_map/ppermute | solution.py:427
  57.6 6.5 %collective-permute-start.14 = (bf16[96,256]{1,0:T(8,128)(2,1)S(1)}, bf16[96,256]{1,0:T(8,128)(2,1)S(1)}, u32[]{:S(2)}, u32[]{:S(2)}) collective-permute-start(bf16[96,256]{1,0:T(8,128)(2,1)S(1)} %get-tuple-element.54), channel_id=1, source_target_pairs={{0,20},{4,16},{8,28},{12,24},{16,4},{20,0},{24,12},{28,8},{1,21},{... | collective-permute-start | bytes 147464 | tf_op jit(solution)/shard_map/ppermute | solution.py:427
  57.7 7.7 %collective-permute-start.15 = (bf16[96,256]{1,0:T(8,128)(2,1)S(1)}, bf16[96,256]{1,0:T(8,128)(2,1)S(1)}, u32[]{:S(2)}, u32[]{:S(2)}) collective-permute-start(bf16[96,256]{1,0:T(8,128)(2,1)S(1)} %get-tuple-element.55), channel_id=1, source_target_pairs={{0,16},{4,24},{8,20},{12,28},{16,0},{20,8},{24,4},{28,12},{1,17},{... | collective-permute-start | bytes 147464 | tf_op jit(solution)/shard_map/ppermute | solution.py:427
  62.4 5.5 %collective-permute-start.16 = (bf16[96,256]{1,0:T(8,128)(2,1)S(1)}, bf16[96,256]{1,0:T(8,128)(2,1)S(1)}, u32[]{:S(2)}, u32[]{:S(2)}) collective-permute-start(bf16[96,256]{1,0:T(8,128)(2,1)S(1)} %get-tuple-element.56), channel_id=1, source_target_pairs={{0,12},{4,20},{8,24},{12,0},{16,28},{20,4},{24,8},{28,16},{1,13},{... | collective-permute-start | bytes 147464 | tf_op jit(solution)/shard_map/ppermute | solution.py:427
  64.1 4.1 %collective-permute-start.17 = (bf16[96,256]{1,0:T(8,128)(2,1)S(1)}, bf16[96,256]{1,0:T(8,128)(2,1)S(1)}, u32[]{:S(2)}, u32[]{:S(2)}) collective-permute-start(bf16[96,256]{1,0:T(8,128)(2,1)S(1)} %get-tuple-element.57), channel_id=1, source_target_pairs={{0,8},{4,12},{8,0},{12,4},{16,24},{20,28},{24,16},{28,20},{1,9},{5... | collective-permute-start | bytes 147464 | tf_op jit(solution)/shard_map/ppermute | solution.py:427
  68.2 9.8 %collective-permute-start.24 = (bf16[96,256]{1,0:T(8,128)(2,1)S(1)}, bf16[96,256]{1,0:T(8,128)(2,1)S(1)}, u32[]{:S(2)}, u32[]{:S(2)}) collective-permute-start(bf16[96,256]{1,0:T(8,128)(2,1)S(1)} %sum.1.refs_0_), channel_id=1, source_target_pairs={{0,8},{4,12},{8,0},{12,4},{16,24},{20,28},{24,16},{28,20},{1,9},{5... | collective-permute-start | bytes 147464 | tf_op jit(solution)/shard_map/ppermute | solution.py:430
  70.0 10.6 %collective-permute-start.23 = (bf16[96,256]{1,0:T(8,128)(2,1)S(1)}, bf16[96,256]{1,0:T(8,128)(2,1)S(1)}, u32[]{:S(2)}, u32[]{:S(2)}) collective-permute-start(bf16[96,256]{1,0:T(8,128)(2,1)S(1)} %sum.1.refs_0_), channel_id=1, source_target_pairs={{0,12},{4,20},{8,24},{12,0},{16,28},{20,4},{24,8},{28,16},{1,13},{... | collective-permute-start | bytes 147464 | tf_op jit(solution)/shard_map/ppermute | solution.py:430
  73.0 8.6 %collective-permute-start.22 = (bf16[96,256]{1,0:T(8,128)(2,1)S(1)}, bf16[96,256]{1,0:T(8,128)(2,1)S(1)}, u32[]{:S(2)}, u32[]{:S(2)}) collective-permute-start(bf16[96,256]{1,0:T(8,128)(2,1)S(1)} %sum.1.refs_0_), channel_id=1, source_target_pairs={{0,16},{4,24},{8,20},{12,28},{16,0},{20,8},{24,4},{28,12},{1,17},{... | collective-permute-start | bytes 147464 | tf_op jit(solution)/shard_map/ppermute | solution.py:430
  73.0 8.6 %collective-permute-start.21 = (bf16[96,256]{1,0:T(8,128)(2,1)S(1)}, bf16[96,256]{1,0:T(8,128)(2,1)S(1)}, u32[]{:S(2)}, u32[]{:S(2)}) collective-permute-start(bf16[96,256]{1,0:T(8,128)(2,1)S(1)} %sum.1.refs_0_), channel_id=1, source_target_pairs={{0,20},{4,16},{8,28},{12,24},{16,4},{20,0},{24,12},{28,8},{1,21},{... | collective-permute-start | bytes 147464 | tf_op jit(solution)/shard_map/ppermute | solution.py:430
  75.2 6.4 %collective-permute-start.20 = (bf16[96,256]{1,0:T(8,128)(2,1)S(1)}, bf16[96,256]{1,0:T(8,128)(2,1)S(1)}, u32[]{:S(2)}, u32[]{:S(2)}) collective-permute-start(bf16[96,256]{1,0:T(8,128)(2,1)S(1)} %sum.1.refs_0_), channel_id=1, source_target_pairs={{0,24},{4,28},{8,16},{12,20},{16,8},{20,12},{24,0},{28,4},{1,25},{... | collective-permute-start | bytes 147464 | tf_op jit(solution)/shard_map/ppermute | solution.py:430
  78.0 6.9 %collective-permute-start.19 = (bf16[96,256]{1,0:T(8,128)(2,1)S(1)}, bf16[96,256]{1,0:T(8,128)(2,1)S(1)}, u32[]{:S(2)}, u32[]{:S(2)}) collective-permute-start(bf16[96,256]{1,0:T(8,128)(2,1)S(1)} %sum.1.refs_0_), channel_id=1, source_target_pairs={{0,28},{4,8},{8,4},{12,16},{16,12},{20,24},{24,20},{28,0},{1,29},{... | collective-permute-start | bytes 147464 | tf_op jit(solution)/shard_map/ppermute | solution.py:430
  80.6 4.6 %collective-permute-start.18 = (bf16[96,256]{1,0:T(8,128)(2,1)S(1)}, bf16[96,256]{1,0:T(8,128)(2,1)S(1)}, u32[]{:S(2)}, u32[]{:S(2)}) collective-permute-start(bf16[96,256]{1,0:T(8,128)(2,1)S(1)} %sum.1.refs_0_), channel_id=1, source_target_pairs={{0,4},{4,0},{8,12},{12,8},{16,20},{20,16},{24,28},{28,24},{1,5},{5... | collective-permute-start | bytes 147464 | tf_op jit(solution)/shard_map/ppermute | solution.py:430

commit v3 on v2

--- a/solution.py
+++ b/solution.py
@@ -6,6 +6,7 @@
 from jax.experimental import pallas as pl
 from jax.experimental.pallas import tpu as pltpu
 from jax.sharding import PartitionSpec as P
+
 
 KB = 3
 BLK = 64
@@ -77,19 +78,23 @@
 def slant_pairs(lats, sections, turn, upward):
     last, low = lats - 1, turn - 1
     ways = {(i, turn): (i + 1, low) for i in range(last)}
-    ways[last, turn] = (last - 1, turn)
-    ways[last, low] = (last, turn)
-    ways.update({(i, low): (i - 1, turn) for i in range(2, last)})
-    ways[1, low] = (0, low)
-    ways[0, low] = (0, turn)
+    if turn % 2 and sections > 2:
+        aside = (turn - 2) % sections
+        ways[last, turn] = (last, aside)
+        ways.update({(i, aside): (i - 1, aside) for i in range(1, lats)})
+        ways[0, aside] = (0, low)
+        ways.update({(i, low): (i, turn) for i in range(lats)})
+        for i in range(lats):
+            for s in range(sections):
+                ways.setdefault((i, s), (i ^ 1, s))
+        assert len(set(ways.values())) == lats * sections
     if not upward:
         ways = {(last - i, s): (last - j, r) for (i, s), (j, r) in ways.items()}
-    for i in range(lats):
-        for s in range(sections):
-            ways.setdefault((i, s), (i, s ^ 1) if turn % 2 else (i ^ 1, s))
-    pairs = [(i * sections + s, j * sections + r) for (i, s), (j, r) in ways.items()]
-    assert len({b for _, b in pairs}) == lats * sections
-    return pairs
+    return [(i * sections + s, j * sections + r) for (i, s), (j, r) in ways.items()]
+
+
+def cost(flops):
+    return pl.CostEstimate(flops=flops, bytes_accessed=flops // 256, transcendentals=0)
 
 
 def dot(a, b):
@@ -153,7 +158,7 @@
         ],
         compiler_params=params(),
         name="band",
-    )(block_index, block_mask, quad)
+    )(*(pltpu.with_memory_space_constraint(a, pltpu.HBM) for a in (block_index, block_mask, quad)))
 
 
 def hidden_kernel(x_ref, near_ref, far_ref, band_ref, w_ref, hid_ref, gp_ref, ext_ref, sems):
@@ -202,43 +207,74 @@
     )(x, near, far, band, weights)
 
 
-def step_kernel(turn, lats, *refs):
+PARTS = {"edge": ("left", "right", "slope"), "bulk": ("out",), "whole": ("left", "right", "slope", "out")}
+
+
+def back_terms(slope, w_ref, stack_ref):
+    size = slope.shape[0]
+    for k in range(KB):
+        back = lax.dot_general(
+            slope, w_ref[0, k], (((1,), (1,)), ((), ())), preferred_element_type=F32
+        )
+        stack_ref[k * size : (k + 1) * size, :] = back.astype(BF)
+
+
+def step_kernel(turn, lats, part, *refs):
     first = lats is None
     (main_ref, gp_ref, flip_ref, w_ref), rest = refs[:4], refs[4:]
     if not first:
-        (below_ref, above_ref), rest = rest[:2], rest[6:]
+        (below_ref, above_ref), rest = rest[:2], rest[2 + len(PARTS[part]) :]
+    outs, (stack_ref, term_ref) = dict(zip(PARTS[part], rest)), rest[-2:]
     lat = lax.axis_index("lat")
-    out_ref, left_ref, right_ref, slope_ref, stack_ref, term_ref = rest
     rows = gp_ref.shape[1]
     size = GRP * BLK
     edge = HALO * BLK
+    lap = 2 * edge
     groups = rows // size
+
+    def grad_of(m, g):
+        grad = main_ref[m, g * size : (g + 1) * size, :].astype(F32)
+        if first:
+            return grad
+        parts = [grad[i * edge : (i + 1) * edge] for i in range(size // edge)]
+        if g == 0:
+            parts[0] += jnp.where(lat > 0, below_ref[m].astype(F32), 0.0)
+        if g == groups - 1:
+            parts[-1] += jnp.where(lat < lats - 1, above_ref[m].astype(F32), 0.0)
+        return jnp.concatenate(parts, axis=0).astype(BF).astype(F32)
+
+    def edges(m):
+        for name, g, rim, at, low in (
+            ("left", 0, 0, 0, 0),
+            ("right", groups - 1, size + edge, rows - edge, size - edge),
+        ):
+            back_terms(outs["slope"][m, at : at + edge, :], w_ref, stack_ref)
+            term = None
+            for k in range(KB):
+                band = flip_ref[g, rim : rim + edge, k * size + low : k * size + low + edge]
+                new = dot(band, stack_ref[k * edge : (k + 1) * edge, :])
+                term = new if term is None else term + new
+            outs[name][m] = term.astype(BF)
 
     @pl.when(lax.axis_index("section") == turn)
     def _():
         for m in range(MB):
             for g in range(groups):
-                at = pl.ds(g * size, size)
-                grad = main_ref[m, at, :].astype(F32)
-                if not first:
-                    parts = [grad[i * edge : (i + 1) * edge] for i in range(size // edge)]
-                    if g == 0:
-                        parts[0] += jnp.where(lat > 0, below_ref[m].astype(F32), 0.0)
-                    if g == groups - 1:
-                        parts[-1] += jnp.where(lat < lats - 1, above_ref[m].astype(F32), 0.0)
-                    grad = jnp.concatenate(parts, axis=0).astype(BF).astype(F32)
-                slope = (grad * gp_ref[m, at, :]).astype(BF)
-                slope_ref[m, at, :] = slope
-                for k in range(KB):
-                    back = lax.dot_general(
-                        slope, w_ref[0, k], (((1,), (1,)), ((), ())), preferred_element_type=F32
-                    )
-                    stack_ref[k * size : (k + 1) * size, :] = back.astype(BF)
+                grad = grad_of(m, g)
+                at = slice(g * size, (g + 1) * size)
+                if part == "bulk":
+                    slope = gp_ref[m, at, :]
+                else:
+                    slope = (grad * gp_ref[m, at, :]).astype(BF)
+                    outs["slope"][m, at, :] = slope
+                if part == "edge":
+                    continue
+                back_terms(slope, w_ref, stack_ref)
                 term = dot(flip_ref[g], stack_ref[...])
-                lap = 2 * edge
                 low = g * size
                 if g == 0:
-                    left_ref[m] = term[:edge].astype(BF)
+                    if part == "whole":
+                        outs["left"][m] = term[:edge].astype(BF)
                     term_ref[low + edge : low + lap, :] = term[edge:lap] + grad[: lap - edge]
                 else:
                     term_ref[low : low + lap, :] += term[:lap]
@@ -246,44 +282,45 @@
                 term_ref[low + lap : low + size + edge, :] = (
                     term[lap : size + edge] + grad[lap - edge :]
                 )
-                if g == groups - 1:
-                    right_ref[m] = term[size + edge :].astype(BF)
-                else:
+                if g < groups - 1:
                     term_ref[low + size + edge : low + size + lap, :] = term[size + edge :]
-            out_ref[m] = term_ref[edge : edge + rows, :].astype(BF)
-
-
-def step_call(turn, lats, main, sides, gp, flip, weights, olds):
-    mb, rows, ch = gp.shape
+                elif part == "whole":
+                    outs["right"][m] = term[size + edge :].astype(BF)
+            if part == "edge":
+                edges(m)
+            else:
+                outs["out"][m] = term_ref[edge : edge + rows, :].astype(BF)
+
+
+def step_call(turn, lats, part, main, factor, sides, flip, weights, state):
+    mb, rows, ch = main.shape
     edge = HALO * BLK
-    shapes = ((mb, rows, ch), (mb, edge, ch), (mb, edge, ch), (mb, rows, ch))
-    args = (main, gp, flip, weights) + sides + olds
-    aliases = {6 + i: i for i in range(len(olds))}
-    return pl.pallas_call(
-        functools.partial(step_kernel, turn, lats if olds else None),
-        out_shape=tuple(pltpu.VMEM(s, BF) for s in shapes),
+    names = PARTS[part]
+    olds = tuple(state[name] for name in names) if sides else ()
+    args = (main, factor, flip, weights) + sides + olds
+    tall = {"left": edge, "right": edge, "slope": rows, "out": rows}
+    outs = pl.pallas_call(
+        functools.partial(step_kernel, turn, lats if sides else None, part),
+        out_shape=tuple(pltpu.VMEM((mb, tall[name], ch), BF) for name in names),
         in_specs=[VM] * len(args),
-        out_specs=(VM,) * 4,
-        input_output_aliases=aliases,
+        out_specs=(VM,) * len(names),
+        input_output_aliases={6 + i: i for i in range(len(olds))},
         scratch_shapes=[
             pltpu.VMEM((KB * GRP * BLK, ch), BF),
             pltpu.VMEM((rows + 2 * edge, ch), F32),
         ],
         compiler_params=params(),
-        name=f"step{turn}",
+        cost_estimate=cost(3 * MB * rows * KB * ch * ch * 2) if part == "bulk" else None,
     )(*args)
-
-
-def weight_kernel(ways, hid_ref, slope_ref, left_ref, right_ref, *refs):
-    out_refs, acc_ref = refs[:-1], refs[-1]
-    n = len(ways) + 1
-    me = lax.axis_index("lat")
+    state.update(zip(names, outs))
+
+
+def weight_terms(hid_ref, slope_ref, acc_ref):
     size = GRP * BLK
-    groups = hid_ref.shape[1]
     for k in range(KB):
         total = None
         for m in range(MB):
-            for g in range(groups):
+            for g in range(hid_ref.shape[1]):
                 part = lax.dot_general(
                     hid_ref[m, g, k * size : (k + 1) * size, :],
                     slope_ref[m, g * size : (g + 1) * size, :],
@@ -292,59 +329,162 @@
                 )
                 total = part if total is None else total + part
         acc_ref[k * total.shape[0] : (k + 1) * total.shape[0], :] = total
-    piece = acc_ref.shape[0] // n
+
+
+def weight_call(hid, slope):
+    ch = slope.shape[2]
+    return pl.pallas_call(
+        weight_terms,
+        out_shape=pltpu.VMEM((KB * ch, ch), F32),
+        in_specs=[VM] * 2,
+        out_specs=VM,
+        compiler_params=params(),
+        name="weight",
+    )(hid, slope)
+
+
+def shared(ways, j, own):
+    me, second = lax.axis_index("lat"), lax.axis_index("section") % 2 == 1
+    ends = [partner_of(ways[2 * j + c], me) for c in range(2)]
+    return jnp.where(second == own, ends[1], ends[0])
+
+
+def lay_edges(out_ref, skip, even_ref, odd_ref):
+    odd = lax.axis_index("lat") % 2 == 1
+    edge = even_ref.shape[1]
+    for m in range(MB):
+        out_ref[skip + m * edge : skip + (m + 1) * edge, :] = jnp.where(odd, odd_ref[m], even_ref[m])
+
+
+def cut_kernel(way, ways, hid_ref, slope_ref, left_ref, right_ref, own_ref, ride_ref, keep_ref, give_ref, acc_ref):
+    weight_terms(hid_ref, slope_ref, acc_ref)
+    me = lax.axis_index("lat")
+    piece = own_ref.shape[0]
 
     def cut(i):
         return acc_ref[pl.ds(pl.multiple_of(i * piece, piece), piece), :]
 
-    if n == 1:
-        out_refs[0][...] = acc_ref[...]
-        return
-    out_refs[0][...] = cut(me)
-    odd = me % 2 == 1
-    edge = left_ref.shape[1]
-    for s, way in enumerate(ways):
-        out_refs[s + 1][:piece, :] = cut(partner_of(way, me)).astype(BF)
-        if s < 2:
-            for m in range(MB):
-                rows = slice(piece + m * edge, piece + (m + 1) * edge)
-                low, high = (right_ref, left_ref) if s == 0 else (left_ref, right_ref)
-                out_refs[s + 1][rows, :] = jnp.where(odd, high[m], low[m])
-
-
-def weight_call(ways, hid, slope, left, right):
+    own_ref[...] = cut(me)
+    ride_ref[:piece, :] = cut(partner_of(way, me)).astype(BF)
+    lay_edges(ride_ref, piece, right_ref, left_ref)
+    for j in range(len(ways) // 2):
+        keep_ref[j * piece : (j + 1) * piece, :] = cut(shared(ways, j, True)).astype(BF)
+        give_ref[j * piece : (j + 1) * piece, :] = cut(shared(ways, j, False)).astype(BF)
+
+
+def pack_kernel(keep_ref, got_ref, *out_refs):
+    piece = out_refs[0].shape[0] // 2
+    for j, ref in enumerate(out_refs):
+        ref[:piece, :] = keep_ref[j * piece : (j + 1) * piece, :]
+        ref[piece:, :] = got_ref[j * piece : (j + 1) * piece, :]
+
+
+def sum_kernel(own_ref, ride_ref, *refs):
+    piece = own_ref.shape[0]
+    mine, theirs = own_ref[...] + ride_ref[:piece, :].astype(F32), 0.0
+    for ref in refs[:-1]:
+        mine += ref[:piece, :].astype(F32)
+        theirs += ref[piece:, :].astype(F32)
+    refs[-1][:piece, :] = mine.astype(BF)
+    refs[-1][piece:, :] = theirs.astype(BF)
+
+
+def final_kernel(both_ref, got_ref, left_ref, right_ref, pair_ref, ride_ref):
+    piece = both_ref.shape[0] // 2
+    mine = (both_ref[:piece, :].astype(F32) + got_ref[piece:, :].astype(F32)).astype(BF)
+    theirs = (both_ref[piece:, :].astype(F32) + got_ref[:piece, :].astype(F32)).astype(BF)
+    pair_ref[:piece, :] = mine
+    pair_ref[piece:, :] = theirs
+    ride_ref[:piece, :] = mine
+    lay_edges(ride_ref, piece, left_ref, right_ref)
+
+
+def split_kernel(*refs):
+    piece = refs[0].shape[0] // 2
+    for j, ref in enumerate(refs[:-1]):
+        refs[-1][j * piece : (j + 1) * piece, :] = ref[piece:, :]
+
+
+def join_kernel(way, ways, pair_ref, ride_ref, got_ref, *refs):
+    met, weight_ref = refs[:-1], refs[-1]
+    me = lax.axis_index("lat")
+    piece = pair_ref.shape[0] // 2
+
+    def place(i, value):
+        weight_ref[pl.ds(pl.multiple_of(i * piece, piece), piece), :] = value.astype(F32)
+
+    place(me, pair_ref[:piece, :])
+    place(partner_of(way, me), ride_ref[:piece, :])
+    for j, ref in enumerate(met):
+        place(shared(ways, j, True), ref[:piece, :])
+        place(shared(ways, j, False), got_ref[j * piece : (j + 1) * piece, :])
+
+
+def small_call(kernel, shapes, *args, scratch=()):
+    return pl.pallas_call(
+        kernel,
+        out_shape=tuple(shapes),
+        in_specs=[VM] * len(args),
+        out_specs=(VM,) * len(shapes),
+        scratch_shapes=list(scratch),
+        compiler_params=params(),
+    )(*args)
+
+
+def reduce_weight(lats, sections, hid, slope, left, right):
     ch = slope.shape[2]
-    piece = KB * ch // (len(ways) + 1)
-    extra = MB * left.shape[1]
-    return pl.pallas_call(
-        functools.partial(weight_kernel, ways),
-        out_shape=(pltpu.VMEM((piece, ch), F32),)
-        + tuple(pltpu.VMEM((piece + (extra if s < 2 else 0), ch), BF) for s in range(len(ways))),
-        in_specs=[VM] * 4,
-        out_specs=(VM,) * (len(ways) + 1),
-        scratch_shapes=[pltpu.VMEM((KB * ch, ch), F32)],
-        compiler_params=params(),
-        name="weight",
-    )(hid, slope, left, right)
-
-
-def sum_kernel(own_ref, *refs):
-    piece = own_ref.shape[0]
-    total = own_ref[...]
-    for ref in refs[:-1]:
-        total += ref[:piece, :].astype(F32)
-    refs[-1][...] = total.astype(BF)
-
-
-def sum_call(own, others):
-    return pl.pallas_call(
-        sum_kernel,
-        out_shape=pltpu.VMEM(own.shape, BF),
-        in_specs=[VM] * (1 + len(others)),
-        out_specs=VM,
-        compiler_params=params(),
-        name="sum",
-    )(own, *others)
+    ways = matchings(lats)
+    first, second = ways[1:], ways[:1] + ways[2:]
+    count = len(first) // 2
+    piece = KB * ch // lats
+    ride = piece + MB * left.shape[1]
+    swap = [(s, s ^ 1) for s in range(sections)]
+
+    def vmem(rows, dtype=BF):
+        return pltpu.VMEM((rows, ch), dtype)
+
+    def meet(arrays, ways):
+        return [
+            lax.ppermute(
+                a,
+                ("lat", "section"),
+                [
+                    (i * sections + s, ways[2 * j + s % 2][i] * sections + s)
+                    for i in range(lats)
+                    for s in range(sections)
+                ],
+            )
+            for j, a in enumerate(arrays)
+        ]
+
+    own, out, keep, give = small_call(
+        functools.partial(cut_kernel, ways[0], first),
+        (vmem(piece, F32), vmem(ride), vmem(count * piece), vmem(count * piece)),
+        hid,
+        slope,
+        left,
+        right,
+        scratch=(vmem(KB * ch, F32),),
+    )
+    got = lax.ppermute(give, "section", swap)
+    near = lax.ppermute(out, "lat", list(enumerate(ways[0])))
+    packs = small_call(pack_kernel, (vmem(2 * piece),) * count, keep, got)
+    (both,) = small_call(sum_kernel, (vmem(2 * piece),), own, near, *meet(packs, first))
+    got = lax.ppermute(both, "section", swap)
+    pair, out = small_call(final_kernel, (vmem(2 * piece), vmem(ride)), both, got, left, right)
+    met = meet([pair] * count, second)
+    far = lax.ppermute(out, "lat", list(enumerate(ways[1])))
+    (give,) = small_call(split_kernel, (vmem(count * piece),), *met)
+    got = lax.ppermute(give, "section", swap)
+    (weight,) = small_call(
+        functools.partial(join_kernel, ways[1], second),
+        (jax.ShapeDtypeStruct((KB * ch, ch), F32),),
+        pair,
+        far,
+        got,
+        *met,
+    )
+    return weight, near, far, piece
 
 
 def grad_kernel(lats, skip, main_ref, near_ref, far_ref, grad_ref):
@@ -373,26 +513,6 @@
     )(main, near, far)
 
 
-def join_kernel(ways, *refs):
-    pieces, weight_ref = refs[:-1], refs[-1]
-    me = lax.axis_index("lat")
-    piece = pieces[0].shape[0]
-    for ref, other in zip(pieces, [me] + [partner_of(way, me) for way in ways]):
-        weight_ref[pl.ds(pl.multiple_of(other * piece, piece), piece), :] = ref[...].astype(F32)
-
-
-def join_call(ways, pieces):
-    piece, ch = pieces[0].shape
-    return pl.pallas_call(
-        functools.partial(join_kernel, ways),
-        out_shape=jax.ShapeDtypeStruct((piece * len(pieces), ch), F32),
-        in_specs=[VM] * len(pieces),
-        out_specs=VM,
-        compiler_params=params(),
-        name="join",
-    )(*pieces)
-
-
 def per_device(saved_input, cotangent, quad_values, block_index, block_mask, weights):
     sections = lax.axis_size("section")
     lats = lax.axis_size("lat")
@@ -410,30 +530,29 @@
     band, flip = band_call(block_index, block_mask, quad_values)
     hid, gp = hidden_call(saved_input, near, far, band, weights)
 
-    state, main, terms = (), cotangent, ()
+    state, main, terms = {}, cotangent, ()
     for turn in reversed(range(sections)):
-        state = step_call(turn, lats, main, terms, gp, flip, weights, state)
-        out, left, right, slope = state
+        if turn % 2 or turn == 0:
+            step_call(turn, lats, "edge", main, gp, terms, flip, weights, state)
+            step_call(turn, lats, "bulk", main, state["slope"], terms, flip, weights, state)
+        else:
+            step_call(turn, lats, "whole", main, gp, terms, flip, weights, state)
         if turn > 0:
-            low = lax.ppermute(right, both, slant_pairs(lats, sections, turn, True))
-            high = lax.ppermute(left, both, slant_pairs(lats, sections, turn, False))
-            main = lax.ppermute(out, "section", hop_pairs(sections, turn))
+            low = lax.ppermute(state["right"], both, slant_pairs(lats, sections, turn, True))
+            high = lax.ppermute(state["left"], both, slant_pairs(lats, sections, turn, False))
+            main = lax.ppermute(state["out"], "section", hop_pairs(sections, turn))
             terms = (low, high)
 
+    left, right, slope = (state[name] for name in PARTS["edge"])
     channels = saved_input.shape[3]
-    if lats == 8:
-        ways = matchings(lats)
-        own, *cuts = weight_call(ways, hid, slope, left, right)
-        met = [lax.ppermute(cut, "lat", list(enumerate(way))) for cut, way in zip(cuts, ways)]
-        mine = sum_call(own, met)
-        grad = grad_call(lats, own.shape[0], out, met[0], met[1])
-        pieces = [mine] + [lax.ppermute(mine, "lat", list(enumerate(way))) for way in ways]
-        weight = join_call(ways, pieces)
+    if lats == 8 and sections % 2 == 0:
+        weight, near, far, skip = reduce_weight(lats, sections, hid, slope, left, right)
     else:
         give = jnp.where(odd == 1, left, right), jnp.where(odd == 1, right, left)
         near, far = (lax.ppermute(g, both, p).reshape(-1, channels) for g, p in zip(give, sides))
-        grad = grad_call(lats, 0, out, near, far)
-        weight = lax.psum(weight_call([], hid, slope, left, right)[0], "lat")
+        skip = 0
+        weight = lax.psum(weight_call(hid, slope), "lat")
+    grad = grad_call(lats, skip, state["out"], near, far)
     return grad, weight.reshape(1, KB, channels, channels)
 
 

time: 86.4 us -> 84.5 us (0.978)
  starting transfers between devices: 46.8 us -> 36.5 us
  waiting for transfers between devices: 25.5 us -> 34.9 us
  local copies, waits for them, and re-layouts: 3.97 us -> 1.08 us
  Pallas kernels: 9.18 us -> 11 us
    ppermute x23 -> x20, starting transfers between devices: 42.2 us -> 31.9 us  [the longest x6 11.5 us: meet(): lax.ppermute(a, ('lat', 'section'), [(i * sections + s, ways[2 * j + s %...]
    ppermute x23 -> x20, waiting for transfers between devices: 25.4 us -> 32.2 us  [the longest x6 14.3 us: meet(): lax.ppermute(a, ('lat', 'section'), [(i * sections + s, ways[2 * j + s %...]
    unnamed x12 -> x6, local copies, waits for them, and re-layouts: 2.93 us -> 0.01 us
    ppermute x1, waiting for transfers between devices: 0.07 us -> 2.72 us  [per_device(): near = lax.ppermute(rim(1 - odd), both, sides[0])]
    pallas_call x7 -> x13, Pallas kernels: 3.58 us -> 5.13 us  [the longest x7 3.4 us: step_call(): pl.pallas_call(functools.partial(step_kernel, turn, lats if sides else No...]
  transfers between devices with their start and end apart: 25 -> 22, of which waited for: 15 -> 11; matrix products, arithmetic and copies ran while one was open for 0% -> 0% of each run, Pallas kernels for 3% -> 6%
where the time goes in v3:
time: 84.5 us; the launch traced here: 84.3 us
  starting transfers between devices  36.5 us (43%)
  waiting for transfers between devices  34.9 us (41%)
  Pallas kernels  11 us (13%)
  local copies, waits for them, and re-layouts  1.08 us (1%)
    ppermute x6, waiting for transfers between devices, meet(): lax.ppermute(a, ('lat', 'section'), [(i * sections + s, ways[2 * j + s %...  14.3 us
    ppermute x6, starting transfers between devices, meet(): lax.ppermute(a, ('lat', 'section'), [(i * sections + s, ways[2 * j + s %...  11.5 us
    ppermute x3, starting transfers between devices, per_device(): main = lax.ppermute(state['out'], 'section', hop_pairs(sections, turn))  8.86 us
    ppermute x3, waiting for transfers between devices, per_device(): lax.ppermute(state['right'], both, slant_pairs(lats, sections, turn, True))  5.74 us
    ppermute x3, waiting for transfers between devices, per_device(): lax.ppermute(state['left'], both, slant_pairs(lats, sections, turn, False))  5.58 us
    ppermute x3, waiting for transfers between devices, per_device(): main = lax.ppermute(state['out'], 'section', hop_pairs(sections, turn))  5.34 us
    ppermute x3, starting transfers between devices, per_device(): lax.ppermute(state['left'], both, slant_pairs(lats, sections, turn, False))  4.07 us
    ppermute x1, starting transfers between devices, per_device(): near = lax.ppermute(rim(1 - odd), both, sides[0])  4.02 us
  transfers between devices with their start and end apart: 22, of which 11 were waited for; matrix products, arithmetic and copies ran while one was open for 0% of the time, Pallas kernels for 6%

profile of v3, /device:TPU:0, one launch (start us, length us, event | category | flops | bytes accessed | tf_op | source)
XLA Modules:
  0.0 84.3 jit_solution(10866006864020203626)
XLA Ops:
  0.6 0.0 copy-start.1
  0.6 0.0 copy-start
  0.7 1.1 %dynamic-slice_bitcast_fusion = (bf16[2,128,256]{2,1,0:T(8,128)(2,1)S(1)}, bf16[2,128,256]{2,1,0:T(8,128)(2,1)S(1)}) fusion(bf16[1,2,512,256]{3,2,1,0:T(8,128)(2,1)} %x_ref.1, s32[]{:T(128)S(6)} %select_n.15, s32[]{:T(128)S(6)} %select_n.14), kind=kLoop, calls=%fused_computation | loop fusion | bytes 524296 | tf_op jit(solution)/shard_map/dynamic_slice | solution.py:526
  1.7 0.6 collective-permute-start.1
  2.3 4.0 %collective-permute-start = (bf16[2,128,256]{2,1,0:T(8,128)(2,1)S(1)}, bf16[2,128,256]{2,1,0:T(8,128)(2,1)S(1)}, u32[]{:S(2)}, u32[]{:S(2)}) collective-permute-start(bf16[2,128,256]{2,1,0:T(8,128)(2,1)S(1)} %get-tuple-element.55), channel_id=1, source_target_pairs={{0,4},{1,5},{2,6},{3,7},{4,0},{5,1},{6,2},{7,3},{8,12},{9,13},{10,... | collective-permute-start | bytes 393224 | tf_op jit(solution)/shard_map/ppermute | solution.py:529
  6.3 2.2 %band.1 = (bf16[2,768,512]{2,1,0:T(8,128)(2,1)S(1)}, bf16[2,512,768]{2,1,0:T(8,128)(2,1)S(1)}) custom-call(s32[8,5]{1,0:T(8,128)} %index_in.1, s32[8,5]{1,0:T(8,128)} %mask_in.1, bf16[3,8,5,64,64]{4,3,2,1,0:T(8,128)(2,1)} %quad_in.1), custom_call_target="tpu_custom_call" | custom-call | tf_op jit(solution)/shard_map/band/pallas_call | solution.py:144
  8.5 0.0 copy-start.2
  8.5 0.0 collective-permute-done.1.far_ref
  8.5 2.7 %collective-permute-done.near_ref = bf16[2,128,256]{2,1,0:T(8,128)(2,1)S(1)} collective-permute-done((bf16[2,128,256]{2,1,0:T(8,128)(2,1)S(1)}, bf16[2,128,256]{2,1,0:T(8,128)(2,1)S(1)}, u32[]{:S(2)}, u32[]{:S(2)}) %collective-permute-start) | collective-permute-done | bytes 131104 | tf_op jit(solution)/shard_map/ppermute | solution.py:529
  11.2 0.0 copy-done.1
  11.2 0.0 copy-done
  11.2 2.8 %hidden.1 = (bf16[2,2,768,256]{3,2,1,0:T(8,128)(2,1)S(1)}, f32[2,512,256]{2,1,0:T(8,128)S(1)}) custom-call(bf16[1,2,512,256]{3,2,1,0:T(8,128)(2,1)S(1)} %copy-done.1, bf16[2,128,256]{2,1,0:T(8,128)(2,1)S(1)} %collective-permute-done.near_ref, bf16[2,128,256]{2,1,0:T(8,128)(2,1)S(1)} %collective-permute-done.1.far_ref, ...), custom_call_target="tpu_custom_call" | custom-call | tf_op jit(solution)/shard_map/hidden/pallas_call | solution.py:193
  14.0 0.0 copy-done.2
  14.1 0.1 collective-permute-start.2
  14.2 2.5 %collective-permute-start.3 = (bf16[2,128,256]{2,1,0:T(8,128)(2,1)S(1)}, bf16[2,128,256]{2,1,0:T(8,128)(2,1)S(1)}, u32[]{:S(2)}, u32[]{:S(2)}) collective-permute-start(bf16[2,128,256]{2,1,0:T(8,128)(2,1)S(1)} %get-tuple-element.32.refs_7_), channel_id=1, source_target_pairs={{3,6},{7,10},{11,14},{15,18},{19,22},{23,26},{27,30},{31,29},{5,1}... | collective-permute-start | bytes 393224 | tf_op jit(solution)/shard_map/ppermute | solution.py:541
  16.7 0.1 collective-permute-start.4
  16.8 4.8 %collective-permute-done.3.refs_4_ = bf16[2,128,256]{2,1,0:T(8,128)(2,1)S(1)} collective-permute-done((bf16[2,128,256]{2,1,0:T(8,128)(2,1)S(1)}, bf16[2,128,256]{2,1,0:T(8,128)(2,1)S(1)}, u32[]{:S(2)}, u32[]{:S(2)}) %collective-permute-start.3) | collective-permute-done | bytes 131104 | tf_op jit(solution)/shard_map/ppermute | solution.py:541
  21.5 1.9 %collective-permute-done.4.refs_5_ = bf16[2,128,256]{2,1,0:T(8,128)(2,1)S(1)} collective-permute-done((bf16[2,128,256]{2,1,0:T(8,128)(2,1)S(1)}, bf16[2,128,256]{2,1,0:T(8,128)(2,1)S(1)}, u32[]{:S(2)}, u32[]{:S(2)}) %collective-permute-start.4) | collective-permute-done | bytes 131104 | tf_op jit(solution)/shard_map/ppermute | solution.py:542
  23.4 0.0 collective-permute-done.2.refs_0_
  23.4 1.0 %collective-permute-start.5 = (bf16[2,512,256]{2,1,0:T(8,128)(2,1)S(1)}, bf16[2,512,256]{2,1,0:T(8,128)(2,1)S(1)}, u32[]{:S(2)}, u32[]{:S(2)}) collective-permute-start(bf16[2,512,256]{2,1,0:T(8,128)(2,1)S(1)} %get-tuple-element.34.refs_6_), channel_id=1, source_target_pairs={{0,3},{1,0},{2,1},{3,2},{4,7},{5,4},{6,5},{7,6},{8,11},{9,8},{10,9... | collective-permute-start | bytes 1572872 | tf_op jit(solution)/shard_map/ppermute | solution.py:543
  24.4 0.7 collective-permute-start.6
  25.1 0.7 collective-permute-start.7
  25.7 0.0 collective-permute-done.6.refs_4_
  25.7 0.0 collective-permute-done.7.refs_5_
  25.7 5.3 %collective-permute-done.5.refs_0_ = bf16[2,512,256]{2,1,0:T(8,128)(2,1)S(1)} collective-permute-done((bf16[2,512,256]{2,1,0:T(8,128)(2,1)S(1)}, bf16[2,512,256]{2,1,0:T(8,128)(2,1)S(1)}, u32[]{:S(2)}, u32[]{:S(2)}) %collective-permute-start.5) | collective-permute-done | bytes 524320 | tf_op jit(solution)/shard_map/ppermute | solution.py:543
  31.1 7.8 %collective-permute-start.8 = (bf16[2,512,256]{2,1,0:T(8,128)(2,1)S(1)}, bf16[2,512,256]{2,1,0:T(8,128)(2,1)S(1)}, u32[]{:S(2)}, u32[]{:S(2)}) collective-permute-start(bf16[2,512,256]{2,1,0:T(8,128)(2,1)S(1)} %shard_map.81.refs_6_), channel_id=1, source_target_pairs={{0,1},{1,0},{2,3},{3,2},{4,5},{5,4},{6,7},{7,6},{8,9},{9,8},{10,11... | collective-permute-start | bytes 1572872 | tf_op jit(solution)/shard_map/ppermute | solution.py:543
  38.9 0.1 collective-permute-start.9
  39.0 3.3 %collective-permute-start.10 = (bf16[2,128,256]{2,1,0:T(8,128)(2,1)S(1)}, bf16[2,128,256]{2,1,0:T(8,128)(2,1)S(1)}, u32[]{:S(2)}, u32[]{:S(2)}) collective-permute-start(bf16[2,128,256]{2,1,0:T(8,128)(2,1)S(1)} %get-tuple-element.40.refs_6_), channel_id=1, source_target_pairs={{29,24},{25,20},{21,16},{17,12},{13,8},{9,4},{5,0},{1,3},{27,31},{... | collective-permute-start | bytes 393224 | tf_op jit(solution)/shard_map/ppermute | solution.py:542
  42.3 1.0 %collective-permute-done.9.refs_4_ = bf16[2,128,256]{2,1,0:T(8,128)(2,1)S(1)} collective-permute-done((bf16[2,128,256]{2,1,0:T(8,128)(2,1)S(1)}, bf16[2,128,256]{2,1,0:T(8,128)(2,1)S(1)}, u32[]{:S(2)}, u32[]{:S(2)}) %collective-permute-start.9) | collective-permute-done | bytes 131104 | tf_op jit(solution)/shard_map/ppermute | solution.py:541
  43.3 3.7 %collective-permute-done.10.refs_5_ = bf16[2,128,256]{2,1,0:T(8,128)(2,1)S(1)} collective-permute-done((bf16[2,128,256]{2,1,0:T(8,128)(2,1)S(1)}, bf16[2,128,256]{2,1,0:T(8,128)(2,1)S(1)}, u32[]{:S(2)}, u32[]{:S(2)}) %collective-permute-start.10) | collective-permute-done | bytes 131104 | tf_op jit(solution)/shard_map/ppermute | solution.py:542
  47.0 0.0 collective-permute-done.8.refs_0_
  47.0 1.4 %shard_map.82 = (bf16[2,128,256]{2,1,0:T(8,128)(2,1)S(1)}, bf16[2,128,256]{2,1,0:T(8,128)(2,1)S(1)}, bf16[2,512,256]{2,1,0:T(8,128)(2,1)S(1)}) custom-call(bf16[2,512,256]{2,1,0:T(8,128)(2,1)S(1)} %collective-permute-done.8.refs_0_, f32[2,512,256]{2,1,0:T(8,128)S(1)} %get-tuple-element.29.refs_1_, ...), custom_call_target="tpu_custom_call", output_to_operand_aliasing={{0}: (6, {}), {1}: (7, {}), {2}: (8, {})} | custom-call | tf_op jit(solution)/shard_map/pallas_call | solution.py:302
  48.4 0.7 shard_map.84
  49.1 0.1 collective-permute-start.12
  49.2 1.1 %collective-permute-start.11 = (bf16[352,256]{1,0:T(8,128)(2,1)S(1)}, bf16[352,256]{1,0:T(8,128)(2,1)S(1)}, u32[]{:S(2)}, u32[]{:S(2)}) collective-permute-start(bf16[352,256]{1,0:T(8,128)(2,1)S(1)} %get-tuple-element.45), channel_id=1, source_target_pairs={{0,4},{4,0},{8,12},{12,8},{16,20},{20,16},{24,28},{28,24},{1,5},{5... | collective-permute-start | bytes 540680 | tf_op jit(solution)/shard_map/ppermute | solution.py:470
  50.2 0.3 collective-permute-done.12.got_ref
  50.6 3.5 %collective-permute-start.13 = (bf16[192,256]{1,0:T(8,128)(2,1)S(1)}, bf16[192,256]{1,0:T(8,128)(2,1)S(1)}, u32[]{:S(2)}, u32[]{:S(2)}) collective-permute-start(bf16[192,256]{1,0:T(8,128)(2,1)S(1)} %get-tuple-element.49), channel_id=1, source_target_pairs={{0,28},{1,25},{2,30},{3,27},{4,8},{5,29},{6,10},{7,31},{8,4},{9,17... | collective-permute-start | bytes 294920 | tf_op jit(solution)/shard_map/ppermute | solution.py:448
  54.0 1.3 %collective-permute-start.14 = (bf16[192,256]{1,0:T(8,128)(2,1)S(1)}, bf16[192,256]{1,0:T(8,128)(2,1)S(1)}, u32[]{:S(2)}, u32[]{:S(2)}) collective-permute-start(bf16[192,256]{1,0:T(8,128)(2,1)S(1)} %get-tuple-element.50), channel_id=1, source_target_pairs={{0,20},{1,17},{2,22},{3,19},{4,16},{5,25},{6,18},{7,27},{8,28},{9,... | collective-permute-start | bytes 294920 | tf_op jit(solution)/shard_map/ppermute | solution.py:448
  55.3 1.6 %collective-permute-start.15 = (bf16[192,256]{1,0:T(8,128)(2,1)S(1)}, bf16[192,256]{1,0:T(8,128)(2,1)S(1)}, u32[]{:S(2)}, u32[]{:S(2)}) collective-permute-start(bf16[192,256]{1,0:T(8,128)(2,1)S(1)} %get-tuple-element.51), channel_id=1, source_target_pairs={{0,12},{1,9},{2,14},{3,11},{4,20},{5,13},{6,22},{7,15},{8,24},{9,1... | collective-permute-start | bytes 294920 | tf_op jit(solution)/shard_map/ppermute | solution.py:448
  56.9 0.0 collective-permute-done.11.ride_ref.near_ref
  56.9 1.7 %collective-permute-done.13.refs_0_ = bf16[192,256]{1,0:T(8,128)(2,1)S(1)} collective-permute-done((bf16[192,256]{1,0:T(8,128)(2,1)S(1)}, bf16[192,256]{1,0:T(8,128)(2,1)S(1)}, u32[]{:S(2)}, u32[]{:S(2)}) %collective-permute-start.13) | collective-permute-done | bytes 98336 | tf_op jit(solution)/shard_map/ppermute | solution.py:448
  58.6 3.6 %collective-permute-done.14.refs_1_ = bf16[192,256]{1,0:T(8,128)(2,1)S(1)} collective-permute-done((bf16[192,256]{1,0:T(8,128)(2,1)S(1)}, bf16[192,256]{1,0:T(8,128)(2,1)S(1)}, u32[]{:S(2)}, u32[]{:S(2)}) %collective-permute-start.14) | collective-permute-done | bytes 98336 | tf_op jit(solution)/shard_map/ppermute | solution.py:448
  62.2 0.0 collective-permute-done.15.refs_2_
  62.2 0.9 %collective-permute-start.16 = (bf16[192,256]{1,0:T(8,128)(2,1)S(1)}, bf16[192,256]{1,0:T(8,128)(2,1)S(1)}, u32[]{:S(2)}, u32[]{:S(2)}) collective-permute-start(bf16[192,256]{1,0:T(8,128)(2,1)S(1)} %shard_map.86.both_ref), channel_id=1, source_target_pairs={{0,1},{1,0},{2,3},{3,2},{4,5},{5,4},{6,7},{7,6},{8,9},{9,8},{10,11... | collective-permute-start | bytes 294920 | tf_op jit(solution)/shard_map/ppermute | solution.py:473
  63.1 0.9 %collective-permute-done.16.got_ref = bf16[192,256]{1,0:T(8,128)(2,1)S(1)} collective-permute-done((bf16[192,256]{1,0:T(8,128)(2,1)S(1)}, bf16[192,256]{1,0:T(8,128)(2,1)S(1)}, u32[]{:S(2)}, u32[]{:S(2)}) %collective-permute-start.16) | collective-permute-done | bytes 98336 | tf_op jit(solution)/shard_map/ppermute | solution.py:473
  64.1 1.3 %collective-permute-start.20 = (bf16[192,256]{1,0:T(8,128)(2,1)S(1)}, bf16[192,256]{1,0:T(8,128)(2,1)S(1)}, u32[]{:S(2)}, u32[]{:S(2)}) collective-permute-start(bf16[192,256]{1,0:T(8,128)(2,1)S(1)} %get-tuple-element.53.pair_ref), channel_id=1, source_target_pairs={{0,12},{1,9},{2,14},{3,11},{4,20},{5,13},{6,22},{7,15},{8,24},{9,1... | collective-permute-start | bytes 294920 | tf_op jit(solution)/shard_map/ppermute | solution.py:448
  65.4 3.6 %collective-permute-start.19 = (bf16[192,256]{1,0:T(8,128)(2,1)S(1)}, bf16[192,256]{1,0:T(8,128)(2,1)S(1)}, u32[]{:S(2)}, u32[]{:S(2)}) collective-permute-start(bf16[192,256]{1,0:T(8,128)(2,1)S(1)} %get-tuple-element.53.pair_ref), channel_id=1, source_target_pairs={{0,20},{1,17},{2,22},{3,19},{4,16},{5,25},{6,18},{7,27},{8,28},{9,... | collective-permute-start | bytes 294920 | tf_op jit(solution)/shard_map/ppermute | solution.py:448
  68.9 0.3 collective-permute-start.18
  69.3 2.1 %collective-permute-start.17 = (bf16[352,256]{1,0:T(8,128)(2,1)S(1)}, bf16[352,256]{1,0:T(8,128)(2,1)S(1)}, u32[]{:S(2)}, u32[]{:S(2)}) collective-permute-start(bf16[352,256]{1,0:T(8,128)(2,1)S(1)} %get-tuple-element.52), channel_id=1, source_target_pairs={{0,28},{4,8},{8,4},{12,16},{16,12},{20,24},{24,20},{28,0},{1,29},{... | collective-permute-start | bytes 540680 | tf_op jit(solution)/shard_map/ppermute | solution.py:476
  71.4 0.0 collective-permute-done.20.refs_2_
  71.4 9.0 %collective-permute-done.19.refs_1_ = bf16[192,256]{1,0:T(8,128)(2,1)S(1)} collective-permute-done((bf16[192,256]{1,0:T(8,128)(2,1)S(1)}, bf16[192,256]{1,0:T(8,128)(2,1)S(1)}, u32[]{:S(2)}, u32[]{:S(2)}) %collective-permute-start.19) | collective-permute-done | bytes 98336 | tf_op jit(solution)/shard_map/ppermute | solution.py:448
  80.4 0.0 collective-permute-done.18.refs_0_
  80.4 0.1 collective-permute-start.21
  80.5 1.9 %shard_map.83.main_ref = bf16[2,512,256]{2,1,0:T(8,128)(2,1)S(1)} custom-call(bf16[2,512,256]{2,1,0:T(8,128)(2,1)S(1)} %collective-permute-done.8.refs_0_, bf16[2,512,256]{2,1,0:T(8,128)(2,1)S(1)} %get-tuple-element.41.refs_1_.slope_ref, bf16[2,512,768]{2,1,0:T(8,128)(2,1)S(1)} %get-tuple-element.30.refs_2_, ...), custom_call_target="tpu_custom_call", output_to_operand_aliasing={{}: (6, {})} | custom-call | flops 1207959552 | bytes 4718592 | tf_op jit(solution)/shard_map/pallas_call | solution.py:302
  82.4 0.0 collective-permute-done.17.far_ref.ride_ref
  82.5 0.9 %grad.1 = bf16[1,2,512,256]{3,2,1,0:T(8,128)(2,1)} custom-call(bf16[2,512,256]{2,1,0:T(8,128)(2,1)S(1)} %shard_map.83.main_ref, bf16[352,256]{1,0:T(8,128)(2,1)S(1)} %collective-permute-done.11.ride_ref.near_ref, bf16[352,256]{1,0:T(8,128)(2,1)S(1)} %collective-permute-done.17.far_ref.ride_ref), custom_call_target="tpu_custom_call" | custom-call | tf_op jit(solution)/shard_map/grad/pallas_call | solution.py:506
  83.4 0.0 collective-permute-done.21.got_ref
  83.4 1.0 %shard_map.89 = f32[768,256]{1,0:T(8,128)} custom-call(bf16[192,256]{1,0:T(8,128)(2,1)S(1)} %get-tuple-element.53.pair_ref, bf16[352,256]{1,0:T(8,128)(2,1)S(1)} %collective-permute-done.17.far_ref.ride_ref, bf16[288,256]{1,0:T(8,128)(2,1)S(1)} %collective-permute-done.21.got_ref, bf16[192,256]{1,0:T(8,128)(2,1)S(1)} %collective-permute-done.18.refs_0_, ...), custom_call_target="tpu_custom_call" | custom-call | tf_op jit(solution)/shard_map/pallas_call | solution.py:424
  (9 shorter events, 0.1 us)
Async XLA Ops:
  0.6 10.6 %copy-start.1 = (bf16[1,2,512,256]{3,2,1,0:T(8,128)(2,1)S(1)}, bf16[1,2,512,256]{3,2,1,0:T(8,128)(2,1)}, u32[]{:S(2)}) copy-start(bf16[1,2,512,256]{3,2,1,0:T(8,128)(2,1)} %x_ref.1) | copy-start | bytes 1572868
  0.6 10.6 %copy-start = (bf16[1,3,256,256]{3,2,1,0:T(8,128)(2,1)S(1)}, bf16[1,3,256,256]{3,2,1,0:T(8,128)(2,1)}, u32[]{:S(2)}) copy-start(bf16[1,3,256,256]{3,2,1,0:T(8,128)(2,1)} %refs_3_.13) | copy-start | bytes 1179652
  1.7 6.8 %collective-permute-start.1 = (bf16[2,128,256]{2,1,0:T(8,128)(2,1)S(1)}, bf16[2,128,256]{2,1,0:T(8,128)(2,1)S(1)}, u32[]{:S(2)}, u32[]{:S(2)}) collective-permute-start(bf16[2,128,256]{2,1,0:T(8,128)(2,1)S(1)} %get-tuple-element.54), channel_id=1, source_target_pairs={{0,1},{1,0},{2,3},{3,2},{4,8},{5,9},{6,10},{7,11},{8,4},{9,5},{10,... | collective-permute-start | bytes 393224 | tf_op jit(solution)/shard_map/ppermute | solution.py:528
  2.3 8.9 %collective-permute-start = (bf16[2,128,256]{2,1,0:T(8,128)(2,1)S(1)}, bf16[2,128,256]{2,1,0:T(8,128)(2,1)S(1)}, u32[]{:S(2)}, u32[]{:S(2)}) collective-permute-start(bf16[2,128,256]{2,1,0:T(8,128)(2,1)S(1)} %get-tuple-element.55), channel_id=1, source_target_pairs={{0,4},{1,5},{2,6},{3,7},{4,0},{5,1},{6,2},{7,3},{8,12},{9,13},{10,... | collective-permute-start | bytes 393224 | tf_op jit(solution)/shard_map/ppermute | solution.py:529
  8.5 5.5 %copy-start.2 = (bf16[2,512,256]{2,1,0:T(8,128)(2,1)S(1)}, bf16[2,512,256]{2,1,0:T(8,128)(2,1)}, u32[]{:S(2)}) copy-start(bf16[2,512,256]{2,1,0:T(8,128)(2,1)} %refs_0_.3) | copy-start | bytes 1572868
  14.1 9.3 %collective-permute-start.2 = (bf16[2,512,256]{2,1,0:T(8,128)(2,1)S(1)}, bf16[2,512,256]{2,1,0:T(8,128)(2,1)S(1)}, u32[]{:S(2)}, u32[]{:S(2)}) collective-permute-start(bf16[2,512,256]{2,1,0:T(8,128)(2,1)S(1)} %shard_map.78.refs_9_), channel_id=1, source_target_pairs={{0,1},{1,0},{2,3},{3,2},{4,5},{5,4},{6,7},{7,6},{8,9},{9,8},{10,11... | collective-permute-start | bytes 1572872 | tf_op jit(solution)/shard_map/ppermute | solution.py:543
  14.2 7.4 %collective-permute-start.3 = (bf16[2,128,256]{2,1,0:T(8,128)(2,1)S(1)}, bf16[2,128,256]{2,1,0:T(8,128)(2,1)S(1)}, u32[]{:S(2)}, u32[]{:S(2)}) collective-permute-start(bf16[2,128,256]{2,1,0:T(8,128)(2,1)S(1)} %get-tuple-element.32.refs_7_), channel_id=1, source_target_pairs={{3,6},{7,10},{11,14},{15,18},{19,22},{23,26},{27,30},{31,29},{5,1}... | collective-permute-start | bytes 393224 | tf_op jit(solution)/shard_map/ppermute | solution.py:541
  16.7 6.7 %collective-permute-start.4 = (bf16[2,128,256]{2,1,0:T(8,128)(2,1)S(1)}, bf16[2,128,256]{2,1,0:T(8,128)(2,1)S(1)}, u32[]{:S(2)}, u32[]{:S(2)}) collective-permute-start(bf16[2,128,256]{2,1,0:T(8,128)(2,1)S(1)} %get-tuple-element.33.refs_6_), channel_id=1, source_target_pairs={{31,26},{27,22},{23,18},{19,14},{15,10},{11,6},{7,2},{3,1},{25,29}... | collective-permute-start | bytes 393224 | tf_op jit(solution)/shard_map/ppermute | solution.py:542
  23.4 7.7 %collective-permute-start.5 = (bf16[2,512,256]{2,1,0:T(8,128)(2,1)S(1)}, bf16[2,512,256]{2,1,0:T(8,128)(2,1)S(1)}, u32[]{:S(2)}, u32[]{:S(2)}) collective-permute-start(bf16[2,512,256]{2,1,0:T(8,128)(2,1)S(1)} %get-tuple-element.34.refs_6_), channel_id=1, source_target_pairs={{0,3},{1,0},{2,1},{3,2},{4,7},{5,4},{6,5},{7,6},{8,11},{9,8},{10,9... | collective-permute-start | bytes 1572872 | tf_op jit(solution)/shard_map/ppermute | solution.py:543
  24.4 1.3 %collective-permute-start.6 = (bf16[2,128,256]{2,1,0:T(8,128)(2,1)S(1)}, bf16[2,128,256]{2,1,0:T(8,128)(2,1)S(1)}, u32[]{:S(2)}, u32[]{:S(2)}) collective-permute-start(bf16[2,128,256]{2,1,0:T(8,128)(2,1)S(1)} %get-tuple-element.35.refs_7_), channel_id=1, source_target_pairs={{2,5},{6,9},{10,13},{14,17},{18,21},{22,25},{26,29}} | collective-permute-start | bytes 393224 | tf_op jit(solution)/shard_map/ppermute | solution.py:541
  25.1 0.7 collective-permute-start.7
  31.1 15.9 %collective-permute-start.8 = (bf16[2,512,256]{2,1,0:T(8,128)(2,1)S(1)}, bf16[2,512,256]{2,1,0:T(8,128)(2,1)S(1)}, u32[]{:S(2)}, u32[]{:S(2)}) collective-permute-start(bf16[2,512,256]{2,1,0:T(8,128)(2,1)S(1)} %shard_map.81.refs_6_), channel_id=1, source_target_pairs={{0,1},{1,0},{2,3},{3,2},{4,5},{5,4},{6,7},{7,6},{8,9},{9,8},{10,11... | collective-permute-start | bytes 1572872 | tf_op jit(solution)/shard_map/ppermute | solution.py:543
  38.9 4.4 %collective-permute-start.9 = (bf16[2,128,256]{2,1,0:T(8,128)(2,1)S(1)}, bf16[2,128,256]{2,1,0:T(8,128)(2,1)S(1)}, u32[]{:S(2)}, u32[]{:S(2)}) collective-permute-start(bf16[2,128,256]{2,1,0:T(8,128)(2,1)S(1)} %get-tuple-element.39.refs_7_), channel_id=1, source_target_pairs={{1,4},{5,8},{9,12},{13,16},{17,20},{21,24},{25,28},{29,31},{7,3},{... | collective-permute-start | bytes 393224 | tf_op jit(solution)/shard_map/ppermute | solution.py:541
  39.0 8.0 %collective-permute-start.10 = (bf16[2,128,256]{2,1,0:T(8,128)(2,1)S(1)}, bf16[2,128,256]{2,1,0:T(8,128)(2,1)S(1)}, u32[]{:S(2)}, u32[]{:S(2)}) collective-permute-start(bf16[2,128,256]{2,1,0:T(8,128)(2,1)S(1)} %get-tuple-element.40.refs_6_), channel_id=1, source_target_pairs={{29,24},{25,20},{21,16},{17,12},{13,8},{9,4},{5,0},{1,3},{27,31},{... | collective-permute-start | bytes 393224 | tf_op jit(solution)/shard_map/ppermute | solution.py:542
  49.1 1.4 %collective-permute-start.12 = (bf16[288,256]{1,0:T(8,128)(2,1)S(1)}, bf16[288,256]{1,0:T(8,128)(2,1)S(1)}, u32[]{:S(2)}, u32[]{:S(2)}) collective-permute-start(bf16[288,256]{1,0:T(8,128)(2,1)S(1)} %get-tuple-element.48), channel_id=1, source_target_pairs={{0,1},{1,0},{2,3},{3,2},{4,5},{5,4},{6,7},{7,6},{8,9},{9,8},{10,11... | collective-permute-start | bytes 442376 | tf_op jit(solution)/shard_map/ppermute | solution.py:469
  49.2 7.7 %collective-permute-start.11 = (bf16[352,256]{1,0:T(8,128)(2,1)S(1)}, bf16[352,256]{1,0:T(8,128)(2,1)S(1)}, u32[]{:S(2)}, u32[]{:S(2)}) collective-permute-start(bf16[352,256]{1,0:T(8,128)(2,1)S(1)} %get-tuple-element.45), channel_id=1, source_target_pairs={{0,4},{4,0},{8,12},{12,8},{16,20},{20,16},{24,28},{28,24},{1,5},{5... | collective-permute-start | bytes 540680 | tf_op jit(solution)/shard_map/ppermute | solution.py:470
  50.6 8.0 %collective-permute-start.13 = (bf16[192,256]{1,0:T(8,128)(2,1)S(1)}, bf16[192,256]{1,0:T(8,128)(2,1)S(1)}, u32[]{:S(2)}, u32[]{:S(2)}) collective-permute-start(bf16[192,256]{1,0:T(8,128)(2,1)S(1)} %get-tuple-element.49), channel_id=1, source_target_pairs={{0,28},{1,25},{2,30},{3,27},{4,8},{5,29},{6,10},{7,31},{8,4},{9,17... | collective-permute-start | bytes 294920 | tf_op jit(solution)/shard_map/ppermute | solution.py:448
  54.0 8.1 %collective-permute-start.14 = (bf16[192,256]{1,0:T(8,128)(2,1)S(1)}, bf16[192,256]{1,0:T(8,128)(2,1)S(1)}, u32[]{:S(2)}, u32[]{:S(2)}) collective-permute-start(bf16[192,256]{1,0:T(8,128)(2,1)S(1)} %get-tuple-element.50), channel_id=1, source_target_pairs={{0,20},{1,17},{2,22},{3,19},{4,16},{5,25},{6,18},{7,27},{8,28},{9,... | collective-permute-start | bytes 294920 | tf_op jit(solution)/shard_map/ppermute | solution.py:448
  55.3 6.8 %collective-permute-start.15 = (bf16[192,256]{1,0:T(8,128)(2,1)S(1)}, bf16[192,256]{1,0:T(8,128)(2,1)S(1)}, u32[]{:S(2)}, u32[]{:S(2)}) collective-permute-start(bf16[192,256]{1,0:T(8,128)(2,1)S(1)} %get-tuple-element.51), channel_id=1, source_target_pairs={{0,12},{1,9},{2,14},{3,11},{4,20},{5,13},{6,22},{7,15},{8,24},{9,1... | collective-permute-start | bytes 294920 | tf_op jit(solution)/shard_map/ppermute | solution.py:448
  62.2 1.8 %collective-permute-start.16 = (bf16[192,256]{1,0:T(8,128)(2,1)S(1)}, bf16[192,256]{1,0:T(8,128)(2,1)S(1)}, u32[]{:S(2)}, u32[]{:S(2)}) collective-permute-start(bf16[192,256]{1,0:T(8,128)(2,1)S(1)} %shard_map.86.both_ref), channel_id=1, source_target_pairs={{0,1},{1,0},{2,3},{3,2},{4,5},{5,4},{6,7},{7,6},{8,9},{9,8},{10,11... | collective-permute-start | bytes 294920 | tf_op jit(solution)/shard_map/ppermute | solution.py:473
  64.1 7.3 %collective-permute-start.20 = (bf16[192,256]{1,0:T(8,128)(2,1)S(1)}, bf16[192,256]{1,0:T(8,128)(2,1)S(1)}, u32[]{:S(2)}, u32[]{:S(2)}) collective-permute-start(bf16[192,256]{1,0:T(8,128)(2,1)S(1)} %get-tuple-element.53.pair_ref), channel_id=1, source_target_pairs={{0,12},{1,9},{2,14},{3,11},{4,20},{5,13},{6,22},{7,15},{8,24},{9,1... | collective-permute-start | bytes 294920 | tf_op jit(solution)/shard_map/ppermute | solution.py:448
  65.4 15.0 %collective-permute-start.19 = (bf16[192,256]{1,0:T(8,128)(2,1)S(1)}, bf16[192,256]{1,0:T(8,128)(2,1)S(1)}, u32[]{:S(2)}, u32[]{:S(2)}) collective-permute-start(bf16[192,256]{1,0:T(8,128)(2,1)S(1)} %get-tuple-element.53.pair_ref), channel_id=1, source_target_pairs={{0,20},{1,17},{2,22},{3,19},{4,16},{5,25},{6,18},{7,27},{8,28},{9,... | collective-permute-start | bytes 294920 | tf_op jit(solution)/shard_map/ppermute | solution.py:448
  68.9 11.5 %collective-permute-start.18 = (bf16[192,256]{1,0:T(8,128)(2,1)S(1)}, bf16[192,256]{1,0:T(8,128)(2,1)S(1)}, u32[]{:S(2)}, u32[]{:S(2)}) collective-permute-start(bf16[192,256]{1,0:T(8,128)(2,1)S(1)} %get-tuple-element.53.pair_ref), channel_id=1, source_target_pairs={{0,4},{1,25},{2,6},{3,27},{4,0},{5,29},{6,2},{7,31},{8,12},{9,17},... | collective-permute-start | bytes 294920 | tf_op jit(solution)/shard_map/ppermute | solution.py:448
  69.3 13.2 %collective-permute-start.17 = (bf16[352,256]{1,0:T(8,128)(2,1)S(1)}, bf16[352,256]{1,0:T(8,128)(2,1)S(1)}, u32[]{:S(2)}, u32[]{:S(2)}) collective-permute-start(bf16[352,256]{1,0:T(8,128)(2,1)S(1)} %get-tuple-element.52), channel_id=1, source_target_pairs={{0,28},{4,8},{8,4},{12,16},{16,12},{20,24},{24,20},{28,0},{1,29},{... | collective-permute-start | bytes 540680 | tf_op jit(solution)/shard_map/ppermute | solution.py:476
  80.4 3.0 %collective-permute-start.21 = (bf16[288,256]{1,0:T(8,128)(2,1)S(1)}, bf16[288,256]{1,0:T(8,128)(2,1)S(1)}, u32[]{:S(2)}, u32[]{:S(2)}) collective-permute-start(bf16[288,256]{1,0:T(8,128)(2,1)S(1)} %shard_map.88), channel_id=1, source_target_pairs={{0,1},{1,0},{2,3},{3,2},{4,5},{5,4},{6,7},{7,6},{8,9},{9,8},{10,11... | collective-permute-start | bytes 442376 | tf_op jit(solution)/shard_map/ppermute | solution.py:478

commit v4 on v3

--- a/solution.py
+++ b/solution.py
@@ -131,10 +131,11 @@
                 tile = quad_ref[k, b, jnp.maximum(entry - 1, 0)]
                 tiles.append(jnp.where(entry > 0, tile, empty))
             tiles += [empty] * (GRP - 1 - r)
-            row = k * GRP * BLK + r * BLK
+            half, rest = divmod(r * BLK, HALO * BLK)
+            row = (half * KB + k) * HALO * BLK + rest
             band_ref[g, row : row + BLK, :] = jnp.concatenate(tiles, axis=1)
-            if r == GRP - 1:
-                part = slice(k * GRP * BLK, (k + 1) * GRP * BLK)
+            if rest + BLK == HALO * BLK:
+                part = slice(row - rest, row + BLK)
                 flip_ref[g, :, part] = band_ref[g, part, :].T
 
 
@@ -161,70 +162,81 @@
     )(*(pltpu.with_memory_space_constraint(a, pltpu.HBM) for a in (block_index, block_mask, quad)))
 
 
-def hidden_kernel(x_ref, near_ref, far_ref, band_ref, w_ref, hid_ref, gp_ref, ext_ref, sems):
-    rows = x_ref.shape[2]
-    edge = HALO * BLK
-    odd = lax.axis_index("lat") % 2
-    ends = [pl.multiple_of(side * (edge + rows), edge) for side in (1 - odd, odd)]
-    copies = [
-        pltpu.make_async_copy(near_ref, ext_ref.at[:, pl.ds(ends[0], edge)], sems.at[0]),
-        pltpu.make_async_copy(x_ref.at[0], ext_ref.at[:, pl.ds(edge, rows)], sems.at[1]),
-        pltpu.make_async_copy(far_ref, ext_ref.at[:, pl.ds(ends[1], edge)], sems.at[2]),
-    ]
-    for c in copies:
-        c.start()
-    for c in copies:
-        c.wait()
-    size = GRP * BLK
+def hidden_kernel(inner, x_ref, band_ref, w_ref, *refs):
+    hid_ref, gp_ref = refs[-2:]
+    pair = HALO * BLK
+    deep = KB * pair
+    groups = band_ref.shape[0]
+    spots = [(g, h) for g in range(groups) for h in range(2)]
+    spots = spots[1:-1] if inner else [spots[0], spots[-1]]
+    odd = lax.axis_index("lat") % 2 == 1
+    parts = []
     for m in range(MB):
-        for g in range(rows // size):
-            window = ext_ref[m, g * size : g * size + SPAN * BLK, :]
-            hid = dot(band_ref[g], window).astype(BF)
-            hid_ref[m, g] = hid
-            z = dot(hid[:size], w_ref[0, 0])
-            for k in range(1, KB):
-                z += dot(hid[k * size : (k + 1) * size], w_ref[0, k])
-            gp_ref[m, g * size : (g + 1) * size, :] = gelu_slope(z)
-
-
-def hidden_call(x, near, far, band, weights):
+        for g, h in spots:
+            at = (2 * g + h - 1) * pair
+            if inner:
+                window = x_ref[0, m, at : at + 3 * pair, :]
+            elif g == 0:
+                rim = jnp.where(odd, refs[0][m], refs[1][m])
+                window = jnp.concatenate([rim, x_ref[0, m, : 2 * pair, :]], axis=0)
+            else:
+                rim = jnp.where(odd, refs[1][m], refs[0][m])
+                window = jnp.concatenate([x_ref[0, m, at:, :], rim], axis=0)
+            band = band_ref[g, h * deep : (h + 1) * deep, h * pair : h * pair + 3 * pair]
+            parts.append(dot(band, window).astype(BF))
+            hid_ref[m, g, h * deep : (h + 1) * deep, :] = parts[-1]
+    z = None
+    for k in range(KB):
+        rows = jnp.concatenate([p[k * pair : (k + 1) * pair] for p in parts], axis=0)
+        new = dot(rows, w_ref[0, k])
+        z = new if z is None else z + new
+    gp = gelu_slope(z)
+    for i, (m, g, h) in enumerate((m, g, h) for m in range(MB) for g, h in spots):
+        gp_ref[m, (2 * g + h) * pair : (2 * g + h + 1) * pair, :] = gp[i * pair : (i + 1) * pair]
+
+
+def hidden_call(x, band, weights, *rest):
     _, mb, rows, ch = x.shape
-    groups = band.shape[0]
+    args = (x, band, weights) + rest
     return pl.pallas_call(
-        hidden_kernel,
+        functools.partial(hidden_kernel, not rest),
         out_shape=(
-            pltpu.VMEM((mb, groups, KB * GRP * BLK, ch), BF),
+            pltpu.VMEM((mb, band.shape[0], KB * GRP * BLK, ch), BF),
             pltpu.VMEM((mb, rows, ch), F32),
         ),
-        in_specs=[ANY, ANY, ANY, VM, VM],
+        in_specs=[VM] * len(args),
         out_specs=(VM, VM),
-        scratch_shapes=[
-            pltpu.VMEM((mb, rows + 2 * HALO * BLK, ch), BF),
-            pltpu.SemaphoreType.DMA((3,)),
-        ],
+        input_output_aliases={5: 0, 6: 1} if rest else {},
         compiler_params=params(),
-        name="hidden",
-    )(x, near, far, band, weights)
-
-
-PARTS = {"edge": ("left", "right", "slope"), "bulk": ("out",), "whole": ("left", "right", "slope", "out")}
+        cost_estimate=None if rest else cost(1 << 30),
+        name="outer" if rest else "inner",
+    )(*args)
+
+
+PARTS = {
+    "edge": ("left", "right", "slope"),
+    "rims": ("left", "right", "slope", "done"),
+    "bulk": ("out",),
+    "whole": ("left", "right", "slope", "done", "out"),
+}
 
 
 def back_terms(slope, w_ref, stack_ref):
-    size = slope.shape[0]
+    pair = HALO * BLK
     for k in range(KB):
         back = lax.dot_general(
             slope, w_ref[0, k], (((1,), (1,)), ((), ())), preferred_element_type=F32
-        )
-        stack_ref[k * size : (k + 1) * size, :] = back.astype(BF)
+        ).astype(BF)
+        for h in range(slope.shape[0] // pair):
+            stack_ref[(h * KB + k) * pair : (h * KB + k + 1) * pair, :] = back[h * pair : (h + 1) * pair]
 
 
 def step_kernel(turn, lats, part, *refs):
     first = lats is None
     (main_ref, gp_ref, flip_ref, w_ref), rest = refs[:4], refs[4:]
     if not first:
-        (below_ref, above_ref), rest = rest[:2], rest[2 + len(PARTS[part]) :]
-    outs, (stack_ref, term_ref) = dict(zip(PARTS[part], rest)), rest[-2:]
+        below_ref, above_ref = rest[:2]
+    outs, (stack_ref, term_ref) = dict(zip(PARTS[part], rest[-2 - len(PARTS[part]) :])), rest[-2:]
     lat = lax.axis_index("lat")
     rows = gp_ref.shape[1]
     size = GRP * BLK
@@ -243,18 +255,16 @@
             parts[-1] += jnp.where(lat < lats - 1, above_ref[m].astype(F32), 0.0)
         return jnp.concatenate(parts, axis=0).astype(BF).astype(F32)
 
-    def edges(m):
-        for name, g, rim, at, low in (
-            ("left", 0, 0, 0, 0),
-            ("right", groups - 1, size + edge, rows - edge, size - edge),
-        ):
-            back_terms(outs["slope"][m, at : at + edge, :], w_ref, stack_ref)
-            term = None
-            for k in range(KB):
-                band = flip_ref[g, rim : rim + edge, k * size + low : k * size + low + edge]
-                new = dot(band, stack_ref[k * edge : (k + 1) * edge, :])
-                term = new if term is None else term + new
-            outs[name][m] = term.astype(BF)
+    def edges():
+        slope = outs["slope"]
+        rims = [slope[m, at : at + edge, :] for m in range(MB) for at in (0, rows - edge)]
+        back_terms(jnp.concatenate(rims, axis=0), w_ref, stack_ref)
+        deep = KB * edge
+        for m in range(MB):
+            low = stack_ref[2 * m * deep : (2 * m + 1) * deep, :]
+            outs["left"][m] = dot(flip_ref[0, :edge, :deep], low).astype(BF)
+            high = stack_ref[(2 * m + 1) * deep : (2 * m + 2) * deep, :]
+            outs["right"][m] = dot(flip_ref[groups - 1, size + edge :, deep:], high).astype(BF)
 
     @pl.when(lax.axis_index("section") == turn)
     def _():
@@ -267,10 +277,14 @@
                 else:
                     slope = (grad * gp_ref[m, at, :]).astype(BF)
                     outs["slope"][m, at, :] = slope
-                if part == "edge":
+                if "done" in outs and g == 0:
+                    outs["done"][m, :edge, :] = grad[:edge].astype(BF)
+                if "done" in outs and g == groups - 1:
+                    outs["done"][m, edge:, :] = grad[size - edge :].astype(BF)
+                if part in ("edge", "rims"):
                     continue
                 back_terms(slope, w_ref, stack_ref)
-                term = dot(flip_ref[g], stack_ref[...])
+                term = dot(flip_ref[g], stack_ref[: KB * size, :])
                 low = g * size
                 if g == 0:
                     if part == "whole":
@@ -286,27 +300,29 @@
                     term_ref[low + size + edge : low + size + lap, :] = term[size + edge :]
                 elif part == "whole":
                     outs["right"][m] = term[size + edge :].astype(BF)
-            if part == "edge":
-                edges(m)
-            else:
+            if "out" in outs:
                 outs["out"][m] = term_ref[edge : edge + rows, :].astype(BF)
+        if "out" not in outs:
+            edges()
 
 
 def step_call(turn, lats, part, main, factor, sides, flip, weights, state):
     mb, rows, ch = main.shape
     edge = HALO * BLK
     names = PARTS[part]
-    olds = tuple(state[name] for name in names) if sides else ()
-    args = (main, factor, flip, weights) + sides + olds
-    tall = {"left": edge, "right": edge, "slope": rows, "out": rows}
+    known = [name for name in names if name in state]
+    args = (main, factor, flip, weights) + sides + tuple(state[name] for name in known)
+    tall = {"left": edge, "right": edge, "slope": rows, "done": 2 * edge, "out": rows}
     outs = pl.pallas_call(
         functools.partial(step_kernel, turn, lats if sides else None, part),
         out_shape=tuple(pltpu.VMEM((mb, tall[name], ch), BF) for name in names),
         in_specs=[VM] * len(args),
         out_specs=(VM,) * len(names),
-        input_output_aliases={6 + i: i for i in range(len(olds))},
+        input_output_aliases={
+            len(args) - len(known) + i: names.index(name) for i, name in enumerate(known)
+        },
         scratch_shapes=[
-            pltpu.VMEM((KB * GRP * BLK, ch), BF),
+            pltpu.VMEM((KB * max(GRP * BLK, 2 * MB * edge), ch), BF),
             pltpu.VMEM((rows + 2 * edge, ch), F32),
         ],
         compiler_params=params(),
@@ -317,12 +333,14 @@
 
 def weight_terms(hid_ref, slope_ref, acc_ref):
     size = GRP * BLK
+    edge = HALO * BLK
     for k in range(KB):
         total = None
         for m in range(MB):
             for g in range(hid_ref.shape[1]):
+                pairs = [hid_ref[m, g, i * edge : (i + 1) * edge, :] for i in (k, KB + k)]
                 part = lax.dot_general(
-                    hid_ref[m, g, k * size : (k + 1) * size, :],
+                    jnp.concatenate(pairs, axis=0),
                     slope_ref[m, g * size : (g + 1) * size, :],
                     (((0,), (0,)), ((), ())),
                     preferred_element_type=F32,
@@ -349,11 +367,9 @@
     return jnp.where(second == own, ends[1], ends[0])
 
 
-def lay_edges(out_ref, skip, even_ref, odd_ref):
+def lay_edges(even_ref, odd_ref):
     odd = lax.axis_index("lat") % 2 == 1
-    edge = even_ref.shape[1]
-    for m in range(MB):
-        out_ref[skip + m * edge : skip + (m + 1) * edge, :] = jnp.where(odd, odd_ref[m], even_ref[m])
+    return jnp.concatenate([jnp.where(odd, odd_ref[m], even_ref[m]) for m in range(MB)], axis=0)
 
 
 def cut_kernel(way, ways, hid_ref, slope_ref, left_ref, right_ref, own_ref, ride_ref, keep_ref, give_ref, acc_ref):
@@ -365,38 +381,46 @@
         return acc_ref[pl.ds(pl.multiple_of(i * piece, piece), piece), :]
 
     own_ref[...] = cut(me)
-    ride_ref[:piece, :] = cut(partner_of(way, me)).astype(BF)
-    lay_edges(ride_ref, piece, right_ref, left_ref)
-    for j in range(len(ways) // 2):
+    ride_ref[...] = cut(partner_of(way, me)).astype(BF)
+    count = len(ways) // 2
+    for j in range(count):
         keep_ref[j * piece : (j + 1) * piece, :] = cut(shared(ways, j, True)).astype(BF)
         give_ref[j * piece : (j + 1) * piece, :] = cut(shared(ways, j, False)).astype(BF)
-
-
-def pack_kernel(keep_ref, got_ref, *out_refs):
-    piece = out_refs[0].shape[0] // 2
+    give_ref[count * piece :, :] = lay_edges(left_ref, right_ref)
+
+
+def pack_kernel(keep_ref, got_ref, left_ref, right_ref, *out_refs):
+    piece = out_refs[-1].shape[0] // 2
     for j, ref in enumerate(out_refs):
         ref[:piece, :] = keep_ref[j * piece : (j + 1) * piece, :]
-        ref[piece:, :] = got_ref[j * piece : (j + 1) * piece, :]
+        ref[piece : 2 * piece, :] = got_ref[j * piece : (j + 1) * piece, :]
+    second = lax.axis_index("section") % 2 == 1
+    rims = jnp.where(second, got_ref[len(out_refs) * piece :, :], lay_edges(right_ref, left_ref))
+    out_refs[0][2 * piece :, :] = rims
 
 
 def sum_kernel(own_ref, ride_ref, *refs):
     piece = own_ref.shape[0]
-    mine, theirs = own_ref[...] + ride_ref[:piece, :].astype(F32), 0.0
+    mine, theirs = own_ref[...] + ride_ref[...].astype(F32), 0.0
     for ref in refs[:-1]:
         mine += ref[:piece, :].astype(F32)
-        theirs += ref[piece:, :].astype(F32)
+        theirs += ref[piece : 2 * piece, :].astype(F32)
     refs[-1][:piece, :] = mine.astype(BF)
     refs[-1][piece:, :] = theirs.astype(BF)
 
 
-def final_kernel(both_ref, got_ref, left_ref, right_ref, pair_ref, ride_ref):
+def final_kernel(both_ref, got_ref, rims_ref, done_ref, pair_ref, ride_ref, aside_ref):
     piece = both_ref.shape[0] // 2
     mine = (both_ref[:piece, :].astype(F32) + got_ref[piece:, :].astype(F32)).astype(BF)
     theirs = (both_ref[piece:, :].astype(F32) + got_ref[:piece, :].astype(F32)).astype(BF)
     pair_ref[:piece, :] = mine
     pair_ref[piece:, :] = theirs
-    ride_ref[:piece, :] = mine
-    lay_edges(ride_ref, piece, left_ref, right_ref)
+    ride_ref[...] = mine
+    edges = rims_ref.shape[0] - 2 * piece
+    aside_ref[:edges, :] = rims_ref[2 * piece :, :]
+    rows = done_ref.shape[1]
+    for m in range(MB):
+        aside_ref[edges + m * rows : edges + (m + 1) * rows, :] = done_ref[m]
 
 
 def split_kernel(*refs):
@@ -414,7 +438,7 @@
         weight_ref[pl.ds(pl.multiple_of(i * piece, piece), piece), :] = value.astype(F32)
 
     place(me, pair_ref[:piece, :])
-    place(partner_of(way, me), ride_ref[:piece, :])
+    place(partner_of(way, me), ride_ref[...])
     for j, ref in enumerate(met):
         place(shared(ways, j, True), ref[:piece, :])
         place(shared(ways, j, False), got_ref[j * piece : (j + 1) * piece, :])
@@ -431,60 +455,64 @@
     )(*args)
 
 
-def reduce_weight(lats, sections, hid, slope, left, right):
+def reduce_weight(lats, sections, hid, state):
+    left, right, slope, done = (state[name] for name in PARTS["rims"])
     ch = slope.shape[2]
-    ways = matchings(lats)
-    first, second = ways[1:], ways[:1] + ways[2:]
-    count = len(first) // 2
+    near, far, way, *others = matchings(lats)
+    ways = [near, far] + others
+    count = len(ways) // 2
     piece = KB * ch // lats
-    ride = piece + MB * left.shape[1]
+    edges = MB * left.shape[1]
     swap = [(s, s ^ 1) for s in range(sections)]
 
     def vmem(rows, dtype=BF):
         return pltpu.VMEM((rows, ch), dtype)
 
-    def meet(arrays, ways):
-        return [
-            lax.ppermute(
-                a,
-                ("lat", "section"),
-                [
-                    (i * sections + s, ways[2 * j + s % 2][i] * sections + s)
-                    for i in range(lats)
-                    for s in range(sections)
-                ],
-            )
-            for j, a in enumerate(arrays)
-        ]
+    def meet(arrays):
+        got = []
+        for j, a in enumerate(arrays):
+            pairs = [
+                (i * sections + s, ways[2 * j + s % 2][i] * sections + s)
+                for i in range(lats)
+                for s in range(sections)
+            ]
+            got.append(lax.ppermute(a, ("lat", "section"), pairs))
+        return got
 
     own, out, keep, give = small_call(
-        functools.partial(cut_kernel, ways[0], first),
-        (vmem(piece, F32), vmem(ride), vmem(count * piece), vmem(count * piece)),
+        functools.partial(cut_kernel, way, ways),
+        (vmem(piece, F32), vmem(piece), vmem(count * piece), vmem(count * piece + edges)),
         hid,
         slope,
         left,
         right,
         scratch=(vmem(KB * ch, F32),),
     )
+    straight = list(enumerate(way))
+    ride = lax.ppermute(out, "lat", straight)
     got = lax.ppermute(give, "section", swap)
-    near = lax.ppermute(out, "lat", list(enumerate(ways[0])))
-    packs = small_call(pack_kernel, (vmem(2 * piece),) * count, keep, got)
-    (both,) = small_call(sum_kernel, (vmem(2 * piece),), own, near, *meet(packs, first))
+    shapes = [vmem(2 * piece + (0 if j else edges)) for j in range(count)]
+    packs = small_call(pack_kernel, shapes, keep, got, left, right)
+    met = meet(packs)
+    rims = met[0]
+    (both,) = small_call(sum_kernel, (vmem(2 * piece),), own, ride, *met)
     got = lax.ppermute(both, "section", swap)
-    pair, out = small_call(final_kernel, (vmem(2 * piece), vmem(ride)), both, got, left, right)
-    met = meet([pair] * count, second)
-    far = lax.ppermute(out, "lat", list(enumerate(ways[1])))
+    shapes = (vmem(2 * piece), vmem(piece), vmem(edges + MB * done.shape[1]))
+    pair, out, aside = small_call(final_kernel, shapes, both, got, rims, done)
+    met = meet([pair] * count)
+    ride = lax.ppermute(out, "lat", straight)
+    aside = lax.ppermute(aside, "section", swap)
     (give,) = small_call(split_kernel, (vmem(count * piece),), *met)
     got = lax.ppermute(give, "section", swap)
     (weight,) = small_call(
-        functools.partial(join_kernel, ways[1], second),
+        functools.partial(join_kernel, way, ways),
         (jax.ShapeDtypeStruct((KB * ch, ch), F32),),
         pair,
-        far,
+        ride,
         got,
         *met,
     )
-    return weight, near, far, piece
+    return weight, rims, aside, 2 * piece
 
 
 def grad_kernel(lats, skip, main_ref, near_ref, far_ref, grad_ref):
@@ -492,14 +520,22 @@
     edge = HALO * BLK
     me = lax.axis_index("lat")
     odd = me % 2 == 1
+    behind = far_ref.shape[0] > MB * edge
+    finished = jnp.logical_and(lax.axis_index("section") % 2 == 1, behind)
     for m in range(MB):
-        at = slice(skip + m * edge, skip + (m + 1) * edge)
-        near, far = near_ref[at, :].astype(F32), far_ref[at, :].astype(F32)
+        near = near_ref[skip + m * edge : skip + (m + 1) * edge, :].astype(F32)
+        far = far_ref[m * edge : (m + 1) * edge, :].astype(F32)
         below = jnp.where(me > 0, jnp.where(odd, near, far), 0.0)
         above = jnp.where(me < lats - 1, jnp.where(odd, far, near), 0.0)
-        grad_ref[0, m, :edge, :] = (main_ref[m, :edge, :].astype(F32) + below).astype(BF)
+        low = (main_ref[m, :edge, :].astype(F32) + below).astype(BF)
+        high = (main_ref[m, rows - edge :, :].astype(F32) + above).astype(BF)
+        if behind:
+            at = (MB + 2 * m) * edge
+            low = jnp.where(finished, far_ref[at : at + edge, :], low)
+            high = jnp.where(finished, far_ref[at + edge : at + 2 * edge, :], high)
+        grad_ref[0, m, :edge, :] = low
         grad_ref[0, m, edge : rows - edge, :] = main_ref[m, edge : rows - edge, :]
-        grad_ref[0, m, rows - edge :, :] = (main_ref[m, rows - edge :, :].astype(F32) + above).astype(BF)
+        grad_ref[0, m, rows - edge :, :] = high
 
 
 def grad_call(lats, skip, main, near, far):
@@ -528,12 +564,13 @@
     far = lax.ppermute(rim(odd), both, sides[1])
     near = lax.ppermute(rim(1 - odd), both, sides[0])
     band, flip = band_call(block_index, block_mask, quad_values)
-    hid, gp = hidden_call(saved_input, near, far, band, weights)
+    hid, gp = hidden_call(saved_input, band, weights)
+    hid, gp = hidden_call(saved_input, band, weights, near, far, hid, gp)
 
     state, main, terms = {}, cotangent, ()
     for turn in reversed(range(sections)):
         if turn % 2 or turn == 0:
-            step_call(turn, lats, "edge", main, gp, terms, flip, weights, state)
+            step_call(turn, lats, "edge" if turn else "rims", main, gp, terms, flip, weights, state)
             step_call(turn, lats, "bulk", main, state["slope"], terms, flip, weights, state)
         else:
             step_call(turn, lats, "whole", main, gp, terms, flip, weights, state)
@@ -546,13 +583,13 @@
     left, right, slope = (state[name] for name in PARTS["edge"])
     channels = saved_input.shape[3]
     if lats == 8 and sections % 2 == 0:
-        weight, near, far, skip = reduce_weight(lats, sections, hid, slope, left, right)
+        weight, near, far, skip = reduce_weight(lats, sections, hid, state)
+        grad = grad_call(lats, skip, state["out"], near, far)
     else:
         give = jnp.where(odd == 1, left, right), jnp.where(odd == 1, right, left)
         near, far = (lax.ppermute(g, both, p).reshape(-1, channels) for g, p in zip(give, sides))
-        skip = 0
         weight = lax.psum(weight_call(hid, slope), "lat")
-    grad = grad_call(lats, skip, state["out"], near, far)
+        grad = grad_call(lats, 0, state["out"], near, far)
     return grad, weight.reshape(1, KB, channels, channels)
 
 

time: 84.5 us -> 82.2 us (0.973)
  Pallas kernels: 11 us -> 9.73 us
  starting transfers between devices: 36.5 us -> 35.5 us
    ppermute x2, waiting for transfers between devices: 0.3 us -> 1.55 us  [reduce_weight(): got = lax.ppermute(give, 'section', swap)]
    ppermute x1, waiting for transfers between devices: 2.72 us -> 1.58 us  [per_device(): near = lax.ppermute(rim(1 - odd), both, sides[0])]
    ppermute x3, starting transfers between devices: 8.86 us -> 7.84 us  [per_device(): main = lax.ppermute(state['out'], 'section', hop_pairs(sections, turn))]
    pallas_call x1 -> x2, Pallas kernels: 2.78 us -> 1.85 us  [hidden_call(): pl.pallas_call(functools.partial(hidden_kernel, not rest), out_shape=(plt...]
    ppermute x8 -> x9, starting transfers between devices: 14.7 us -> 15.5 us  [the longest x6 10.2 us: meet(): got.append(lax.ppermute(a, ('lat', 'section'), pairs))]
    ppermute x8 -> x9, waiting for transfers between devices: 14.3 us -> 13.7 us  [the longest x2 7.54 us: reduce_weight(): ride = lax.ppermute(out, 'lat', straight)]
  transfers between devices with their start and end apart: 22 -> 23, of which waited for: 11 -> 12; matrix products, arithmetic and copies ran while one was open for 0% -> 0% of each run, Pallas kernels for 6% -> 8%
where the time goes in v4:
time: 82.2 us; the launch traced here: 81.9 us
  starting transfers between devices  35.5 us (43%)
  waiting for transfers between devices  34.7 us (42%)
  Pallas kernels  9.73 us (12%)
  local copies, waits for them, and re-layouts  1.18 us (1%)
  between operations  0.84 us (1%)
    ppermute x6, starting transfers between devices, meet(): got.append(lax.ppermute(a, ('lat', 'section'), pairs))  10.2 us
    ppermute x3, starting transfers between devices, per_device(): main = lax.ppermute(state['out'], 'section', hop_pairs(sections, turn))  7.84 us
    ppermute x2, waiting for transfers between devices, reduce_weight(): ride = lax.ppermute(out, 'lat', straight)  7.54 us
    ppermute x6, waiting for transfers between devices, meet(): got.append(lax.ppermute(a, ('lat', 'section'), pairs))  6.12 us
    ppermute x3, waiting for transfers between devices, per_device(): lax.ppermute(state['right'], both, slant_pairs(lats, sections, turn, True))  5.74 us
    ppermute x3, waiting for transfers between devices, per_device(): lax.ppermute(state['left'], both, slant_pairs(lats, sections, turn, False))  5.59 us
    ppermute x3, waiting for transfers between devices, per_device(): main = lax.ppermute(state['out'], 'section', hop_pairs(sections, turn))  5.34 us
    ppermute x2, starting transfers between devices, reduce_weight(): ride = lax.ppermute(out, 'lat', straight)  5.07 us
  transfers between devices with their start and end apart: 23, of which 12 were waited for; matrix products, arithmetic and copies ran while one was open for 0% of the time, Pallas kernels for 8%

profile of v4, /device:TPU:0, one launch (start us, length us, event | category | flops | bytes accessed | tf_op | source)
XLA Modules:
  0.0 81.9 jit_solution(12995507480251491805)
XLA Ops:
  0.6 0.0 copy-start.1
  0.6 0.0 copy-start
  0.7 1.1 %dynamic-slice_bitcast_fusion = (bf16[2,128,256]{2,1,0:T(8,128)(2,1)S(1)}, bf16[2,128,256]{2,1,0:T(8,128)(2,1)S(1)}) fusion(bf16[1,2,512,256]{3,2,1,0:T(8,128)(2,1)} %x_ref.3, s32[]{:T(128)S(6)} %select_n.15, s32[]{:T(128)S(6)} %select_n.14), kind=kLoop, calls=%fused_computation | loop fusion | bytes 524296 | tf_op jit(solution)/shard_map/dynamic_slice | solution.py:562
  1.7 0.6 collective-permute-start.1
  2.3 4.0 %collective-permute-start = (bf16[2,128,256]{2,1,0:T(8,128)(2,1)S(1)}, bf16[2,128,256]{2,1,0:T(8,128)(2,1)S(1)}, u32[]{:S(2)}, u32[]{:S(2)}) collective-permute-start(bf16[2,128,256]{2,1,0:T(8,128)(2,1)S(1)} %get-tuple-element.65), channel_id=1, source_target_pairs={{0,4},{1,5},{2,6},{3,7},{4,0},{5,1},{6,2},{7,3},{8,12},{9,13},{10,... | collective-permute-start | bytes 393224 | tf_op jit(solution)/shard_map/ppermute | solution.py:565
  6.3 2.4 %band.1 = (bf16[2,768,512]{2,1,0:T(8,128)(2,1)S(1)}, bf16[2,512,768]{2,1,0:T(8,128)(2,1)S(1)}) custom-call(s32[8,5]{1,0:T(8,128)} %index_in.1, s32[8,5]{1,0:T(8,128)} %mask_in.1, bf16[3,8,5,64,64]{4,3,2,1,0:T(8,128)(2,1)} %quad_in.1), custom_call_target="tpu_custom_call" | custom-call | tf_op jit(solution)/shard_map/band/pallas_call | solution.py:145
  8.7 0.0 copy-done.1
  8.7 0.0 copy-done
  8.7 0.9 %inner.1 = (bf16[2,2,768,256]{3,2,1,0:T(8,128)(2,1)S(1)}, f32[2,512,256]{2,1,0:T(8,128)S(1)}) custom-call(bf16[1,2,512,256]{3,2,1,0:T(8,128)(2,1)S(1)} %copy-done.1, bf16[2,768,512]{2,1,0:T(8,128)(2,1)S(1)} %get-tuple-element.33.band_ref, bf16[1,3,256,256]{3,2,1,0:T(8,128)(2,1)S(1)} %copy-done), custom_call_target="tpu_custom_call" | custom-call | flops 1073741824 | bytes 4194304 | tf_op jit(solution)/shard_map/inner/pallas_call | solution.py:201
  9.6 0.0 collective-permute-done.1.refs_1_
  9.7 1.6 %collective-permute-done.refs_0_ = bf16[2,128,256]{2,1,0:T(8,128)(2,1)S(1)} collective-permute-done((bf16[2,128,256]{2,1,0:T(8,128)(2,1)S(1)}, bf16[2,128,256]{2,1,0:T(8,128)(2,1)S(1)}, u32[]{:S(2)}, u32[]{:S(2)}) %collective-permute-start) | collective-permute-done | bytes 131104 | tf_op jit(solution)/shard_map/ppermute | solution.py:565
  11.2 0.0 copy-start.2
  11.2 0.9 %outer.1 = (bf16[2,2,768,256]{3,2,1,0:T(8,128)(2,1)S(1)}, f32[2,512,256]{2,1,0:T(8,128)S(1)}) custom-call(bf16[1,2,512,256]{3,2,1,0:T(8,128)(2,1)S(1)} %copy-done.1, bf16[2,768,512]{2,1,0:T(8,128)(2,1)S(1)} %get-tuple-element.33.band_ref, bf16[1,3,256,256]{3,2,1,0:T(8,128)(2,1)S(1)} %copy-done, ...), custom_call_target="tpu_custom_call", output_to_operand_aliasing={{0}: (5, {}), {1}: (6, {})} | custom-call | tf_op jit(solution)/shard_map/outer/pallas_call | solution.py:201
  12.2 0.1 copy-done.2
  12.3 0.0 collective-permute-start.2
  12.3 2.5 %collective-permute-start.3 = (bf16[2,128,256]{2,1,0:T(8,128)(2,1)S(1)}, bf16[2,128,256]{2,1,0:T(8,128)(2,1)S(1)}, u32[]{:S(2)}, u32[]{:S(2)}) collective-permute-start(bf16[2,128,256]{2,1,0:T(8,128)(2,1)S(1)} %get-tuple-element.39.refs_7_), channel_id=1, source_target_pairs={{3,6},{7,10},{11,14},{15,18},{19,22},{23,26},{27,30},{31,29},{5,1}... | collective-permute-start | bytes 393224 | tf_op jit(solution)/shard_map/ppermute | solution.py:578
  14.8 0.1 collective-permute-start.4
  14.9 4.8 %collective-permute-done.3.refs_4_ = bf16[2,128,256]{2,1,0:T(8,128)(2,1)S(1)} collective-permute-done((bf16[2,128,256]{2,1,0:T(8,128)(2,1)S(1)}, bf16[2,128,256]{2,1,0:T(8,128)(2,1)S(1)}, u32[]{:S(2)}, u32[]{:S(2)}) %collective-permute-start.3) | collective-permute-done | bytes 131104 | tf_op jit(solution)/shard_map/ppermute | solution.py:578
  19.7 1.9 %collective-permute-done.4.refs_5_ = bf16[2,128,256]{2,1,0:T(8,128)(2,1)S(1)} collective-permute-done((bf16[2,128,256]{2,1,0:T(8,128)(2,1)S(1)}, bf16[2,128,256]{2,1,0:T(8,128)(2,1)S(1)}, u32[]{:S(2)}, u32[]{:S(2)}) %collective-permute-start.4) | collective-permute-done | bytes 131104 | tf_op jit(solution)/shard_map/ppermute | solution.py:579
  21.5 0.0 collective-permute-done.2.refs_0_
  21.5 0.5 collective-permute-start.5
  22.1 0.7 collective-permute-start.6
  22.7 0.7 collective-permute-start.7
  23.4 0.0 collective-permute-done.6.refs_4_
  23.4 0.0 collective-permute-done.7.refs_5_
  23.4 5.3 %collective-permute-done.5.refs_0_ = bf16[2,512,256]{2,1,0:T(8,128)(2,1)S(1)} collective-permute-done((bf16[2,512,256]{2,1,0:T(8,128)(2,1)S(1)}, bf16[2,512,256]{2,1,0:T(8,128)(2,1)S(1)}, u32[]{:S(2)}, u32[]{:S(2)}) %collective-permute-start.5) | collective-permute-done | bytes 524320 | tf_op jit(solution)/shard_map/ppermute | solution.py:580
  28.8 7.3 %collective-permute-start.8 = (bf16[2,512,256]{2,1,0:T(8,128)(2,1)S(1)}, bf16[2,512,256]{2,1,0:T(8,128)(2,1)S(1)}, u32[]{:S(2)}, u32[]{:S(2)}) collective-permute-start(bf16[2,512,256]{2,1,0:T(8,128)(2,1)S(1)} %shard_map.81.refs_6_), channel_id=1, source_target_pairs={{0,1},{1,0},{2,3},{3,2},{4,5},{5,4},{6,7},{7,6},{8,9},{9,8},{10,11... | collective-permute-start | bytes 1572872 | tf_op jit(solution)/shard_map/ppermute | solution.py:580
  36.1 0.1 collective-permute-start.9
  36.1 3.3 %collective-permute-start.10 = (bf16[2,128,256]{2,1,0:T(8,128)(2,1)S(1)}, bf16[2,128,256]{2,1,0:T(8,128)(2,1)S(1)}, u32[]{:S(2)}, u32[]{:S(2)}) collective-permute-start(bf16[2,128,256]{2,1,0:T(8,128)(2,1)S(1)} %get-tuple-element.47.refs_6_), channel_id=1, source_target_pairs={{29,24},{25,20},{21,16},{17,12},{13,8},{9,4},{5,0},{1,3},{27,31},{... | collective-permute-start | bytes 393224 | tf_op jit(solution)/shard_map/ppermute | solution.py:579
  39.5 1.0 %collective-permute-done.9.refs_4_ = bf16[2,128,256]{2,1,0:T(8,128)(2,1)S(1)} collective-permute-done((bf16[2,128,256]{2,1,0:T(8,128)(2,1)S(1)}, bf16[2,128,256]{2,1,0:T(8,128)(2,1)S(1)}, u32[]{:S(2)}, u32[]{:S(2)}) %collective-permute-start.9) | collective-permute-done | bytes 131104 | tf_op jit(solution)/shard_map/ppermute | solution.py:578
  40.4 3.7 %collective-permute-done.10.refs_5_ = bf16[2,128,256]{2,1,0:T(8,128)(2,1)S(1)} collective-permute-done((bf16[2,128,256]{2,1,0:T(8,128)(2,1)S(1)}, bf16[2,128,256]{2,1,0:T(8,128)(2,1)S(1)}, u32[]{:S(2)}, u32[]{:S(2)}) %collective-permute-start.10) | collective-permute-done | bytes 131104 | tf_op jit(solution)/shard_map/ppermute | solution.py:579
  44.2 0.0 collective-permute-done.8.refs_0_
  44.2 0.9 %shard_map.82 = (bf16[2,128,256]{2,1,0:T(8,128)(2,1)S(1)}, bf16[2,128,256]{2,1,0:T(8,128)(2,1)S(1)}, bf16[2,512,256]{2,1,0:T(8,128)(2,1)S(1)}, bf16[2,256,256]{2,1,0:T(8,128)(2,1)S(1)}) custom-call(bf16[2,512,256]{2,1,0:T(8,128)(2,1)S(1)} %collective-permute-done.8.refs_0_, ...), custom_call_target="tpu_custom_call", output_to_operand_aliasing={{0}: (6, {}), {1}: (7, {}), {2}: (8, {}), {3}: (9, {})} | custom-call | tf_op jit(solution)/shard_map/pallas_call | solution.py:316
  45.0 0.7 shard_map.84
  45.7 0.1 collective-permute-start.11
  45.8 1.5 %collective-permute-done.11.got_ref = bf16[544,256]{1,0:T(8,128)(2,1)S(1)} collective-permute-done((bf16[544,256]{1,0:T(8,128)(2,1)S(1)}, bf16[544,256]{1,0:T(8,128)(2,1)S(1)}, u32[]{:S(2)}, u32[]{:S(2)}) %collective-permute-start.11) | collective-permute-done | bytes 278560 | tf_op jit(solution)/shard_map/ppermute | solution.py:493
  47.4 1.1 %collective-permute-start.12 = (bf16[448,256]{1,0:T(8,128)(2,1)S(1)}, bf16[448,256]{1,0:T(8,128)(2,1)S(1)}, u32[]{:S(2)}, u32[]{:S(2)}) collective-permute-start(bf16[448,256]{1,0:T(8,128)(2,1)S(1)} %get-tuple-element.55), channel_id=1, source_target_pairs={{0,4},{1,29},{2,6},{3,31},{4,0},{5,9},{6,2},{7,11},{8,12},{9,5},{1... | collective-permute-start | bytes 688136 | tf_op jit(solution)/shard_map/ppermute | solution.py:479
  48.4 3.6 %collective-permute-start.14 = (bf16[192,256]{1,0:T(8,128)(2,1)S(1)}, bf16[192,256]{1,0:T(8,128)(2,1)S(1)}, u32[]{:S(2)}, u32[]{:S(2)}) collective-permute-start(bf16[192,256]{1,0:T(8,128)(2,1)S(1)} %get-tuple-element.58), channel_id=1, source_target_pairs={{0,20},{1,17},{2,22},{3,19},{4,16},{5,25},{6,18},{7,27},{8,28},{9,... | collective-permute-start | bytes 294920 | tf_op jit(solution)/shard_map/ppermute | solution.py:479
  52.1 0.1 collective-permute-start.15
  52.2 2.8 %collective-permute-start.13 = (bf16[96,256]{1,0:T(8,128)(2,1)S(1)}, bf16[96,256]{1,0:T(8,128)(2,1)S(1)}, u32[]{:S(2)}, u32[]{:S(2)}) collective-permute-start(bf16[96,256]{1,0:T(8,128)(2,1)S(1)} %get-tuple-element.57), channel_id=1, source_target_pairs={{0,24},{4,28},{8,16},{12,20},{16,8},{20,12},{24,0},{28,4},{1,25},{... | collective-permute-start | bytes 147464 | tf_op jit(solution)/shard_map/ppermute | solution.py:492
  55.1 5.8 %collective-permute-done.13.ride_ref = bf16[96,256]{1,0:T(8,128)(2,1)S(1)} collective-permute-done((bf16[96,256]{1,0:T(8,128)(2,1)S(1)}, bf16[96,256]{1,0:T(8,128)(2,1)S(1)}, u32[]{:S(2)}, u32[]{:S(2)}) %collective-permute-start.13) | collective-permute-done | bytes 49184 | tf_op jit(solution)/shard_map/ppermute | solution.py:492
  60.8 0.0 collective-permute-done.14.refs_1_
  60.8 0.0 collective-permute-done.15.refs_2_
  60.8 0.0 collective-permute-done.12.refs_0_.rims_ref.near_ref
  60.8 0.1 shard_map.86.both_ref
  60.9 0.2 collective-permute-start.16
  61.1 1.2 %collective-permute-done.16.got_ref = bf16[192,256]{1,0:T(8,128)(2,1)S(1)} collective-permute-done((bf16[192,256]{1,0:T(8,128)(2,1)S(1)}, bf16[192,256]{1,0:T(8,128)(2,1)S(1)}, u32[]{:S(2)}, u32[]{:S(2)}) %collective-permute-start.16) | collective-permute-done | bytes 98336 | tf_op jit(solution)/shard_map/ppermute | solution.py:499
  62.3 0.2 collective-permute-start.17
  62.5 2.5 %collective-permute-start.21 = (bf16[192,256]{1,0:T(8,128)(2,1)S(1)}, bf16[192,256]{1,0:T(8,128)(2,1)S(1)}, u32[]{:S(2)}, u32[]{:S(2)}) collective-permute-start(bf16[192,256]{1,0:T(8,128)(2,1)S(1)} %get-tuple-element.62.pair_ref), channel_id=1, source_target_pairs={{0,12},{1,9},{2,14},{3,11},{4,20},{5,13},{6,22},{7,15},{8,24},{9,1... | collective-permute-start | bytes 294920 | tf_op jit(solution)/shard_map/ppermute | solution.py:479
  65.0 1.8 %collective-permute-start.20 = (bf16[192,256]{1,0:T(8,128)(2,1)S(1)}, bf16[192,256]{1,0:T(8,128)(2,1)S(1)}, u32[]{:S(2)}, u32[]{:S(2)}) collective-permute-start(bf16[192,256]{1,0:T(8,128)(2,1)S(1)} %get-tuple-element.62.pair_ref), channel_id=1, source_target_pairs={{0,20},{1,17},{2,22},{3,19},{4,16},{5,25},{6,18},{7,27},{8,28},{9,... | collective-permute-start | bytes 294920 | tf_op jit(solution)/shard_map/ppermute | solution.py:479
  66.8 1.1 %collective-permute-start.19 = (bf16[192,256]{1,0:T(8,128)(2,1)S(1)}, bf16[192,256]{1,0:T(8,128)(2,1)S(1)}, u32[]{:S(2)}, u32[]{:S(2)}) collective-permute-start(bf16[192,256]{1,0:T(8,128)(2,1)S(1)} %get-tuple-element.62.pair_ref), channel_id=1, source_target_pairs={{0,4},{1,29},{2,6},{3,31},{4,0},{5,9},{6,2},{7,11},{8,12},{9,5},{1... | collective-permute-start | bytes 294920 | tf_op jit(solution)/shard_map/ppermute | solution.py:479
  67.9 2.1 %collective-permute-done.21.refs_2_ = bf16[192,256]{1,0:T(8,128)(2,1)S(1)} collective-permute-done((bf16[192,256]{1,0:T(8,128)(2,1)S(1)}, bf16[192,256]{1,0:T(8,128)(2,1)S(1)}, u32[]{:S(2)}, u32[]{:S(2)}) %collective-permute-start.21) | collective-permute-done | bytes 98336 | tf_op jit(solution)/shard_map/ppermute | solution.py:479
  70.0 4.0 %collective-permute-done.20.refs_1_ = bf16[192,256]{1,0:T(8,128)(2,1)S(1)} collective-permute-done((bf16[192,256]{1,0:T(8,128)(2,1)S(1)}, bf16[192,256]{1,0:T(8,128)(2,1)S(1)}, u32[]{:S(2)}, u32[]{:S(2)}) %collective-permute-start.20) | collective-permute-done | bytes 98336 | tf_op jit(solution)/shard_map/ppermute | solution.py:479
  74.0 0.0 collective-permute-done.19.refs_0_
  74.0 0.1 collective-permute-start.22
  74.1 2.2 %collective-permute-start.18 = (bf16[96,256]{1,0:T(8,128)(2,1)S(1)}, bf16[96,256]{1,0:T(8,128)(2,1)S(1)}, u32[]{:S(2)}, u32[]{:S(2)}) collective-permute-start(bf16[96,256]{1,0:T(8,128)(2,1)S(1)} %get-tuple-element.63), channel_id=1, source_target_pairs={{0,24},{4,28},{8,16},{12,20},{16,8},{20,12},{24,0},{28,4},{1,25},{... | collective-permute-start | bytes 147464 | tf_op jit(solution)/shard_map/ppermute | solution.py:503
  76.3 1.9 %shard_map.83.main_ref = bf16[2,512,256]{2,1,0:T(8,128)(2,1)S(1)} custom-call(bf16[2,512,256]{2,1,0:T(8,128)(2,1)S(1)} %collective-permute-done.8.refs_0_, bf16[2,512,256]{2,1,0:T(8,128)(2,1)S(1)} %get-tuple-element.49.refs_1_.slope_ref, bf16[2,512,768]{2,1,0:T(8,128)(2,1)S(1)} %get-tuple-element.37.refs_2_, ...), custom_call_target="tpu_custom_call", output_to_operand_aliasing={{}: (6, {})} | custom-call | flops 1207959552 | bytes 4718592 | tf_op jit(solution)/shard_map/pallas_call | solution.py:316
  78.3 1.8 %collective-permute-done.18.ride_ref = bf16[96,256]{1,0:T(8,128)(2,1)S(1)} collective-permute-done((bf16[96,256]{1,0:T(8,128)(2,1)S(1)}, bf16[96,256]{1,0:T(8,128)(2,1)S(1)}, u32[]{:S(2)}, u32[]{:S(2)}) %collective-permute-start.18) | collective-permute-done | bytes 49184 | tf_op jit(solution)/shard_map/ppermute | solution.py:503
  80.0 0.0 collective-permute-done.22.got_ref
  80.0 1.0 %shard_map.89 = f32[768,256]{1,0:T(8,128)} custom-call(bf16[192,256]{1,0:T(8,128)(2,1)S(1)} %get-tuple-element.62.pair_ref, bf16[96,256]{1,0:T(8,128)(2,1)S(1)} %collective-permute-done.18.ride_ref, bf16[288,256]{1,0:T(8,128)(2,1)S(1)} %collective-permute-done.22.got_ref, bf16[192,256]{1,0:T(8,128)(2,1)S(1)} %collective-permute-done.19.refs_0_, ...), custom_call_target="tpu_custom_call" | custom-call | tf_op jit(solution)/shard_map/pallas_call | solution.py:448
  81.0 0.0 collective-permute-done.17.far_ref
  81.0 0.9 %grad.1 = bf16[1,2,512,256]{3,2,1,0:T(8,128)(2,1)} custom-call(bf16[2,512,256]{2,1,0:T(8,128)(2,1)S(1)} %shard_map.83.main_ref, bf16[448,256]{1,0:T(8,128)(2,1)S(1)} %collective-permute-done.12.refs_0_.rims_ref.near_ref, bf16[768,256]{1,0:T(8,128)(2,1)S(1)} %collective-permute-done.17.far_ref), custom_call_target="tpu_custom_call" | custom-call | tf_op jit(solution)/shard_map/grad/pallas_call | solution.py:542
  (8 shorter events, 0.1 us)
Async XLA Ops:
  0.6 8.1 %copy-start.1 = (bf16[1,2,512,256]{3,2,1,0:T(8,128)(2,1)S(1)}, bf16[1,2,512,256]{3,2,1,0:T(8,128)(2,1)}, u32[]{:S(2)}) copy-start(bf16[1,2,512,256]{3,2,1,0:T(8,128)(2,1)} %x_ref.3) | copy-start | bytes 1572868
  0.6 8.1 %copy-start = (bf16[1,3,256,256]{3,2,1,0:T(8,128)(2,1)S(1)}, bf16[1,3,256,256]{3,2,1,0:T(8,128)(2,1)}, u32[]{:S(2)}) copy-start(bf16[1,3,256,256]{3,2,1,0:T(8,128)(2,1)} %refs_3_.13) | copy-start | bytes 1179652
  1.7 7.9 %collective-permute-start.1 = (bf16[2,128,256]{2,1,0:T(8,128)(2,1)S(1)}, bf16[2,128,256]{2,1,0:T(8,128)(2,1)S(1)}, u32[]{:S(2)}, u32[]{:S(2)}) collective-permute-start(bf16[2,128,256]{2,1,0:T(8,128)(2,1)S(1)} %get-tuple-element.64), channel_id=1, source_target_pairs={{0,1},{1,0},{2,3},{3,2},{4,8},{5,9},{6,10},{7,11},{8,4},{9,5},{10,... | collective-permute-start | bytes 393224 | tf_op jit(solution)/shard_map/ppermute | solution.py:564
  2.3 8.9 %collective-permute-start = (bf16[2,128,256]{2,1,0:T(8,128)(2,1)S(1)}, bf16[2,128,256]{2,1,0:T(8,128)(2,1)S(1)}, u32[]{:S(2)}, u32[]{:S(2)}) collective-permute-start(bf16[2,128,256]{2,1,0:T(8,128)(2,1)S(1)} %get-tuple-element.65), channel_id=1, source_target_pairs={{0,4},{1,5},{2,6},{3,7},{4,0},{5,1},{6,2},{7,3},{8,12},{9,13},{10,... | collective-permute-start | bytes 393224 | tf_op jit(solution)/shard_map/ppermute | solution.py:565
  11.2 1.0 %copy-start.2 = (bf16[2,512,256]{2,1,0:T(8,128)(2,1)S(1)}, bf16[2,512,256]{2,1,0:T(8,128)(2,1)}, u32[]{:S(2)}) copy-start(bf16[2,512,256]{2,1,0:T(8,128)(2,1)} %refs_0_.3) | copy-start | bytes 1572868
  12.3 9.3 %collective-permute-start.2 = (bf16[2,512,256]{2,1,0:T(8,128)(2,1)S(1)}, bf16[2,512,256]{2,1,0:T(8,128)(2,1)S(1)}, u32[]{:S(2)}, u32[]{:S(2)}) collective-permute-start(bf16[2,512,256]{2,1,0:T(8,128)(2,1)S(1)} %shard_map.78.refs_9_), channel_id=1, source_target_pairs={{0,1},{1,0},{2,3},{3,2},{4,5},{5,4},{6,7},{7,6},{8,9},{9,8},{10,11... | collective-permute-start | bytes 1572872 | tf_op jit(solution)/shard_map/ppermute | solution.py:580
  12.3 7.4 %collective-permute-start.3 = (bf16[2,128,256]{2,1,0:T(8,128)(2,1)S(1)}, bf16[2,128,256]{2,1,0:T(8,128)(2,1)S(1)}, u32[]{:S(2)}, u32[]{:S(2)}) collective-permute-start(bf16[2,128,256]{2,1,0:T(8,128)(2,1)S(1)} %get-tuple-element.39.refs_7_), channel_id=1, source_target_pairs={{3,6},{7,10},{11,14},{15,18},{19,22},{23,26},{27,30},{31,29},{5,1}... | collective-permute-start | bytes 393224 | tf_op jit(solution)/shard_map/ppermute | solution.py:578
  14.8 6.7 %collective-permute-start.4 = (bf16[2,128,256]{2,1,0:T(8,128)(2,1)S(1)}, bf16[2,128,256]{2,1,0:T(8,128)(2,1)S(1)}, u32[]{:S(2)}, u32[]{:S(2)}) collective-permute-start(bf16[2,128,256]{2,1,0:T(8,128)(2,1)S(1)} %get-tuple-element.40.refs_6_), channel_id=1, source_target_pairs={{31,26},{27,22},{23,18},{19,14},{15,10},{11,6},{7,2},{3,1},{25,29}... | collective-permute-start | bytes 393224 | tf_op jit(solution)/shard_map/ppermute | solution.py:579
  21.5 7.2 %collective-permute-start.5 = (bf16[2,512,256]{2,1,0:T(8,128)(2,1)S(1)}, bf16[2,512,256]{2,1,0:T(8,128)(2,1)S(1)}, u32[]{:S(2)}, u32[]{:S(2)}) collective-permute-start(bf16[2,512,256]{2,1,0:T(8,128)(2,1)S(1)} %get-tuple-element.41.refs_6_), channel_id=1, source_target_pairs={{0,3},{1,0},{2,1},{3,2},{4,7},{5,4},{6,5},{7,6},{8,11},{9,8},{10,9... | collective-permute-start | bytes 1572872 | tf_op jit(solution)/shard_map/ppermute | solution.py:580
  22.1 1.3 %collective-permute-start.6 = (bf16[2,128,256]{2,1,0:T(8,128)(2,1)S(1)}, bf16[2,128,256]{2,1,0:T(8,128)(2,1)S(1)}, u32[]{:S(2)}, u32[]{:S(2)}) collective-permute-start(bf16[2,128,256]{2,1,0:T(8,128)(2,1)S(1)} %get-tuple-element.42.refs_7_), channel_id=1, source_target_pairs={{2,5},{6,9},{10,13},{14,17},{18,21},{22,25},{26,29}} | collective-permute-start | bytes 393224 | tf_op jit(solution)/shard_map/ppermute | solution.py:578
  22.7 0.7 collective-permute-start.7
  28.8 15.4 %collective-permute-start.8 = (bf16[2,512,256]{2,1,0:T(8,128)(2,1)S(1)}, bf16[2,512,256]{2,1,0:T(8,128)(2,1)S(1)}, u32[]{:S(2)}, u32[]{:S(2)}) collective-permute-start(bf16[2,512,256]{2,1,0:T(8,128)(2,1)S(1)} %shard_map.81.refs_6_), channel_id=1, source_target_pairs={{0,1},{1,0},{2,3},{3,2},{4,5},{5,4},{6,7},{7,6},{8,9},{9,8},{10,11... | collective-permute-start | bytes 1572872 | tf_op jit(solution)/shard_map/ppermute | solution.py:580
  36.1 4.4 %collective-permute-start.9 = (bf16[2,128,256]{2,1,0:T(8,128)(2,1)S(1)}, bf16[2,128,256]{2,1,0:T(8,128)(2,1)S(1)}, u32[]{:S(2)}, u32[]{:S(2)}) collective-permute-start(bf16[2,128,256]{2,1,0:T(8,128)(2,1)S(1)} %get-tuple-element.46.refs_7_), channel_id=1, source_target_pairs={{1,4},{5,8},{9,12},{13,16},{17,20},{21,24},{25,28},{29,31},{7,3},{... | collective-permute-start | bytes 393224 | tf_op jit(solution)/shard_map/ppermute | solution.py:578
  36.1 8.0 %collective-permute-start.10 = (bf16[2,128,256]{2,1,0:T(8,128)(2,1)S(1)}, bf16[2,128,256]{2,1,0:T(8,128)(2,1)S(1)}, u32[]{:S(2)}, u32[]{:S(2)}) collective-permute-start(bf16[2,128,256]{2,1,0:T(8,128)(2,1)S(1)} %get-tuple-element.47.refs_6_), channel_id=1, source_target_pairs={{29,24},{25,20},{21,16},{17,12},{13,8},{9,4},{5,0},{1,3},{27,31},{... | collective-permute-start | bytes 393224 | tf_op jit(solution)/shard_map/ppermute | solution.py:579
  45.7 1.6 %collective-permute-start.11 = (bf16[544,256]{1,0:T(8,128)(2,1)S(1)}, bf16[544,256]{1,0:T(8,128)(2,1)S(1)}, u32[]{:S(2)}, u32[]{:S(2)}) collective-permute-start(bf16[544,256]{1,0:T(8,128)(2,1)S(1)} %get-tuple-element.54), channel_id=1, source_target_pairs={{0,1},{1,0},{2,3},{3,2},{4,5},{5,4},{6,7},{7,6},{8,9},{9,8},{10,11... | collective-permute-start | bytes 835592 | tf_op jit(solution)/shard_map/ppermute | solution.py:493
  47.4 13.4 %collective-permute-start.12 = (bf16[448,256]{1,0:T(8,128)(2,1)S(1)}, bf16[448,256]{1,0:T(8,128)(2,1)S(1)}, u32[]{:S(2)}, u32[]{:S(2)}) collective-permute-start(bf16[448,256]{1,0:T(8,128)(2,1)S(1)} %get-tuple-element.55), channel_id=1, source_target_pairs={{0,4},{1,29},{2,6},{3,31},{4,0},{5,9},{6,2},{7,11},{8,12},{9,5},{1... | collective-permute-start | bytes 688136 | tf_op jit(solution)/shard_map/ppermute | solution.py:479
  48.4 12.4 %collective-permute-start.14 = (bf16[192,256]{1,0:T(8,128)(2,1)S(1)}, bf16[192,256]{1,0:T(8,128)(2,1)S(1)}, u32[]{:S(2)}, u32[]{:S(2)}) collective-permute-start(bf16[192,256]{1,0:T(8,128)(2,1)S(1)} %get-tuple-element.58), channel_id=1, source_target_pairs={{0,20},{1,17},{2,22},{3,19},{4,16},{5,25},{6,18},{7,27},{8,28},{9,... | collective-permute-start | bytes 294920 | tf_op jit(solution)/shard_map/ppermute | solution.py:479
  52.1 8.7 %collective-permute-start.15 = (bf16[192,256]{1,0:T(8,128)(2,1)S(1)}, bf16[192,256]{1,0:T(8,128)(2,1)S(1)}, u32[]{:S(2)}, u32[]{:S(2)}) collective-permute-start(bf16[192,256]{1,0:T(8,128)(2,1)S(1)} %get-tuple-element.59), channel_id=1, source_target_pairs={{0,12},{1,9},{2,14},{3,11},{4,20},{5,13},{6,22},{7,15},{8,24},{9,1... | collective-permute-start | bytes 294920 | tf_op jit(solution)/shard_map/ppermute | solution.py:479
  52.2 8.6 %collective-permute-start.13 = (bf16[96,256]{1,0:T(8,128)(2,1)S(1)}, bf16[96,256]{1,0:T(8,128)(2,1)S(1)}, u32[]{:S(2)}, u32[]{:S(2)}) collective-permute-start(bf16[96,256]{1,0:T(8,128)(2,1)S(1)} %get-tuple-element.57), channel_id=1, source_target_pairs={{0,24},{4,28},{8,16},{12,20},{16,8},{20,12},{24,0},{28,4},{1,25},{... | collective-permute-start | bytes 147464 | tf_op jit(solution)/shard_map/ppermute | solution.py:492
  60.9 1.4 %collective-permute-start.16 = (bf16[192,256]{1,0:T(8,128)(2,1)S(1)}, bf16[192,256]{1,0:T(8,128)(2,1)S(1)}, u32[]{:S(2)}, u32[]{:S(2)}) collective-permute-start(bf16[192,256]{1,0:T(8,128)(2,1)S(1)} %shard_map.86.both_ref), channel_id=1, source_target_pairs={{0,1},{1,0},{2,3},{3,2},{4,5},{5,4},{6,7},{7,6},{8,9},{9,8},{10,11... | collective-permute-start | bytes 294920 | tf_op jit(solution)/shard_map/ppermute | solution.py:499
  62.3 18.7 %collective-permute-start.17 = (bf16[768,256]{1,0:T(8,128)(2,1)S(1)}, bf16[768,256]{1,0:T(8,128)(2,1)S(1)}, u32[]{:S(2)}, u32[]{:S(2)}) collective-permute-start(bf16[768,256]{1,0:T(8,128)(2,1)S(1)} %get-tuple-element.61), channel_id=1, source_target_pairs={{0,1},{1,0},{2,3},{3,2},{4,5},{5,4},{6,7},{7,6},{8,9},{9,8},{10,11... | collective-permute-start | bytes 1179656 | tf_op jit(solution)/shard_map/ppermute | solution.py:504
  62.5 7.5 %collective-permute-start.21 = (bf16[192,256]{1,0:T(8,128)(2,1)S(1)}, bf16[192,256]{1,0:T(8,128)(2,1)S(1)}, u32[]{:S(2)}, u32[]{:S(2)}) collective-permute-start(bf16[192,256]{1,0:T(8,128)(2,1)S(1)} %get-tuple-element.62.pair_ref), channel_id=1, source_target_pairs={{0,12},{1,9},{2,14},{3,11},{4,20},{5,13},{6,22},{7,15},{8,24},{9,1... | collective-permute-start | bytes 294920 | tf_op jit(solution)/shard_map/ppermute | solution.py:479
  65.0 9.0 %collective-permute-start.20 = (bf16[192,256]{1,0:T(8,128)(2,1)S(1)}, bf16[192,256]{1,0:T(8,128)(2,1)S(1)}, u32[]{:S(2)}, u32[]{:S(2)}) collective-permute-start(bf16[192,256]{1,0:T(8,128)(2,1)S(1)} %get-tuple-element.62.pair_ref), channel_id=1, source_target_pairs={{0,20},{1,17},{2,22},{3,19},{4,16},{5,25},{6,18},{7,27},{8,28},{9,... | collective-permute-start | bytes 294920 | tf_op jit(solution)/shard_map/ppermute | solution.py:479
  66.8 7.2 %collective-permute-start.19 = (bf16[192,256]{1,0:T(8,128)(2,1)S(1)}, bf16[192,256]{1,0:T(8,128)(2,1)S(1)}, u32[]{:S(2)}, u32[]{:S(2)}) collective-permute-start(bf16[192,256]{1,0:T(8,128)(2,1)S(1)} %get-tuple-element.62.pair_ref), channel_id=1, source_target_pairs={{0,4},{1,29},{2,6},{3,31},{4,0},{5,9},{6,2},{7,11},{8,12},{9,5},{1... | collective-permute-start | bytes 294920 | tf_op jit(solution)/shard_map/ppermute | solution.py:479
  74.0 6.0 %collective-permute-start.22 = (bf16[288,256]{1,0:T(8,128)(2,1)S(1)}, bf16[288,256]{1,0:T(8,128)(2,1)S(1)}, u32[]{:S(2)}, u32[]{:S(2)}) collective-permute-start(bf16[288,256]{1,0:T(8,128)(2,1)S(1)} %shard_map.88), channel_id=1, source_target_pairs={{0,1},{1,0},{2,3},{3,2},{4,5},{5,4},{6,7},{7,6},{8,9},{9,8},{10,11... | collective-permute-start | bytes 442376 | tf_op jit(solution)/shard_map/ppermute | solution.py:506
  74.1 6.0 %collective-permute-start.18 = (bf16[96,256]{1,0:T(8,128)(2,1)S(1)}, bf16[96,256]{1,0:T(8,128)(2,1)S(1)}, u32[]{:S(2)}, u32[]{:S(2)}) collective-permute-start(bf16[96,256]{1,0:T(8,128)(2,1)S(1)} %get-tuple-element.63), channel_id=1, source_target_pairs={{0,24},{4,28},{8,16},{12,20},{16,8},{20,12},{24,0},{28,4},{1,25},{... | collective-permute-start | bytes 147464 | tf_op jit(solution)/shard_map/ppermute | solution.py:503
